TPU v7x, 32 devices: a whole 2x2x4 slice. The times are simulated.
32 devices in a mesh: dom: 8 (over z, core), cls: 4 (over y, x).
Axes of the slice: x: 2, y: 2, z: 4, core: 2. Of those that a mesh axis runs over, the one named last changes fastest.
Arguments:
- particles: bfloat16 [768, 2048], P('dom', 'cls'), may hold values from -12 to 12
- references: float32 [32, 36, 2048], P('cls', None, 'dom'), may hold values from -0.4 to 0.4
- noise_weight: float32 [1024], replicated, may hold values from 0.5 to 2
Outputs:
- class_sums: float32 [32, 36, 2048], P('cls', None, 'dom')
- class_weight: float32 [32, 36], P('cls')
All inputs are finite; a program needn't handle non-finite values.
Results may differ from a plain program's by a relative error of at most 0.0033.
Values may be sent and summed in bfloat16 or wider, within the bound.
No kernel may reach another device: no remote copies, remote signals or barrier semaphores. Data moves between devices by JAX's collectives and lax.ppermute only.
A program may use at most 64 MiB of HBM per device.

v0:
```python
import math

import jax
import jax.numpy as jnp
from jax import lax
from jax.sharding import PartitionSpec as P

WIN = 32
BOX = 64
SHIFT_SIDE = 9


def phase_tables():
    freq = jnp.arange(WIN * WIN)
    freq_y = (freq // WIN - WIN // 2).astype(jnp.float32)
    freq_x = (freq % WIN - WIN // 2).astype(jnp.float32)
    offset = jnp.arange(SHIFT_SIDE * SHIFT_SIDE)
    shift_y = (offset // SHIFT_SIDE - SHIFT_SIDE // 2).astype(jnp.float32)
    shift_x = (offset % SHIFT_SIDE - SHIFT_SIDE // 2).astype(jnp.float32)
    theta = (
        2.0
        * math.pi
        / BOX
        * (shift_x[:, None] * freq_x[None, :] + shift_y[:, None] * freq_y[None, :])
    )
    return (jnp.cos(theta), jnp.sin(theta))


def shifted_block(real_part, imag_part, cosine, sine):
    moved_real = real_part[None] * cosine[:, None] + imag_part[None] * sine[:, None]
    moved_imag = imag_part[None] * cosine[:, None] - real_part[None] * sine[:, None]
    return jnp.concatenate([moved_real, moved_imag], axis=2).astype(jnp.bfloat16)


def on_device(particles, references, noise_weight):
    columns = lax.all_gather(particles, "cls", axis=1, tiled=True)
    quarter = WIN * WIN
    real_part = columns[:, :quarter].astype(jnp.float32)
    imag_part = columns[:, quarter:].astype(jnp.float32)
    weight_full = jnp.concatenate([noise_weight, noise_weight])
    gathered = lax.all_gather(references, "dom", axis=2, tiled=True)
    weighted = (gathered * weight_full).astype(jnp.bfloat16)
    half_norm = 0.5 * jnp.sum(gathered * gathered * weight_full, axis=2)
    classes_here = weighted.shape[0]
    rotations = weighted.shape[1]
    hypotheses = classes_here * rotations
    ref_matrix = weighted.reshape(hypotheses, -1)
    half_flat = half_norm.reshape(hypotheses)
    cosine, sine = phase_tables()
    block_shifts = 3
    blocks = cosine.shape[0] // block_shifts
    rows_here = particles.shape[0]

    def block_scores(index, ref_rows, half_rows):
        cos_block = lax.dynamic_slice_in_dim(cosine, index * block_shifts, block_shifts)
        sin_block = lax.dynamic_slice_in_dim(sine, index * block_shifts, block_shifts)
        moved = shifted_block(real_part, imag_part, cos_block, sin_block)
        flat = moved.reshape(block_shifts * rows_here, -1)
        scores = (
            lax.dot_general(
                flat, ref_rows, (((1,), (1,)), ((), ())), preferred_element_type=jnp.float32
            )
            - half_rows
        )
        return (flat, scores.reshape(block_shifts, rows_here, ref_rows.shape[0]))

    def first_pass(index, carry):
        top, total = carry
        _, scores = block_scores(index, ref_matrix, half_flat)
        new_top = jnp.maximum(top, jnp.max(scores, axis=(0, 2)))
        total = total * jnp.exp(top - new_top) + jnp.sum(
            jnp.exp(scores - new_top[None, :, None]), axis=(0, 2)
        )
        return (new_top, total)

    start = (jnp.full((rows_here,), -jnp.inf, jnp.float32), jnp.zeros((rows_here,), jnp.float32))
    top, total = lax.fori_loop(0, blocks, first_pass, start)
    global_top = lax.pmax(top, "cls")
    total = lax.psum(total * jnp.exp(top - global_top), "cls")
    top = global_top
    count = ref_matrix.shape[0]

    def second_pass(index, carry):
        sums, weights_total = carry
        flat, scores = block_scores(index, ref_matrix, half_flat)
        probs = jnp.exp(scores - top[None, :, None]) / total[None, :, None]
        probs_low = probs.astype(jnp.bfloat16).reshape(block_shifts * rows_here, count)
        sums = sums + lax.dot_general(
            probs_low, flat, (((0,), (0,)), ((), ())), preferred_element_type=jnp.float32
        )
        weights_total = weights_total + jnp.sum(probs, axis=(0, 1))
        return (sums, weights_total)

    start_two = (
        jnp.zeros((count, ref_matrix.shape[1]), jnp.float32),
        jnp.zeros((count,), jnp.float32),
    )
    sums, weights_total = lax.fori_loop(0, blocks, second_pass, start_two)
    class_sums = lax.psum_scatter(
        sums.reshape(classes_here, rotations, -1), "dom", scatter_dimension=2, tiled=True
    )
    class_weight = lax.psum(weights_total, "dom").reshape(classes_here, rotations)
    return (class_sums, class_weight)


def solution(mesh):
    placed = (P("dom", "cls"), P("cls", None, "dom"), P())
    return jax.shard_map(
        on_device,
        mesh=mesh,
        in_specs=placed,
        out_specs=(P("cls", None, "dom"), P("cls", None)),
        check_vma=False,
    )
```

profile of v0, /device:TPU:0, one launch (start us, length us, event | category | flops | bytes accessed | tf_op | source)
XLA Modules:
  0.0 489.8 jit_solution(18415613660315926192)
XLA Ops:
  8.0 11.3 %all_gather.6 = bf16[96,2048]{1,0:T(8,128)(2,1)S(1)} all-gather(bf16[96,512]{1,0:T(8,128)(2,1)} %param.7), channel_id=1, replica_groups=mesh['dom'=8,'cls'=4] {'cls'}, dimensions={1}, use_global_device_ids=true | all-gather | bytes 491520 | tf_op jit(solution)/shard_map/all_gather | solution.py:36
  20.7 2.2 fusion.19
  23.9 20.1 %all-gather.2.cloned.1.call-done = f32[8,36,2048]{2,0,1:T(8,128)} async-done(((f32[8,36,256]{2,0,1:T(8,128)}), f32[8,36,2048]{2,0,1:T(8,128)}) %all-gather.2.cloned.1.call-update) | async-done | bytes 2359312 | tf_op jit(solution)/shard_map/all_gather | solution.py:41
  50.5 2.2 reshape.155
  52.8 100.0 %while.34 = (s32[]{:T(128)}, f32[96]{0:T(128)S(1)}, f32[96]{0:T(128)S(1)}, f32[96,1024]{1,0:T(8,128)}, f32[81,1024]{1,0:T(8,128)}, /*index=5*/f32[96,1024]{1,0:T...) while((s32[]{:T(128)}, f32[96]{0:T(128)S(1)}, ...), condition=%wide.wide.region_6.7_spmd.clone, body=%wide.wide.region_1.6_spmd.clone.sunk | while | flops 344789472 | bytes 9801470 | solution.py:77
  152.8 9.8 %pmax.7 = f32[96]{0:T(128)S(1)} all-reduce(f32[96]{0:T(128)S(1)} %get-tuple-element.342), channel_id=1, replica_groups=mesh['dom'=8,'cls'=4] {'cls'}, use_global_device_ids=true, to_apply=%region_7.8 | all-reduce | flops 96 | bytes 768 | tf_op jit(solution)/shard_map/pmax | solution.py:78
  162.6 8.0 %psum.14 = f32[96]{0:T(128)S(1)} all-reduce(f32[96]{0:T(128)S(1)} %exponential_multiply_fusion), channel_id=1, replica_groups=mesh['dom'=8,'cls'=4] {'cls'}, use_global_device_ids=true, to_apply=%region_8.9 | all-reduce | flops 96 | bytes 768 | tf_op jit(solution)/shard_map/psum | solution.py:79
  170.6 272.8 %while.35 = (s32[]{:T(128)}, f32[288,2048]{1,0:T(8,128)S(1)}, f32[288]{0:T(512)S(1)}, f32[96,1024]{1,0:T(8,128)}, f32[81,1024]{1,0:T(8,128)}, /*index=5*/f32[96,...) while((s32[]{:T(128)}, f32[288,2048]{1,0:T(8,128)S(1)}, ...), condition=%wide.wide.region_11.12_spmd.clone, body=%wide.wide.region_9.11_spmd.clone.sunk | while | flops 688315712 | bytes 16369070 | solution.py:98
  204.1 2.2 fusion.59
  214.2 2.2 fusion.59
  224.3 2.2 fusion.59
  234.4 2.2 fusion.59
  244.5 2.2 fusion.59
  264.7 2.2 fusion.59
  274.8 2.2 fusion.59
  285.0 2.2 fusion.59
  295.1 2.2 fusion.59
  305.2 2.2 fusion.59
  335.5 2.2 fusion.59
  345.6 2.2 fusion.59
  355.7 2.2 fusion.59
  365.8 2.2 fusion.59
  445.2 14.5 %psum.15 = f32[8,36]{1,0:T(8,128)} all-reduce(f32[8,36]{1,0:T(8,128)S(1)} %reshape.157), channel_id=1, replica_groups=mesh['dom'=8,'cls'=4] {'dom'}, use_global_device_ids=true, to_apply=%region_13.14 | all-reduce | flops 288 | bytes 2304 | tf_op jit(solution)/shard_map/psum | solution.py:102
  459.7 21.4 %reduce-scatter.2.cloned.1.call-done = f32[8,36,256]{2,1,0:T(8,128)} async-done(((f32[8,36,2048]{2,1,0:T(8,128)}), f32[8,36,256]{2,1,0:T(8,128)}) %reduce-scatter.2.cloned.1.call-update) | async-done | bytes 294928 | tf_op jit(solution)/shard_map/reduce_scatter | solution.py:99
  (851 shorter events, 351.9 us)
Async XLA Ops:
  7.2 36.8 %all-gather.2.cloned.1.call-start = ((), (), s32[]{:S(2)}) async-start(), calls=%async_computation.1 | async-start | bytes 2654208 | tf_op jit(solution)/shard_map/all_gather | solution.py:41
  7.9 473.2 %reduce-scatter.2.cloned.1.call-start = ((), (), s32[]{:S(2)}) async-start(), calls=%async_computation.2 | async-start | bytes 2949120 | tf_op jit(solution)/shard_map/reduce_scatter | solution.py:99
  47.5 3.1 copy-start.3
  171.4 2.4 copy-start.5
  181.5 2.4 copy-start.5
  191.6 2.4 copy-start.5
  201.7 2.4 copy-start.5
  211.8 2.4 copy-start.5
  221.9 2.4 copy-start.5
  232.0 2.4 copy-start.5
  242.1 2.4 copy-start.5
  252.2 2.4 copy-start.5
  262.3 2.4 copy-start.5
  272.4 2.4 copy-start.5
  282.5 2.4 copy-start.5
  292.6 2.4 copy-start.5
  302.7 2.4 copy-start.5
  312.8 2.4 copy-start.5
  322.9 2.4 copy-start.5
  333.0 2.4 copy-start.5
  343.2 2.4 copy-start.5
  363.4 2.4 copy-start.5
  424.0 2.4 copy-start.5
  434.1 2.4 copy-start.5
  (89 other events, 214.5 us)
Sparse Core Ops, SparseCore 0:
  9.6 34.3 all-gather.1
  445.2 35.8 reduce-scatter.1
where the time goes:
time: 495 us; the launch traced here: 490 us
  local copies, waits for them, and re-layouts  144 us (29%)
  matrix products  135 us (27%)
  other arithmetic  107 us (22%)
  blocking collectives  43.6 us (9%)
  waiting for transfers between devices  42.2 us (9%)
  between operations  14.1 us (3%)
    dot_general x54, matrix products, block_scores(): lax.dot_general(flat, ref_rows, (((1,), (1,)), ((), ())), preferred_eleme...  80.1 us
    another operation x54, other arithmetic  76.2 us
    dot_general x27, matrix products, second_pass(): lax.dot_general(probs_low, flat, (((0,), (0,)), ((), ())), preferred_elem...  55.1 us
    reshape x27, local copies, waits for them, and re-layouts, block_scores(): return (flat, scores.reshape(block_shifts, rows_here, ref_rows.shape[0]))  53.6 us
    dynamic_slice x54, local copies, waits for them, and re-layouts, block_scores(): lax.dynamic_slice_in_dim(sine, index * block_shifts, block_shifts)  52.9 us
    reduce_scatter x1, waiting for transfers between devices, on_device(): lax.psum_scatter(sums.reshape(classes_here, rotations, -1), 'dom', scatte...  21.4 us
    all_gather x1, waiting for transfers between devices, on_device(): gathered = lax.all_gather(references, 'dom', axis=2, tiled=True)  20.1 us
    add x27, other arithmetic, second_pass(): weights_total = weights_total + jnp.sum(probs, axis=(0, 1))  18.6 us
  transfers between devices with their start and end apart: 2, of which 2 were waited for; matrix products, arithmetic and copies ran while one was open for 1% of the time, Pallas kernels for 0%

commit v1 on v0

v1 whole, which is shorter than its diff:
```python
import math

import jax
import jax.numpy as jnp
import numpy as np
from jax import lax
from jax.experimental import pallas as pl
from jax.experimental.pallas import tpu as pltpu
from jax.sharding import PartitionSpec as P

WIN = 32
BOX = 64
SHIFT_SIDE = 9
SHIFTS = SHIFT_SIDE * SHIFT_SIDE
HALF = WIN * WIN
F = 2 * HALF
GROUP = 8
MAIN = SHIFTS // GROUP * GROUP
STEPS = MAIN // GROUP
TAIL = 16
F32 = jnp.float32
BF16 = jnp.bfloat16
PARAMS = pltpu.CompilerParams(vmem_limit_bytes=48 * 1024 * 1024)


def phase_tables():
    freq = np.arange(HALF)
    fy = freq // WIN - WIN // 2
    fx = freq % WIN - WIN // 2
    offset = np.arange(SHIFTS)
    sy = offset // SHIFT_SIDE - SHIFT_SIDE // 2
    sx = offset % SHIFT_SIDE - SHIFT_SIDE // 2
    turns = sx[:, None] * fx[None, :] + sy[:, None] * fy[None, :]
    theta = (2.0 * math.pi / BOX) * turns
    pad = -SHIFTS % GROUP
    cosine = np.pad(np.cos(theta), ((0, pad), (0, 0))).astype(np.float32)
    sine = np.pad(np.sin(theta), ((0, pad), (0, 0))).astype(np.float32)
    return cosine, sine


def contract(x, y, dims):
    return lax.dot_general(x, y, (dims, ((), ())), preferred_element_type=F32)


def spread(row):
    high = row.astype(BF16).astype(F32)
    rest = row - high
    mid = rest.astype(BF16).astype(F32)
    low = (rest - mid).astype(BF16).astype(F32)
    return high, mid, low


def column_to_row(column, length, scratch):
    h = column.shape[0]
    scratch[...] = jnp.zeros(scratch.shape, F32)
    scratch[0:h, :] = jnp.broadcast_to(column, (h, 128))
    return scratch[...].T[0:1, :]


def tail_block(row, width, scratch):
    scratch[...] = jnp.zeros(scratch.shape, F32)
    per = row.shape[1] // width
    for p, part in enumerate(spread(row)):
        for j in range(per):
            r = p * per + j
            scratch[r : r + 1, :] = part[:, j * width : (j + 1) * width]
    return scratch[...].astype(BF16)


def row_of_tail(tail, width, length):
    per = length // width
    pieces = []
    for j in range(per):
        rows = [tail[p * per + j : p * per + j + 1, :] for p in range(3)]
        pieces.append((rows[2] + rows[1]) + rows[0])
    return jnp.concatenate(pieces, axis=1) if per > 1 else pieces[0]


def prepare_body(where, refs, noise, message, flat, tall, tail):
    classes, rotations, width = refs.shape
    h = classes * rotations
    for k in range(classes):
        flat[k * rotations : (k + 1) * rotations, :] = refs[k]
    x = flat[...]
    w = noise[...]
    message[0:h, :] = (x * w).astype(BF16)
    half = 0.5 * jnp.sum(x * x * w, axis=1, keepdims=True)
    row = column_to_row(half, tall.shape[0], tall)
    message[h : h + TAIL, :] = tail_block(row, width, tail)


def shift_body(where, *refs, parts, width):
    pieces = refs[:parts]
    cosine, sine, rest_cos, rest_sin, out, rest, whole = refs[parts:]
    rows = whole.shape[0]

    @pl.when(pl.program_id(0) == 0)
    def _():
        for k in range(parts):
            at = pl.multiple_of(jnp.bitwise_xor(where[2], k) * width, 128)
            whole[:, pl.ds(at, width)] = pieces[k][...].astype(F32)

    def move(c, s, target, at):
        for q in range(0, HALF, 256):
            a = whole[:, q : q + 256]
            b = whole[:, HALF + q : HALF + q + 256]
            cq = c[:, q : q + 256]
            sq = s[:, q : q + 256]
            target[at : at + rows, q : q + 256] = (a * cq + b * sq).astype(BF16)
            target[at : at + rows, HALF + q : HALF + q + 256] = (b * cq - a * sq).astype(BF16)

    for j in range(GROUP):
        move(cosine[j : j + 1, :], sine[j : j + 1, :], out, j * rows)

    @pl.when(pl.program_id(0) == 0)
    def _():
        move(rest_cos[0:1, :], rest_sin[0:1, :], rest, 0)


def score_body(where, *refs, parts, width, length):
    pieces = refs[:parts]
    moved, moved_rest, scores, scores_rest, stats, weighted, half, top, total = refs[parts:]
    h = weighted.shape[0]
    rows = moved_rest.shape[0]
    step = pl.program_id(0)

    @pl.when(step == 0)
    def _():
        row = jnp.zeros((1, length), F32)
        for k in range(parts):
            at = pl.multiple_of(jnp.bitwise_xor(where[0], k) * width, 128)
            weighted[:, pl.ds(at, width)] = pieces[k][0:h, :]
            row += row_of_tail(pieces[k][h : h + TAIL, :].astype(F32), width, length)
        half[...] = jnp.broadcast_to(row, (128, length)).T[0:h, :]
        top[...] = jnp.full(top.shape, -jnp.inf, F32)
        total[...] = jnp.zeros(total.shape, F32)

    block = contract(weighted[...], moved[...], ((1,), (1,))) - half[:, 0:1]
    scores[...] = block
    old = top[...]
    new = jnp.maximum(old, jnp.max(block, axis=0, keepdims=True))
    total[...] = total[...] * jnp.exp(old - new) + jnp.sum(
        jnp.exp(block - new), axis=0, keepdims=True
    )
    top[...] = new

    @pl.when(step == pl.num_programs(0) - 1)
    def _():
        last = contract(weighted[...], moved_rest[...], ((1,), (1,))) - half[:, 0:1]
        scores_rest[...] = last
        tops = [top[:, j * rows : (j + 1) * rows] for j in range(GROUP)]
        best = jnp.max(last, axis=0, keepdims=True)
        for t in tops:
            best = jnp.maximum(best, t)
        mass = jnp.sum(jnp.exp(last - best), axis=0, keepdims=True)
        for j in range(GROUP):
            mass += total[:, j * rows : (j + 1) * rows] * jnp.exp(tops[j] - best)
        stats[...] = jnp.zeros(stats.shape, F32)
        stats[0:1, 0:rows] = best
        stats[1:2, 0:rows] = mass


def first_sums_body(where, *refs, groups, length):
    gathered = refs[:groups]
    (scores, scores_rest, moved, moved_rest, probs, probs_rest, own, other, weight_row) = refs[
        groups : groups + 9
    ]
    sums, top, inverse, mass, tall, tail = refs[groups + 9 :]
    h, width = own.shape
    rows = moved_rest.shape[0]
    step = pl.program_id(0)

    @pl.when(step == 0)
    def _():
        best = gathered[0][0:1, 0:rows]
        for g in gathered[1:]:
            best = jnp.maximum(best, g[0:1, 0:rows])
        whole = jnp.zeros((1, rows), F32)
        for g in gathered:
            whole += g[1:2, 0:rows] * jnp.exp(g[0:1, 0:rows] - best)
        scale = 1.0 / whole
        for j in range(GROUP):
            top[:, j * rows : (j + 1) * rows] = best
            inverse[:, j * rows : (j + 1) * rows] = scale
        last = jnp.exp(scores_rest[...] - best) * scale
        last_low = last.astype(BF16)
        probs_rest[...] = last_low
        mass[...] = jnp.zeros(mass.shape, F32)
        mass[:, 0:1] = jnp.sum(last, axis=1, keepdims=True)
        sums[...] = contract(last_low, moved_rest[...], ((1,), (0,)))

    prob = jnp.exp(scores[...] - top[...]) * inverse[...]
    low = prob.astype(BF16)
    probs[...] = low
    part = prob[:, 0:128]
    for j in range(128, GROUP * rows, 128):
        part += prob[:, j : j + 128]
    mass[...] += part
    sums[...] += contract(low, moved[...], ((1,), (0,)))

    @pl.when(step == pl.num_programs(0) - 1)
    def _():
        here = pl.multiple_of(where[1] * width, 128)
        there = pl.multiple_of((1 - where[1]) * width, 128)
        own[...] = sums[:, pl.ds(here, width)]
        other[0:h, :] = sums[:, pl.ds(there, width)].astype(BF16)
        row = column_to_row(jnp.sum(mass[...], axis=1, keepdims=True), length, tall)
        weight_row[...] = jnp.broadcast_to(row, weight_row.shape)
        other[h : h + TAIL, :] = tail_block(row, width, tail)


def sums_body(where, probs, probs_rest, moved, moved_rest, own, other, sums):
    width = own.shape[1]
    step = pl.program_id(0)

    @pl.when(step == 0)
    def _():
        sums[...] = contract(probs_rest[...], moved_rest[...], ((1,), (0,)))

    sums[...] += contract(probs[...], moved[...], ((1,), (0,)))

    @pl.when(step == pl.num_programs(0) - 1)
    def _():
        here = pl.multiple_of(where[1] * width, 128)
        there = pl.multiple_of((1 - where[1]) * width, 128)
        own[...] = sums[:, pl.ds(here, width)]
        other[...] = sums[:, pl.ds(there, width)].astype(BF16)


def first_pair_body(own, received, weight_row, message, chip_row, tail):
    h, width = own.shape
    message[0:h, :] = (own[...] + received[0:h, :].astype(F32)).astype(BF16)
    length = weight_row.shape[1]
    row = weight_row[0:1, :] + row_of_tail(received[h : h + TAIL, :].astype(F32), width, length)
    chip_row[...] = jnp.broadcast_to(row, chip_row.shape)
    message[h : h + TAIL, :] = tail_block(row, width, tail)


def pair_body(own, received, first, message):
    h = own.shape[0]
    message[0:h, :] = (own[...] + received[...].astype(F32)).astype(BF16)
    message[h : h + TAIL, :] = first[h : h + TAIL, :]


def finish_body(*refs, count):
    messages = refs[:count]
    own, received, chip_row, class_sums, class_weight, flat = refs[count:]
    h, width = own.shape
    classes, rotations, _ = class_sums.shape
    length = chip_row.shape[1]
    x = own[...] + received[...].astype(F32)
    row = chip_row[0:1, :]
    for m in messages:
        x += m[0:h, :].astype(F32)
        row += row_of_tail(m[h : h + TAIL, :].astype(F32), width, length)
    flat[...] = x
    for k in range(classes):
        class_sums[k] = flat[k * rotations : (k + 1) * rotations, :]
        class_weight[k : k + 1, :] = row[:, k * rotations : (k + 1) * rotations]


def full(shape):
    return pl.BlockSpec(shape, lambda *_: (0,) * len(shape))


def make_on_device(dom, cls):
    pairs = dom // 2

    def swap(x, axis, size, k):
        return lax.ppermute(x, axis, [(i, i ^ k) for i in range(size)])

    def on_device(particles, references, noise_weight):
        rows, part_width = particles.shape
        classes, rotations, width = references.shape
        h = classes * rotations
        length = -(-h // width) * width
        block = GROUP * rows
        shape = jax.ShapeDtypeStruct
        place = lax.axis_index("dom")
        column = lax.axis_index("cls")
        where = jnp.stack([place, place % 2, column]).astype(jnp.int32)

        def call(body, grid, ins, outs, shapes, scratch, name, scalars=True):
            spec = pltpu.PrefetchScalarGridSpec(
                num_scalar_prefetch=1 if scalars else 0,
                grid=grid,
                in_specs=ins,
                out_specs=outs,
                scratch_shapes=scratch,
            )
            return pl.pallas_call(
                body, grid_spec=spec, out_shape=shapes, compiler_params=PARAMS, name=name
            )

        pieces = [particles] + [swap(particles, "cls", cls, k) for k in range(1, cls)]

        slabs = HALF // width
        message = call(
            prepare_body,
            (1,),
            [
                full((classes, rotations, width)),
                pl.BlockSpec((1, width), lambda i, w: (0, w[0] % slabs)),
            ],
            full((h + TAIL, width)),
            shape((h + TAIL, width), BF16),
            [
                pltpu.VMEM((h, width), F32),
                pltpu.VMEM((length, 128), F32),
                pltpu.VMEM((TAIL, width), F32),
            ],
            "prepare",
        )(where, references, noise_weight.reshape(1, HALF))

        even = [message] + [swap(message, "dom", dom, 2 * k) for k in range(1, pairs)]
        odd = [swap(m, "dom", dom, 1) for m in even]
        slices = [m for both in zip(even, odd) for m in both]

        cosine, sine = phase_tables()
        moved, moved_rest = call(
            lambda *r: shift_body(*r, parts=cls, width=part_width),
            (STEPS,),
            [full((rows, part_width))] * cls
            + [pl.BlockSpec((GROUP, HALF), lambda i, w: (i, 0))] * 2
            + [pl.BlockSpec((GROUP, HALF), lambda i, w: (STEPS, 0))] * 2,
            [pl.BlockSpec((block, F), lambda i, w: (i, 0)), full((rows, F))],
            [shape((MAIN * rows, F), BF16), shape((rows, F), BF16)],
            [pltpu.VMEM((rows, F), F32)],
            "shift",
        )(where, *pieces, cosine, sine, cosine, sine)

        scores, scores_rest, stats = call(
            lambda *r: score_body(*r, parts=dom, width=width, length=length),
            (STEPS,),
            [full((h + TAIL, width))] * dom
            + [pl.BlockSpec((block, F), lambda i, w: (i, 0)), full((rows, F))],
            [
                pl.BlockSpec((h, block), lambda i, w: (0, i)),
                full((h, rows)),
                full((8, 128)),
            ],
            [
                shape((h, MAIN * rows), F32),
                shape((h, rows), F32),
                shape((8, 128), F32),
            ],
            [
                pltpu.VMEM((h, F), BF16),
                pltpu.VMEM((h, 128), F32),
                pltpu.VMEM((1, block), F32),
                pltpu.VMEM((1, block), F32),
            ],
            "score",
        )(where, *slices, moved, moved_rest)

        gathered = [stats] + [swap(stats, "cls", cls, k) for k in range(1, cls)]

        def moved_specs(k):
            def at(w):
                return jnp.bitwise_xor(w[0] // 2, k)

            return [
                pl.BlockSpec((block, 2 * width), lambda i, w: (i, at(w))),
                pl.BlockSpec((rows, 2 * width), lambda i, w: (0, at(w))),
            ]

        prob_specs = [pl.BlockSpec((h, block), lambda i, w: (0, i)), full((h, rows))]
        accumulator = pltpu.VMEM((h, 2 * width), F32)
        order = list(range(pairs - 1, -1, -1))
        messages = []
        probs, probs_rest, own, other, weight_row = call(
            lambda *r: first_sums_body(*r, groups=cls, length=length),
            (STEPS,),
            [full((8, 128))] * cls + prob_specs + moved_specs(order[0]),
            prob_specs + [full((h, width)), full((h + TAIL, width)), full((8, length))],
            [
                shape((h, MAIN * rows), BF16),
                shape((h, rows), BF16),
                shape((h, width), F32),
                shape((h + TAIL, width), BF16),
                shape((8, length), F32),
            ],
            [
                accumulator,
                pltpu.VMEM((1, block), F32),
                pltpu.VMEM((1, block), F32),
                pltpu.VMEM((h, 128), F32),
                pltpu.VMEM((length, 128), F32),
                pltpu.VMEM((TAIL, width), F32),
            ],
            "sums_first",
        )(where, *gathered, scores, scores_rest, moved, moved_rest)
        received = swap(other, "dom", dom, 1)
        first, chip_row = call(
            first_pair_body,
            (1,),
            [full((h, width)), full((h + TAIL, width)), full((8, length))],
            [full((h + TAIL, width)), full((8, length))],
            [shape((h + TAIL, width), BF16), shape((8, length), F32)],
            [pltpu.VMEM((TAIL, width), F32)],
            "pair_first",
            scalars=False,
        )(own, received, weight_row)
        messages.append(swap(first, "dom", dom, 2 * order[0]))

        for k in order[1:]:
            own, other = call(
                sums_body,
                (STEPS,),
                prob_specs + moved_specs(k),
                [full((h, width)), full((h, width))],
                [shape((h, width), F32), shape((h, width), BF16)],
                [accumulator],
                "sums",
            )(where, probs, probs_rest, moved, moved_rest)
            received = swap(other, "dom", dom, 1)
            if k:
                summed = call(
                    pair_body,
                    (1,),
                    [full((h, width)), full((h, width)), full((h + TAIL, width))],
                    full((h + TAIL, width)),
                    shape((h + TAIL, width), BF16),
                    [],
                    "pair",
                    scalars=False,
                )(own, received, first)
                messages.append(swap(summed, "dom", dom, 2 * k))

        return call(
            lambda *r: finish_body(*r, count=len(messages)),
            (1,),
            [full((h + TAIL, width))] * len(messages)
            + [full((h, width)), full((h, width)), full((8, length))],
            [full((classes, rotations, width)), full((classes, rotations))],
            [
                shape((classes, rotations, width), F32),
                shape((classes, rotations), F32),
            ],
            [pltpu.VMEM((h, width), F32)],
            "finish",
            scalars=False,
        )(*messages, own, received, chip_row)

    return on_device


def solution(mesh):
    return jax.shard_map(
        make_on_device(mesh.shape["dom"], mesh.shape["cls"]),
        mesh=mesh,
        in_specs=(P("dom", "cls"), P("cls", None, "dom"), P()),
        out_specs=(P("cls", None, "dom"), P("cls", None)),
        check_vma=False,
    )
```

time: 495 us -> 122 us (0.25)
  local copies, waits for them, and re-layouts: 144 us -> 5.41 us
  matrix products: 135 us -> 0 us
  other arithmetic: 107 us -> 0.08 us
  Pallas kernels: 0 us -> 76.9 us
  blocking collectives: 43.6 us -> 0 us
  waiting for transfers between devices: 42.2 us -> 16.8 us
  starting transfers between devices: 0.08 us -> 21.2 us
  between operations: 14.1 us -> 0.75 us
    dot_general x81 -> x0, matrix products: 135 us -> none  [the longest x54 80.1 us: block_scores(): lax.dot_general(flat, ref_rows, (((1,), (1,)), ((), ())), preferred_eleme...]
    pallas_call x0 -> x11, Pallas kernels: none -> 76.9 us  [the longest x3 28.4 us: on_device(): call(sums_body, (STEPS,), prob_specs + moved_specs(k), [full((h, width)),...]
    another operation x54 -> x1, other arithmetic: 76.2 us -> 0.08 us  [on_device(): where = jnp.stack([place, place % 2, column]).astype(jnp.int32)]
    reshape x30 -> x0, local copies, waits for them, and re-layouts: 57.6 us -> none  [the longest x27 53.6 us: block_scores(): return (flat, scores.reshape(block_shifts, rows_here, ref_rows.shape[0]))]
    dynamic_slice x54 -> x0, local copies, waits for them, and re-layouts: 52.9 us -> none  [block_scores(): lax.dynamic_slice_in_dim(sine, index * block_shifts, block_shifts)]
    psum x2 -> x0, blocking collectives: 22.6 us -> none  [the longest x1 14.5 us: on_device(): lax.psum(weights_total, 'dom').reshape(classes_here, rotations)]
    sub x110 -> x0, local copies, waits for them, and re-layouts: 21.7 us -> none  [the longest x54 18 us: second_pass(): probs = jnp.exp(scores - top[None, :, None]) / total[None, :, None]]
    reduce_scatter x1 -> x0, waiting for transfers between devices: 21.4 us -> none  [on_device(): lax.psum_scatter(sums.reshape(classes_here, rotations, -1), 'dom', scatte...]
  transfers between devices with their start and end apart: 2 -> 20, of which waited for: 2 -> 7; matrix products, arithmetic and copies ran while one was open for 1% -> 0% of each run, Pallas kernels for 0% -> 35%
where the time goes in v1:
time: 122 us; the launch traced here: 121 us
  Pallas kernels  76.9 us (63%)
  starting transfers between devices  21.2 us (17%)
  waiting for transfers between devices  16.8 us (14%)
  local copies, waits for them, and re-layouts  5.41 us (4%)
    pallas_call x3, Pallas kernels, on_device(): call(sums_body, (STEPS,), prob_specs + moved_specs(k), [full((h, width)),...  28.4 us
    pallas_call x1, Pallas kernels, on_device(): call(lambda *r: score_body(*r, parts=dom, width=width, length=length), (S...  21.6 us
    ppermute x20, starting transfers between devices, swap(): return lax.ppermute(x, axis, [(i, i ^ k) for i in range(size)])  21.2 us
    ppermute x20, waiting for transfers between devices, swap(): return lax.ppermute(x, axis, [(i, i ^ k) for i in range(size)])  16.8 us
    pallas_call x1, Pallas kernels, on_device(): call(lambda *r: shift_body(*r, parts=cls, width=part_width), (STEPS,), [f...  13.9 us
    pallas_call x1, Pallas kernels, on_device(): call(lambda *r: first_sums_body(*r, groups=cls, length=length), (STEPS,),...  11.5 us
    unnamed x9, local copies, waits for them, and re-layouts  4.61 us
  transfers between devices with their start and end apart: 20, of which 7 were waited for; matrix products, arithmetic and copies ran while one was open for 0% of the time, Pallas kernels for 35%

profile of v1, /device:TPU:0, one launch (start us, length us, event | category | flops | bytes accessed | tf_op | source)
XLA Modules:
  0.0 121.2 jit_solution(11372770714300592267)
XLA Ops:
  0.6 1.1 copy.7.refs
  3.2 5.1 %collective-permute-start.5 = (bf16[304,256]{1,0:T(8,128)(2,1)S(1)}, bf16[304,256]{1,0:T(8,128)(2,1)S(1)}, u32[]{:S(2)}, u32[]{:S(2)}) collective-permute-start(bf16[304,256]{1,0:T(8,128)(2,1)S(1)} %prepare.1.r_1_), channel_id=1, source_target_pairs={{0,24},{4,28},{8,16},{12,20},{16,8},{20,12},{24,0},{28,4},{1,25},{... | collective-permute-start | bytes 466952 | tf_op jit(solution)/shard_map/ppermute | solution.py:270
  9.0 1.7 %collective-permute-start.8 = (bf16[96,512]{1,0:T(8,128)(2,1)}, bf16[96,512]{1,0:T(8,128)(2,1)S(1)}, u32[]{:S(2)}, u32[]{:S(2)}) collective-permute-start(bf16[96,512]{1,0:T(8,128)(2,1)} %r_1_.1), channel_id=1, source_target_pairs={{0,2},{1,3},{2,0},{3,1},{4,6},{5,7},{6,4},{7,5},{8,10},{9,11},{10,... | collective-permute-start | bytes 294920 | tf_op jit(solution)/shard_map/ppermute | solution.py:270
  10.6 1.5 %collective-permute-start.7 = (bf16[96,512]{1,0:T(8,128)(2,1)}, bf16[96,512]{1,0:T(8,128)(2,1)S(1)}, u32[]{:S(2)}, u32[]{:S(2)}) collective-permute-start(bf16[96,512]{1,0:T(8,128)(2,1)} %r_1_.1), channel_id=1, source_target_pairs={{0,1},{1,0},{2,3},{3,2},{4,5},{5,4},{6,7},{7,6},{8,9},{9,8},{10,11... | collective-permute-start | bytes 294920 | tf_op jit(solution)/shard_map/ppermute | solution.py:270
  12.1 1.7 %collective-permute-done.8.r_3_ = bf16[96,512]{1,0:T(8,128)(2,1)S(1)} collective-permute-done((bf16[96,512]{1,0:T(8,128)(2,1)}, bf16[96,512]{1,0:T(8,128)(2,1)S(1)}, u32[]{:S(2)}, u32[]{:S(2)}) %collective-permute-start.8) | collective-permute-done | bytes 98336 | tf_op jit(solution)/shard_map/ppermute | solution.py:270
  14.3 7.2 %collective-permute-done.3.r_5_ = bf16[304,256]{1,0:T(8,128)(2,1)S(1)} collective-permute-done((bf16[304,256]{1,0:T(8,128)(2,1)S(1)}, bf16[304,256]{1,0:T(8,128)(2,1)S(1)}, u32[]{:S(2)}, u32[]{:S(2)}) %collective-permute-start.3) | collective-permute-done | bytes 155680 | tf_op jit(solution)/shard_map/ppermute | solution.py:270
  22.0 2.4 %collective-permute-start.9 = (bf16[96,512]{1,0:T(8,128)(2,1)}, bf16[96,512]{1,0:T(8,128)(2,1)S(1)}, u32[]{:S(2)}, u32[]{:S(2)}) collective-permute-start(bf16[96,512]{1,0:T(8,128)(2,1)} %r_1_.1), channel_id=1, source_target_pairs={{0,3},{1,2},{2,1},{3,0},{4,7},{5,6},{6,5},{7,4},{8,11},{9,10},{10,... | collective-permute-start | bytes 294920 | tf_op jit(solution)/shard_map/ppermute | solution.py:270
  24.5 3.4 %collective-permute-done.9.r_4_ = bf16[96,512]{1,0:T(8,128)(2,1)S(1)} collective-permute-done((bf16[96,512]{1,0:T(8,128)(2,1)}, bf16[96,512]{1,0:T(8,128)(2,1)S(1)}, u32[]{:S(2)}, u32[]{:S(2)}) %collective-permute-start.9) | collective-permute-done | bytes 98336 | tf_op jit(solution)/shard_map/ppermute | solution.py:270
  27.9 1.0 copy-done
  28.9 1.0 copy-done.1
  29.9 0.9 copy-done.2
  30.8 13.9 %shift.1 = (bf16[7680,2048]{1,0:T(8,128)(2,1)}, bf16[96,2048]{1,0:T(8,128)(2,1)S(1)}) custom-call(s32[3]{0:T(128)S(1)} %pad_add_fusion.where.r_0_, bf16[96,512]{1,0:T(8,128)(2,1)S(1)} %copy-done.2, bf16[96,512]{1,0:T(8,128)(2,1)S(1)} %collective-permute-done.7.r_2_, bf16[96,512]{1,0:T(8,128)(2,1)S(1)} %collective-permute-done.8.r_3_, ...), custom_call_target="tpu_custom_call" | custom-call | tf_op jit(solution)/shard_map/shift/pallas_call | solution.py:320
  44.7 21.6 %score.1 = (f32[288,7680]{1,0:T(8,128)}, f32[288,96]{1,0:T(8,128)S(1)}, f32[8,128]{1,0:T(8,128)S(1)}) custom-call(s32[3]{0:T(128)S(1)} %pad_add_fusion.where.r_0_, bf16[304,256]{1,0:T(8,128)(2,1)S(1)} %prepare.1.r_1_, bf16[304,256]{1,0:T(8,128)(2,1)S(1)} %collective-permute-done.r_2_, bf16[304,256]{1,0:T(8,128)(2,1)S(1)} %collective-permute-done.1.r_3_, ...), custom_call_target="tpu_custom_call" | custom-call | tf_op jit(solution)/shard_map/score/pallas_call | solution.py:332
  66.3 2.5 %collective-permute-start.12 = (f32[8,128]{1,0:T(8,128)S(1)}, f32[8,128]{1,0:T(8,128)S(1)}, u32[]{:S(2)}, u32[]{:S(2)}) collective-permute-start(f32[8,128]{1,0:T(8,128)S(1)} %get-tuple-element.22.r_1_), channel_id=1, source_target_pairs={{0,3},{1,2},{2,1},{3,0},{4,7},{5,6},{6,5},{7,4},{8,11},{9,10},{10,... | collective-permute-start | bytes 12296 | tf_op jit(solution)/shard_map/ppermute | solution.py:270
  69.8 1.0 collective-permute-done.12.r_4_
  70.8 1.6 %collective-permute-done.11.r_3_ = f32[8,128]{1,0:T(8,128)S(1)} collective-permute-done((f32[8,128]{1,0:T(8,128)S(1)}, f32[8,128]{1,0:T(8,128)S(1)}, u32[]{:S(2)}, u32[]{:S(2)}) %collective-permute-start.11) | collective-permute-done | bytes 4128 | tf_op jit(solution)/shard_map/ppermute | solution.py:270
  72.9 11.5 %sums_first.1 = (bf16[288,7680]{1,0:T(8,128)(2,1)S(1)}, bf16[288,96]{1,0:T(8,128)(2,1)S(1)}, f32[288,256]{1,0:T(8,128)S(1)}, bf16[304,256]{1,0:T(8,128)(2,1)S(1)}, f32[8,512]{1,0:T(8,128)S(1)}) custom-call(s32[3]{0:T(128)S(1)} %pad_add_fusion.where.r_0_, f32[8,128]{1,0:T(8,128)S(1)} %get-tuple-element.22.r_1_, f32[8,128]{1,0:T(8,128)S(1)} %collective-permute-done.10.r_2_, ...), custom_call_target="tpu_custom_call" | custom-call | tf_op jit(solution)/shard_map/sums_first/pallas_call | solution.py:371
  84.4 9.5 %sums.3 = (f32[288,256]{1,0:T(8,128)S(1)}, bf16[288,256]{1,0:T(8,128)(2,1)S(1)}) custom-call(s32[3]{0:T(128)S(1)} %pad_add_fusion.where.r_0_, bf16[288,7680]{1,0:T(8,128)(2,1)S(1)} %get-tuple-element.29.probs, bf16[288,96]{1,0:T(8,128)(2,1)S(1)} %get-tuple-element.30.probs_rest, bf16[7680,2048]{1,0:T(8,128)(2,1)} %get-tuple-element.20.r_9_.r_7_.moved, ...), custom_call_target="tpu_custom_call" | custom-call | tf_op jit(solution)/shard_map/sums/pallas_call | solution.py:407
  94.5 9.5 %sums.4 = (f32[288,256]{1,0:T(8,128)S(1)}, bf16[288,256]{1,0:T(8,128)(2,1)S(1)}) custom-call(s32[3]{0:T(128)S(1)} %pad_add_fusion.where.r_0_, bf16[288,7680]{1,0:T(8,128)(2,1)S(1)} %get-tuple-element.29.probs, bf16[288,96]{1,0:T(8,128)(2,1)S(1)} %get-tuple-element.30.probs_rest, bf16[7680,2048]{1,0:T(8,128)(2,1)} %get-tuple-element.20.r_9_.r_7_.moved, ...), custom_call_target="tpu_custom_call" | custom-call | tf_op jit(solution)/shard_map/sums/pallas_call | solution.py:407
  104.1 2.5 %collective-permute-start.14 = (bf16[304,256]{1,0:T(8,128)(2,1)S(1)}, bf16[304,256]{1,0:T(8,128)(2,1)S(1)}, u32[]{:S(2)}, u32[]{:S(2)}) collective-permute-start(bf16[304,256]{1,0:T(8,128)(2,1)S(1)} %get-tuple-element.28.first), channel_id=1, source_target_pairs={{0,24},{4,28},{8,16},{12,20},{16,8},{20,12},{24,0},{28,4},{1,25},{... | collective-permute-start | bytes 466952 | tf_op jit(solution)/shard_map/ppermute | solution.py:270
  106.8 2.0 %collective-permute-start.18 = (bf16[304,256]{1,0:T(8,128)(2,1)S(1)}, bf16[304,256]{1,0:T(8,128)(2,1)S(1)}, u32[]{:S(2)}, u32[]{:S(2)}) collective-permute-start(bf16[304,256]{1,0:T(8,128)(2,1)S(1)} %pair.3), channel_id=1, source_target_pairs={{0,8},{4,12},{8,0},{12,4},{16,24},{20,28},{24,16},{28,20},{1,9},{5... | collective-permute-start | bytes 466952 | tf_op jit(solution)/shard_map/ppermute | solution.py:270
  108.8 9.4 %sums.5 = (f32[288,256]{1,0:T(8,128)S(1)}, bf16[288,256]{1,0:T(8,128)(2,1)S(1)}) custom-call(s32[3]{0:T(128)S(1)} %pad_add_fusion.where.r_0_, bf16[288,7680]{1,0:T(8,128)(2,1)S(1)} %get-tuple-element.29.probs, bf16[288,96]{1,0:T(8,128)(2,1)S(1)} %get-tuple-element.30.probs_rest, bf16[7680,2048]{1,0:T(8,128)(2,1)} %get-tuple-element.20.r_9_.r_7_.moved, ...), custom_call_target="tpu_custom_call" | custom-call | tf_op jit(solution)/shard_map/sums/pallas_call | solution.py:407
  118.3 1.4 %collective-permute-done.19.r_4_ = bf16[288,256]{1,0:T(8,128)(2,1)S(1)} collective-permute-done((bf16[288,256]{1,0:T(8,128)(2,1)S(1)}, bf16[288,256]{1,0:T(8,128)(2,1)S(1)}, u32[]{:S(2)}, u32[]{:S(2)}) %collective-permute-start.19) | collective-permute-done | bytes 147488 | tf_op jit(solution)/shard_map/ppermute | solution.py:270
  120.4 0.8 copy.8
  (38 shorter events, 6.5 us)
Async XLA Ops:
  1.8 0.7 copy-start.3
  3.2 10.6 %collective-permute-start.5 = (bf16[304,256]{1,0:T(8,128)(2,1)S(1)}, bf16[304,256]{1,0:T(8,128)(2,1)S(1)}, u32[]{:S(2)}, u32[]{:S(2)}) collective-permute-start(bf16[304,256]{1,0:T(8,128)(2,1)S(1)} %prepare.1.r_1_), channel_id=1, source_target_pairs={{0,24},{4,28},{8,16},{12,20},{16,8},{20,12},{24,0},{28,4},{1,25},{... | collective-permute-start | bytes 466952 | tf_op jit(solution)/shard_map/ppermute | solution.py:270
  8.3 13.2 %collective-permute-start.3 = (bf16[304,256]{1,0:T(8,128)(2,1)S(1)}, bf16[304,256]{1,0:T(8,128)(2,1)S(1)}, u32[]{:S(2)}, u32[]{:S(2)}) collective-permute-start(bf16[304,256]{1,0:T(8,128)(2,1)S(1)} %prepare.1.r_1_), channel_id=1, source_target_pairs={{0,16},{4,20},{8,24},{12,28},{16,0},{20,4},{24,8},{28,12},{1,17},{... | collective-permute-start | bytes 466952 | tf_op jit(solution)/shard_map/ppermute | solution.py:270
  8.3 13.2 %collective-permute-start.1 = (bf16[304,256]{1,0:T(8,128)(2,1)S(1)}, bf16[304,256]{1,0:T(8,128)(2,1)S(1)}, u32[]{:S(2)}, u32[]{:S(2)}) collective-permute-start(bf16[304,256]{1,0:T(8,128)(2,1)S(1)} %prepare.1.r_1_), channel_id=1, source_target_pairs={{0,8},{4,12},{8,0},{12,4},{16,24},{20,28},{24,16},{28,20},{1,9},{5... | collective-permute-start | bytes 466952 | tf_op jit(solution)/shard_map/ppermute | solution.py:270
  9.0 4.8 %collective-permute-start.8 = (bf16[96,512]{1,0:T(8,128)(2,1)}, bf16[96,512]{1,0:T(8,128)(2,1)S(1)}, u32[]{:S(2)}, u32[]{:S(2)}) collective-permute-start(bf16[96,512]{1,0:T(8,128)(2,1)} %r_1_.1), channel_id=1, source_target_pairs={{0,2},{1,3},{2,0},{3,1},{4,6},{5,7},{6,4},{7,5},{8,10},{9,11},{10,... | collective-permute-start | bytes 294920 | tf_op jit(solution)/shard_map/ppermute | solution.py:270
  10.6 11.4 %collective-permute-start.7 = (bf16[96,512]{1,0:T(8,128)(2,1)}, bf16[96,512]{1,0:T(8,128)(2,1)S(1)}, u32[]{:S(2)}, u32[]{:S(2)}) collective-permute-start(bf16[96,512]{1,0:T(8,128)(2,1)} %r_1_.1), channel_id=1, source_target_pairs={{0,1},{1,0},{2,3},{3,2},{4,5},{5,4},{6,7},{7,6},{8,9},{9,8},{10,11... | collective-permute-start | bytes 294920 | tf_op jit(solution)/shard_map/ppermute | solution.py:270
  13.8 30.9 %collective-permute-start = (bf16[304,256]{1,0:T(8,128)(2,1)S(1)}, bf16[304,256]{1,0:T(8,128)(2,1)S(1)}, u32[]{:S(2)}, u32[]{:S(2)}) collective-permute-start(bf16[304,256]{1,0:T(8,128)(2,1)S(1)} %prepare.1.r_1_), channel_id=1, source_target_pairs={{0,4},{4,0},{8,12},{12,8},{16,20},{20,16},{24,28},{28,24},{1,5},{5... | collective-permute-start | bytes 466952 | tf_op jit(solution)/shard_map/ppermute | solution.py:270
  13.8 30.9 %collective-permute-start.6 = (bf16[304,256]{1,0:T(8,128)(2,1)S(1)}, bf16[304,256]{1,0:T(8,128)(2,1)S(1)}, u32[]{:S(2)}, u32[]{:S(2)}) collective-permute-start(bf16[304,256]{1,0:T(8,128)(2,1)S(1)} %collective-permute-done.5.r_7_), channel_id=1, source_target_pairs={{0,4},{4,0},{8,12},{12,8},{16,20},{20,16},{24,28},{28,24},{1,5},{5... | collective-permute-start | bytes 466952 | tf_op jit(solution)/shard_map/ppermute | solution.py:270
  21.5 23.2 %collective-permute-start.4 = (bf16[304,256]{1,0:T(8,128)(2,1)S(1)}, bf16[304,256]{1,0:T(8,128)(2,1)S(1)}, u32[]{:S(2)}, u32[]{:S(2)}) collective-permute-start(bf16[304,256]{1,0:T(8,128)(2,1)S(1)} %collective-permute-done.3.r_5_), channel_id=1, source_target_pairs={{0,4},{4,0},{8,12},{12,8},{16,20},{20,16},{24,28},{28,24},{1,5},{5... | collective-permute-start | bytes 466952 | tf_op jit(solution)/shard_map/ppermute | solution.py:270
  21.5 23.2 %collective-permute-start.2 = (bf16[304,256]{1,0:T(8,128)(2,1)S(1)}, bf16[304,256]{1,0:T(8,128)(2,1)S(1)}, u32[]{:S(2)}, u32[]{:S(2)}) collective-permute-start(bf16[304,256]{1,0:T(8,128)(2,1)S(1)} %collective-permute-done.1.r_3_), channel_id=1, source_target_pairs={{0,4},{4,0},{8,12},{12,8},{16,20},{20,16},{24,28},{28,24},{1,5},{5... | collective-permute-start | bytes 466952 | tf_op jit(solution)/shard_map/ppermute | solution.py:270
  22.0 5.9 %collective-permute-start.9 = (bf16[96,512]{1,0:T(8,128)(2,1)}, bf16[96,512]{1,0:T(8,128)(2,1)S(1)}, u32[]{:S(2)}, u32[]{:S(2)}) collective-permute-start(bf16[96,512]{1,0:T(8,128)(2,1)} %r_1_.1), channel_id=1, source_target_pairs={{0,3},{1,2},{2,1},{3,0},{4,7},{5,6},{6,5},{7,4},{8,11},{9,10},{10,... | collective-permute-start | bytes 294920 | tf_op jit(solution)/shard_map/ppermute | solution.py:270
  27.9 1.0 copy-start
  28.9 1.0 copy-start.1
  29.9 0.9 copy-start.2
  66.3 4.5 %collective-permute-start.12 = (f32[8,128]{1,0:T(8,128)S(1)}, f32[8,128]{1,0:T(8,128)S(1)}, u32[]{:S(2)}, u32[]{:S(2)}) collective-permute-start(f32[8,128]{1,0:T(8,128)S(1)} %get-tuple-element.22.r_1_), channel_id=1, source_target_pairs={{0,3},{1,2},{2,1},{3,0},{4,7},{5,6},{6,5},{7,4},{8,11},{9,10},{10,... | collective-permute-start | bytes 12296 | tf_op jit(solution)/shard_map/ppermute | solution.py:270
  68.8 3.6 %collective-permute-start.11 = (f32[8,128]{1,0:T(8,128)S(1)}, f32[8,128]{1,0:T(8,128)S(1)}, u32[]{:S(2)}, u32[]{:S(2)}) collective-permute-start(f32[8,128]{1,0:T(8,128)S(1)} %get-tuple-element.22.r_1_), channel_id=1, source_target_pairs={{0,2},{1,3},{2,0},{3,1},{4,6},{5,7},{6,4},{7,5},{8,10},{9,11},{10,... | collective-permute-start | bytes 12296 | tf_op jit(solution)/shard_map/ppermute | solution.py:270
  69.3 3.6 %collective-permute-start.10 = (f32[8,128]{1,0:T(8,128)S(1)}, f32[8,128]{1,0:T(8,128)S(1)}, u32[]{:S(2)}, u32[]{:S(2)}) collective-permute-start(f32[8,128]{1,0:T(8,128)S(1)} %get-tuple-element.22.r_1_), channel_id=1, source_target_pairs={{0,1},{1,0},{2,3},{3,2},{4,5},{5,4},{6,7},{7,6},{8,9},{9,8},{10,11... | collective-permute-start | bytes 12296 | tf_op jit(solution)/shard_map/ppermute | solution.py:270
  84.4 19.7 %collective-permute-start.13 = (bf16[304,256]{1,0:T(8,128)(2,1)S(1)}, bf16[304,256]{1,0:T(8,128)(2,1)S(1)}, u32[]{:S(2)}, u32[]{:S(2)}) collective-permute-start(bf16[304,256]{1,0:T(8,128)(2,1)S(1)} %get-tuple-element.26), channel_id=1, source_target_pairs={{0,4},{4,0},{8,12},{12,8},{16,20},{20,16},{24,28},{28,24},{1,5},{5... | collective-permute-start | bytes 466952 | tf_op jit(solution)/shard_map/ppermute | solution.py:270
  93.9 12.7 %collective-permute-start.15 = (bf16[288,256]{1,0:T(8,128)(2,1)S(1)}, bf16[288,256]{1,0:T(8,128)(2,1)S(1)}, u32[]{:S(2)}, u32[]{:S(2)}) collective-permute-start(bf16[288,256]{1,0:T(8,128)(2,1)S(1)} %get-tuple-element.32), channel_id=1, source_target_pairs={{0,4},{4,0},{8,12},{12,8},{16,20},{20,16},{24,28},{28,24},{1,5},{5... | collective-permute-start | bytes 442376 | tf_op jit(solution)/shard_map/ppermute | solution.py:270
  103.9 2.8 %collective-permute-start.17 = (bf16[288,256]{1,0:T(8,128)(2,1)S(1)}, bf16[288,256]{1,0:T(8,128)(2,1)S(1)}, u32[]{:S(2)}, u32[]{:S(2)}) collective-permute-start(bf16[288,256]{1,0:T(8,128)(2,1)S(1)} %get-tuple-element.34), channel_id=1, source_target_pairs={{0,4},{4,0},{8,12},{12,8},{16,20},{20,16},{24,28},{28,24},{1,5},{5... | collective-permute-start | bytes 442376 | tf_op jit(solution)/shard_map/ppermute | solution.py:270
  104.1 15.6 %collective-permute-start.14 = (bf16[304,256]{1,0:T(8,128)(2,1)S(1)}, bf16[304,256]{1,0:T(8,128)(2,1)S(1)}, u32[]{:S(2)}, u32[]{:S(2)}) collective-permute-start(bf16[304,256]{1,0:T(8,128)(2,1)S(1)} %get-tuple-element.28.first), channel_id=1, source_target_pairs={{0,24},{4,28},{8,16},{12,20},{16,8},{20,12},{24,0},{28,4},{1,25},{... | collective-permute-start | bytes 466952 | tf_op jit(solution)/shard_map/ppermute | solution.py:270
  106.7 13.0 %collective-permute-start.16 = (bf16[304,256]{1,0:T(8,128)(2,1)S(1)}, bf16[304,256]{1,0:T(8,128)(2,1)S(1)}, u32[]{:S(2)}, u32[]{:S(2)}) collective-permute-start(bf16[304,256]{1,0:T(8,128)(2,1)S(1)} %pair.2), channel_id=1, source_target_pairs={{0,16},{4,20},{8,24},{12,28},{16,0},{20,4},{24,8},{28,12},{1,17},{... | collective-permute-start | bytes 466952 | tf_op jit(solution)/shard_map/ppermute | solution.py:270
  106.8 12.9 %collective-permute-start.18 = (bf16[304,256]{1,0:T(8,128)(2,1)S(1)}, bf16[304,256]{1,0:T(8,128)(2,1)S(1)}, u32[]{:S(2)}, u32[]{:S(2)}) collective-permute-start(bf16[304,256]{1,0:T(8,128)(2,1)S(1)} %pair.3), channel_id=1, source_target_pairs={{0,8},{4,12},{8,0},{12,4},{16,24},{20,28},{24,16},{28,20},{1,9},{5... | collective-permute-start | bytes 466952 | tf_op jit(solution)/shard_map/ppermute | solution.py:270
  118.2 1.4 %collective-permute-start.19 = (bf16[288,256]{1,0:T(8,128)(2,1)S(1)}, bf16[288,256]{1,0:T(8,128)(2,1)S(1)}, u32[]{:S(2)}, u32[]{:S(2)}) collective-permute-start(bf16[288,256]{1,0:T(8,128)(2,1)S(1)} %get-tuple-element.36), channel_id=1, source_target_pairs={{0,4},{4,0},{8,12},{12,8},{16,20},{20,16},{24,28},{28,24},{1,5},{5... | collective-permute-start | bytes 442376 | tf_op jit(solution)/shard_map/ppermute | solution.py:270

commit v2 on v0

v2 whole, which is shorter than its diff:
```python
import math

import jax
import jax.numpy as jnp
import numpy as np
from jax import lax
from jax.experimental import pallas as pl
from jax.experimental.pallas import tpu as pltpu
from jax.sharding import PartitionSpec as P

WIN = 32
BOX = 64
SHIFT_SIDE = 9
SHIFTS = SHIFT_SIDE * SHIFT_SIDE
HALF = WIN * WIN
F = 2 * HALF
GROUP = 8
MAIN = SHIFTS // GROUP * GROUP
STEPS = MAIN // GROUP
TAIL = 16
F32 = jnp.float32
BF16 = jnp.bfloat16


def phase_tables():
    freq = np.arange(HALF)
    fy = freq // WIN - WIN // 2
    fx = freq % WIN - WIN // 2
    offset = np.arange(SHIFTS)
    sy = offset // SHIFT_SIDE - SHIFT_SIDE // 2
    sx = offset % SHIFT_SIDE - SHIFT_SIDE // 2
    turns = sx[:, None] * fx[None, :] + sy[:, None] * fy[None, :]
    theta = (2.0 * math.pi / BOX) * turns
    pad = -SHIFTS % GROUP
    cosine = np.pad(np.cos(theta), ((0, pad), (0, 0))).astype(np.float32)
    sine = np.pad(np.sin(theta), ((0, pad), (0, 0))).astype(np.float32)
    return cosine, sine


def contract(x, y, dims):
    return lax.dot_general(x, y, (dims, ((), ())), preferred_element_type=F32)


def spread(row):
    high = row.astype(BF16).astype(F32)
    rest = row - high
    mid = rest.astype(BF16).astype(F32)
    low = (rest - mid).astype(BF16).astype(F32)
    return high, mid, low


def column_to_row(column, length, scratch):
    h = column.shape[0]
    scratch[...] = jnp.zeros(scratch.shape, F32)
    scratch[0:h, :] = jnp.broadcast_to(column, (h, 128))
    return scratch[...].T[0:1, :]


def tail_block(row, width, scratch):
    scratch[...] = jnp.zeros(scratch.shape, F32)
    per = row.shape[1] // width
    for p, part in enumerate(spread(row)):
        for j in range(per):
            r = p * per + j
            scratch[r : r + 1, :] = part[:, j * width : (j + 1) * width]
    return scratch[...].astype(BF16)


def row_of_tail(tail, width, length):
    per = length // width
    pieces = []
    for j in range(per):
        rows = [tail[p * per + j : p * per + j + 1, :] for p in range(3)]
        pieces.append((rows[2] + rows[1]) + rows[0])
    return jnp.concatenate(pieces, axis=1) if per > 1 else pieces[0]


def prepare_body(where, refs, noise, message, tall, tail):
    h, width = refs.shape
    x = refs[...]
    w = noise[...]
    message[0:h, :] = (x * w).astype(BF16)
    half = 0.5 * jnp.sum(x * x * w, axis=1, keepdims=True)
    row = column_to_row(half, tall.shape[0], tall)
    message[h : h + TAIL, :] = tail_block(row, width, tail)


def table_body(where, tables, cosine, sine, *, width):
    count = HALF // width
    sign = jnp.where(where[0] < count, 1.0, -1.0).astype(F32)
    for k in range(count):
        at = pl.multiple_of(jnp.bitwise_and(jnp.bitwise_xor(where[0], k), count - 1) * width, 128)
        cosine[:, k * width : (k + 1) * width] = tables[0, :, pl.ds(at, width)]
        sine[:, k * width : (k + 1) * width] = tables[1, :, pl.ds(at, width)] * sign


def shift_body(where, *refs, parts, pairs, width):
    pieces = refs[:parts]
    cosine, sine = refs[parts : parts + 2]
    outs = refs[parts + 2 : parts + 2 + pairs]
    rest, plain, whole = refs[parts + 2 + pairs :]
    rows, part_width = pieces[0].shape
    for k in range(parts):
        at = pl.multiple_of(jnp.bitwise_xor(where[2], k) * part_width, 128)
        plain[:, pl.ds(at, part_width)] = pieces[k][...].astype(F32)
    for k in range(2 * pairs):
        at = pl.multiple_of(jnp.bitwise_xor(where[0], k) * width, 128)
        whole[:, k * width : (k + 1) * width] = plain[:, pl.ds(at, width)]

    def move(s, store):
        c_all = cosine[pl.ds(s, 1), :]
        s_all = sine[pl.ds(s, 1), :]
        for k in range(pairs):
            q = k * width
            c_row = c_all[:, q : q + width]
            s_row = s_all[:, q : q + width]
            a = whole[:, q : q + width]
            b = whole[:, HALF + q : HALF + q + width]
            store(k, (a * c_row + b * s_row).astype(BF16))
            store(k + pairs, (b * c_row - a * s_row).astype(BF16))

    def one(s, carry):
        at = pl.multiple_of(s * rows, rows)

        def store(k, value):
            outs[k // 2][pl.ds(at, rows), (k % 2) * width : (k % 2 + 1) * width] = value

        move(s, store)
        return carry

    lax.fori_loop(0, MAIN, one, 0)

    def store_rest(k, value):
        rest[:, k * width : (k + 1) * width] = value

    for s in range(MAIN, SHIFTS):
        move(s, store_rest)


def score_body(*refs, parts, pairs, length):
    pieces = refs[:parts]
    moved = refs[parts : parts + pairs]
    moved_rest = refs[parts + pairs]
    weights, weights_rest, tops, stats = refs[parts + pairs + 1 : parts + pairs + 5]
    weighted, half, even, odd, totals = refs[-5:]
    h, block = even.shape
    rows = moved_rest.shape[0]
    width = pieces[0].shape[1]

    row = jnp.zeros((1, length), F32)
    for k in range(parts):
        weighted[:, k * width : (k + 1) * width] = pieces[k][0:h, :]
        row += row_of_tail(pieces[k][h : h + TAIL, :].astype(F32), width, length)
    half[...] = jnp.broadcast_to(row, (128, length)).T[0:h, :]

    def multiply(i, target):
        at = i * block if isinstance(i, int) else pl.multiple_of(i * block, block)
        x = jnp.concatenate([m[pl.ds(at, block), :] for m in moved], axis=1)
        target[...] = contract(weighted[...], x, ((1,), (1,)))

    def soften(i, source):
        for q in range(0, block, 128):
            x = source[:, q : q + 128] - half[...]
            top = jnp.max(x, axis=0, keepdims=True)
            x = jnp.exp(x - top)
            weights[i, :, q : q + 128] = x
            tops[i, :, q : q + 128] = jnp.broadcast_to(top, (8, 128))
            total = jnp.sum(x, axis=0, keepdims=True)
            totals[i, :, q : q + 128] = jnp.broadcast_to(total, (8, 128))

    multiply(0, even)

    def two(t, carry):
        multiply(2 * t + 1, odd)
        soften(2 * t, even)
        multiply(2 * t + 2, even)
        soften(2 * t + 1, odd)
        return carry

    lax.fori_loop(0, STEPS // 2 - 1, two, 0)
    multiply(STEPS - 1, odd)
    soften(STEPS - 2, even)
    last = contract(weighted[...], moved_rest[...], ((1,), (1,))) - half[:, 0:1]
    soften(STEPS - 1, odd)

    best = jnp.max(last, axis=0, keepdims=True)
    last = jnp.exp(last - best)
    weights_rest[...] = last
    tops[STEPS, 0:1, 0:rows] = best
    mass = jnp.sum(last, axis=0, keepdims=True)
    lane_top = tops[0]
    for i in range(1, STEPS):
        lane_top = jnp.maximum(lane_top, tops[i])
    lane_mass = totals[0] * jnp.exp(tops[0] - lane_top)
    for i in range(1, STEPS):
        lane_mass += totals[i] * jnp.exp(tops[i] - lane_top)
    parts_top = [lane_top[0:1, j * rows : (j + 1) * rows] for j in range(GROUP)]
    peak = best
    for t in parts_top:
        peak = jnp.maximum(peak, t)
    mass = mass * jnp.exp(best - peak)
    for j in range(GROUP):
        mass += lane_mass[0:1, j * rows : (j + 1) * rows] * jnp.exp(parts_top[j] - peak)
    stats[...] = jnp.zeros(stats.shape, F32)
    stats[0:1, 0:rows] = peak
    stats[1:2, 0:rows] = mass


def split_pair(sums, own, other):
    h, width = own.shape
    own[...] = sums[:, 0:width]
    other[0:h, :] = sums[:, width : 2 * width].astype(BF16)


def accumulate(sums, probs, probs_rest, moved, moved_rest, rest_at):
    block = probs.shape[2]
    sums[...] = contract(probs_rest[...], moved_rest[:, rest_at : rest_at + sums.shape[1]], ((1,), (0,)))
    for i in range(STEPS):
        sums[...] += contract(probs[i], moved[i * block : (i + 1) * block, :], ((1,), (0,)))


def first_sums_body(*refs, groups, others, length, rest_at):
    gathered = refs[:groups]
    weights, weights_rest, tops, moved, moved_rest = refs[groups : groups + 5]
    probs, probs_rest, own, other, weight_row = refs[groups + 5 + others : groups + 10 + others]
    sums, peak, inverse, scale, mass, tall, tail = refs[-7:]
    h, width = own.shape
    rows = moved_rest.shape[0]
    block = probs.shape[2]

    best = gathered[0][0:1, 0:rows]
    for g in gathered[1:]:
        best = jnp.maximum(best, g[0:1, 0:rows])
    whole = jnp.zeros((1, rows), F32)
    for g in gathered:
        whole += g[1:2, 0:rows] * jnp.exp(g[0:1, 0:rows] - best)
    over = 1.0 / whole
    for j in range(GROUP):
        peak[:, j * rows : (j + 1) * rows] = jnp.broadcast_to(best, (8, rows))
        inverse[:, j * rows : (j + 1) * rows] = jnp.broadcast_to(over, (8, rows))
    for i in range(STEPS):
        scale[i] = jnp.exp(tops[i] - peak[...]) * inverse[...]

    last = weights_rest[...] * (jnp.exp(tops[STEPS, 0:1, 0:rows] - best) * over)
    last_low = last.astype(BF16)
    probs_rest[...] = last_low
    mass[...] = jnp.zeros(mass.shape, F32)
    mass[:, 0:1] = jnp.sum(last, axis=1, keepdims=True)
    for i in range(STEPS):
        part = mass[...]
        for q in range(0, block, 128):
            prob = weights[i, :, q : q + 128] * scale[i, 0:1, q : q + 128]
            probs[i, :, q : q + 128] = prob.astype(BF16)
            part += prob
        mass[...] = part
    accumulate(sums, probs, probs_rest, moved, moved_rest, rest_at)
    split_pair(sums, own, other)
    row = column_to_row(jnp.sum(mass[...], axis=1, keepdims=True), length, tall)
    weight_row[...] = jnp.broadcast_to(row, weight_row.shape)
    other[h : h + TAIL, :] = tail_block(row, width, tail)


def sums_body(probs, probs_rest, moved, moved_rest, *refs, others, rest_at):
    own, other = refs[others : others + 2]
    sums = refs[-1]
    accumulate(sums, probs, probs_rest, moved, moved_rest, rest_at)
    split_pair(sums, own, other)


def first_pair_body(own, received, weight_row, message, chip_row, tail):
    h, width = own.shape
    message[0:h, :] = (own[...] + received[0:h, :].astype(F32)).astype(BF16)
    length = weight_row.shape[1]
    row = weight_row[0:1, :] + row_of_tail(received[h : h + TAIL, :].astype(F32), width, length)
    chip_row[...] = jnp.broadcast_to(row, chip_row.shape)
    message[h : h + TAIL, :] = tail_block(row, width, tail)


def pair_body(own, received, first, message):
    h = own.shape[0]
    message[0:h, :] = (own[...] + received[...].astype(F32)).astype(BF16)
    message[h : h + TAIL, :] = first[h : h + TAIL, :]


def finish_body(*refs, count):
    messages = refs[:count]
    own, received, chip_row, class_sums, class_weight = refs[count:]
    h, width = own.shape
    rotations, classes = class_weight.shape[1], class_weight.shape[0]
    length = chip_row.shape[1]
    x = own[...] + received[...].astype(F32)
    row = chip_row[0:1, :]
    for m in messages:
        x += m[0:h, :].astype(F32)
        row += row_of_tail(m[h : h + TAIL, :].astype(F32), width, length)
    class_sums[...] = x
    shape = (classes, length)
    at = lax.broadcasted_iota(jnp.int32, shape, 1)
    mine = at - at // classes * classes == lax.broadcasted_iota(jnp.int32, shape, 0)
    spread_out = jnp.where(mine, jnp.broadcast_to(row, shape), 0.0)
    shape = (length, rotations)
    pick = lax.broadcasted_iota(jnp.int32, shape, 0) // classes == lax.broadcasted_iota(
        jnp.int32, shape, 1
    )
    class_weight[...] = lax.dot_general(
        spread_out,
        pick.astype(F32),
        (((1,), (0,)), ((), ())),
        precision=lax.Precision.HIGHEST,
        preferred_element_type=F32,
    )


VMEM = pl.BlockSpec(memory_space=pltpu.VMEM)


def make_on_device(dom, cls):
    pairs = dom // 2

    def swap(x, axis, size, k):
        return lax.ppermute(x, axis, [(i, i ^ k) for i in range(size)])

    def on_device(particles, references, noise_weight):
        rows, part_width = particles.shape
        classes, rotations, width = references.shape
        h = classes * rotations
        length = -(-h // width) * width
        block = GROUP * rows
        shape = jax.ShapeDtypeStruct
        place = lax.axis_index("dom")
        where = jnp.stack([place, place % 2, lax.axis_index("cls")]).astype(jnp.int32)

        def call(body, shapes, name, scratch=(), limit=2, aliases=None):
            def run(*args):
                scalars = args[0] is where
                specs = [VMEM] * (len(args) - scalars)
                spec = pltpu.PrefetchScalarGridSpec(
                    num_scalar_prefetch=int(scalars),
                    grid=(),
                    in_specs=specs,
                    out_specs=[VMEM] * len(shapes),
                    scratch_shapes=list(scratch),
                )
                params = pltpu.CompilerParams(vmem_limit_bytes=limit * 1024 * 1024)
                return pl.pallas_call(
                    body,
                    grid_spec=spec,
                    out_shape=shapes,
                    compiler_params=params,
                    input_output_aliases=aliases or {},
                    name=name,
                )(*args)

            return run

        pieces = [particles] + [swap(particles, "cls", cls, k) for k in range(1, cls)]

        ref_rows = references.transpose(1, 0, 2).reshape(h, width)
        slab = lax.dynamic_slice_in_dim(noise_weight, (place % pairs) * width, width)
        (message,) = call(
            lambda *r: prepare_body(None, *r),
            [shape((h + TAIL, width), BF16)],
            "prepare",
            [pltpu.VMEM((length, 128), F32), pltpu.VMEM((TAIL, width), F32)],
        )(ref_rows, slab.reshape(1, width))

        even = [message] + [swap(message, "dom", dom, 2 * k) for k in range(1, pairs)]
        odd = [swap(m, "dom", dom, 1) for m in even]
        slices = [m for both in zip(even, odd) for m in both]

        tables = np.stack(phase_tables())
        angles = call(
            lambda *r: table_body(*r, width=width),
            [shape(tables.shape[1:], F32)] * 2,
            "tables",
        )(where, tables)

        *moved, moved_rest = call(
            lambda *r: shift_body(*r, parts=cls, pairs=pairs, width=width),
            [pltpu.VMEM((MAIN * rows, 2 * width), BF16)] * pairs + [shape((rows, F), BF16)],
            "shift",
            limit=4,
            scratch=[pltpu.VMEM((rows, F), F32)] * 2,
        )(where, *pieces, *angles)

        weights, weights_rest, tops, stats, *moved = call(
            lambda *r: score_body(*r, parts=dom, pairs=pairs, length=length),
            [
                shape((STEPS, h, block), F32),
                shape((h, rows), F32),
                shape((STEPS + 1, 8, block), F32),
                shape((8, 128), F32),
            ]
            + [pltpu.VMEM((MAIN * rows, 2 * width), BF16)] * pairs,
            "score",
            aliases={dom + k: 4 + k for k in range(pairs)},
            limit=7,
            scratch=[
                pltpu.VMEM((h, F), BF16),
                pltpu.VMEM((h, 128), F32),
                pltpu.VMEM((h, block), F32),
                pltpu.VMEM((h, block), F32),
                pltpu.VMEM((STEPS, 8, block), F32),
            ],
        )(*slices, *moved, moved_rest)

        gathered = [stats] + [swap(stats, "cls", cls, k) for k in range(1, cls)]

        accumulator = pltpu.VMEM((h, 2 * width), F32)
        order = list(range(pairs - 1, -1, -1))
        messages = []
        probs, probs_rest, own, other, weight_row, *kept = call(
            lambda *r: first_sums_body(
                *r, groups=cls, others=pairs - 1, length=length, rest_at=order[0] * 2 * width
            ),
            [
                shape((STEPS, h, block), BF16),
                shape((h, rows), BF16),
                shape((h, width), F32),
                shape((h + TAIL, width), BF16),
                shape((8, length), F32),
            ]
            + [pltpu.VMEM((MAIN * rows, 2 * width), BF16)] * (pairs - 1),
            "sums_first",
            aliases={cls + 5 + k: 5 + k for k in range(pairs - 1)},
            limit=4,
            scratch=[
                accumulator,
                pltpu.VMEM((8, block), F32),
                pltpu.VMEM((8, block), F32),
                pltpu.VMEM(tops.shape, F32),
                pltpu.VMEM((h, 128), F32),
                pltpu.VMEM((length, 128), F32),
                pltpu.VMEM((TAIL, width), F32),
            ],
        )(*gathered, weights, weights_rest, tops, moved[order[0]], moved_rest, *moved[:-1])
        received = swap(other, "dom", dom, 1)
        first, chip_row = call(
            first_pair_body,
            [shape((h + TAIL, width), BF16), shape((8, length), F32)],
            "pair_first",
            [pltpu.VMEM((TAIL, width), F32)],
        )(own, received, weight_row)
        messages.append(swap(first, "dom", dom, 2 * order[0]))

        for k in order[1:]:
            own, other, *kept = call(
                lambda *r: sums_body(*r, others=k, rest_at=k * 2 * width),
                [shape((h, width), F32), shape((h, width), BF16)]
                + [pltpu.VMEM((MAIN * rows, 2 * width), BF16)] * k,
                "sums",
                [accumulator],
                aliases={4 + j: 2 + j for j in range(k)},
            )(probs, probs_rest, kept[k], moved_rest, *kept[:k])
            received = swap(other, "dom", dom, 1)
            if k:
                (summed,) = call(pair_body, [shape((h + TAIL, width), BF16)], "pair")(
                    own, received, first
                )
                messages.append(swap(summed, "dom", dom, 2 * k))

        sums, class_weight = call(
            lambda *r: finish_body(*r, count=len(messages)),
            [shape((h, width), F32), shape((classes, rotations), F32)],
            "finish",
        )(*messages, own, received, chip_row)
        return sums.reshape(rotations, classes, width).transpose(1, 0, 2), class_weight

    return on_device


def solution(mesh):
    return jax.shard_map(
        make_on_device(mesh.shape["dom"], mesh.shape["cls"]),
        mesh=mesh,
        in_specs=(P("dom", "cls"), P("cls", None, "dom"), P()),
        out_specs=(P("cls", None, "dom"), P("cls", None)),
        check_vma=False,
    )
```

time: 495 us -> 84.5 us (0.17)
  local copies, waits for them, and re-layouts: 144 us -> 6.16 us
  matrix products: 135 us -> 0 us
  other arithmetic: 107 us -> 0.08 us
  blocking collectives: 43.6 us -> 0 us
  Pallas kernels: 0 us -> 34.5 us
  starting transfers between devices: 0.08 us -> 21.3 us
  waiting for transfers between devices: 42.2 us -> 21.3 us
  between operations: 14.1 us -> 0.8 us
    dot_general x81 -> x0, matrix products: 135 us -> none  [the longest x54 80.1 us: block_scores(): lax.dot_general(flat, ref_rows, (((1,), (1,)), ((), ())), preferred_eleme...]
    another operation x54 -> x1, other arithmetic: 76.2 us -> 0.08 us  [on_device(): jnp.stack([place, place % 2, lax.axis_index('cls')]).astype(jnp.int32)]
    reshape x30 -> x0, local copies, waits for them, and re-layouts: 57.6 us -> none  [the longest x27 53.6 us: block_scores(): return (flat, scores.reshape(block_shifts, rows_here, ref_rows.shape[0]))]
    dynamic_slice x54 -> x1, local copies, waits for them, and re-layouts: 52.9 us -> 0.76 us  [on_device(): slab = lax.dynamic_slice_in_dim(noise_weight, place % pairs * width, width)]
    pallas_call x0 -> x12, Pallas kernels: none -> 34.5 us  [run(): pl.pallas_call(body, grid_spec=spec, out_shape=shapes, compiler_params=pa...]
    psum x2 -> x0, blocking collectives: 22.6 us -> none  [the longest x1 14.5 us: on_device(): lax.psum(weights_total, 'dom').reshape(classes_here, rotations)]
    sub x110 -> x0, local copies, waits for them, and re-layouts: 21.7 us -> none  [the longest x54 18 us: second_pass(): probs = jnp.exp(scores - top[None, :, None]) / total[None, :, None]]
    reduce_scatter x1 -> x0, waiting for transfers between devices: 21.4 us -> none  [on_device(): lax.psum_scatter(sums.reshape(classes_here, rotations, -1), 'dom', scatte...]
  transfers between devices with their start and end apart: 2 -> 20, of which waited for: 2 -> 9; matrix products, arithmetic and copies ran while one was open for 1% -> 0% of each run, Pallas kernels for 0% -> 20%
where the time goes in v2:
time: 84.5 us; the launch traced here: 84.1 us
  Pallas kernels  34.5 us (41%)
  starting transfers between devices  21.3 us (25%)
  waiting for transfers between devices  21.3 us (25%)
  local copies, waits for them, and re-layouts  6.16 us (7%)
    pallas_call x12, Pallas kernels, run(): pl.pallas_call(body, grid_spec=spec, out_shape=shapes, compiler_params=pa...  34.5 us
    ppermute x20, waiting for transfers between devices, swap(): return lax.ppermute(x, axis, [(i, i ^ k) for i in range(size)])  21.3 us
    ppermute x20, starting transfers between devices, swap(): return lax.ppermute(x, axis, [(i, i ^ k) for i in range(size)])  21.3 us
    unnamed x14, local copies, waits for them, and re-layouts  5.4 us
  transfers between devices with their start and end apart: 20, of which 9 were waited for; matrix products, arithmetic and copies ran while one was open for 0% of the time, Pallas kernels for 20%

profile of v2, /device:TPU:0, one launch (start us, length us, event | category | flops | bytes accessed | tf_op | source)
XLA Modules:
  0.0 84.1 jit_solution(6213433316804244700)
XLA Ops:
  1.4 1.0 %copy-done.1 = f32[8,36,256]{2,0,1:T(8,128)S(1)} copy-done((f32[8,36,256]{2,0,1:T(8,128)S(1)}, f32[8,36,256]{2,0,1:T(8,128)}, u32[]{:S(2)}) %copy-start.1) | copy-done | bytes 294936
  2.6 5.1 %collective-permute-start.5 = (bf16[304,256]{1,0:T(8,128)(2,1)S(1)}, bf16[304,256]{1,0:T(8,128)(2,1)S(1)}, u32[]{:S(2)}, u32[]{:S(2)}) collective-permute-start(bf16[304,256]{1,0:T(8,128)(2,1)S(1)} %prepare.1.r_0_), channel_id=1, source_target_pairs={{0,24},{4,28},{8,16},{12,20},{16,8},{20,12},{24,0},{28,4},{1,25},{... | collective-permute-start | bytes 466952 | tf_op jit(solution)/shard_map/ppermute | solution.py:321
  8.3 1.7 %collective-permute-start.8 = (bf16[96,512]{1,0:T(8,128)(2,1)}, bf16[96,512]{1,0:T(8,128)(2,1)S(1)}, u32[]{:S(2)}, u32[]{:S(2)}) collective-permute-start(bf16[96,512]{1,0:T(8,128)(2,1)} %r_1_.2), channel_id=1, source_target_pairs={{0,2},{1,3},{2,0},{3,1},{4,6},{5,7},{6,4},{7,5},{8,10},{9,11},{10,... | collective-permute-start | bytes 294920 | tf_op jit(solution)/shard_map/ppermute | solution.py:321
  10.0 1.5 %collective-permute-start.7 = (bf16[96,512]{1,0:T(8,128)(2,1)}, bf16[96,512]{1,0:T(8,128)(2,1)S(1)}, u32[]{:S(2)}, u32[]{:S(2)}) collective-permute-start(bf16[96,512]{1,0:T(8,128)(2,1)} %r_1_.2), channel_id=1, source_target_pairs={{0,1},{1,0},{2,3},{3,2},{4,5},{5,4},{6,7},{7,6},{8,9},{9,8},{10,11... | collective-permute-start | bytes 294920 | tf_op jit(solution)/shard_map/ppermute | solution.py:321
  11.5 1.7 %collective-permute-done.8.r_3_ = bf16[96,512]{1,0:T(8,128)(2,1)S(1)} collective-permute-done((bf16[96,512]{1,0:T(8,128)(2,1)}, bf16[96,512]{1,0:T(8,128)(2,1)S(1)}, u32[]{:S(2)}, u32[]{:S(2)}) %collective-permute-start.8) | collective-permute-done | bytes 98336 | tf_op jit(solution)/shard_map/ppermute | solution.py:321
  14.3 6.6 %collective-permute-done.3.r_4_ = bf16[304,256]{1,0:T(8,128)(2,1)S(1)} collective-permute-done((bf16[304,256]{1,0:T(8,128)(2,1)S(1)}, bf16[304,256]{1,0:T(8,128)(2,1)S(1)}, u32[]{:S(2)}, u32[]{:S(2)}) %collective-permute-start.3) | collective-permute-done | bytes 155680 | tf_op jit(solution)/shard_map/ppermute | solution.py:321
  21.4 2.4 %collective-permute-start.9 = (bf16[96,512]{1,0:T(8,128)(2,1)}, bf16[96,512]{1,0:T(8,128)(2,1)S(1)}, u32[]{:S(2)}, u32[]{:S(2)}) collective-permute-start(bf16[96,512]{1,0:T(8,128)(2,1)} %r_1_.2), channel_id=1, source_target_pairs={{0,3},{1,2},{2,1},{3,0},{4,7},{5,6},{6,5},{7,4},{8,11},{9,10},{10,... | collective-permute-start | bytes 294920 | tf_op jit(solution)/shard_map/ppermute | solution.py:321
  23.9 1.1 %copy-done = f32[2,88,1024]{2,1,0:T(8,128)S(1)} copy-done((f32[2,88,1024]{2,1,0:T(8,128)S(1)}, f32[2,88,1024]{2,1,0:T(8,128)}, u32[]{:S(2)}) %copy-start) | copy-done | bytes 720920
  25.6 1.6 %collective-permute-done.9.r_4_ = bf16[96,512]{1,0:T(8,128)(2,1)S(1)} collective-permute-done((bf16[96,512]{1,0:T(8,128)(2,1)}, bf16[96,512]{1,0:T(8,128)(2,1)S(1)}, u32[]{:S(2)}, u32[]{:S(2)}) %collective-permute-start.9) | collective-permute-done | bytes 98336 | tf_op jit(solution)/shard_map/ppermute | solution.py:321
  27.3 0.9 %copy-done.2 = bf16[96,512]{1,0:T(8,128)(2,1)S(1)} copy-done((bf16[96,512]{1,0:T(8,128)(2,1)S(1)}, bf16[96,512]{1,0:T(8,128)(2,1)}, u32[]{:S(2)}) %copy-start.2) | copy-done | bytes 98328
  29.9 8.7 %shift.1 = (bf16[7680,512]{1,0:T(8,128)(2,1)S(1)}, bf16[7680,512]{1,0:T(8,128)(2,1)S(1)}, bf16[7680,512]{1,0:T(8,128)(2,1)S(1)}, bf16[7680,512]{1,0:T(8,128)(2,1)S(1)}, bf16[96,2048]{1,0:T(8,128)(2,1)S(1)}) custom-call(s32[3]{0:T(128)S(1)} %pad_add_fusion.r_0_, bf16[96,512]{1,0:T(8,128)(2,1)S(1)} %copy-done.2, bf16[96,512]{1,0:T(8,128)(2,1)S(1)} %copy-done.6, ...), custom_call_target="tpu_custom_call" | custom-call | tf_op jit(solution)/shard_map/shift/pallas_call | solution.py:345
  38.7 12.4 %score.1 = (f32[10,288,768]{2,1,0:T(8,128)S(1)}, f32[288,96]{1,0:T(8,128)S(1)}, f32[11,8,768]{2,1,0:T(8,128)S(1)}, f32[8,128]{1,0:T(8,128)S(1)}, bf16[7680,512]{...) custom-call(bf16[304,256]{1,0:T(8,128)(2,1)S(1)} %prepare.1.r_0_, ...), custom_call_target="tpu_custom_call", output_to_operand_aliasing={{4}: (8, {}), {5}: (9, {}), {6}: (10, {}), {7}: (11, {})} | custom-call | tf_op jit(solution)/shard_map/score/pallas_call | solution.py:345
  51.1 2.5 %collective-permute-start.12 = (f32[8,128]{1,0:T(8,128)S(1)}, f32[8,128]{1,0:T(8,128)S(1)}, u32[]{:S(2)}, u32[]{:S(2)}) collective-permute-start(f32[8,128]{1,0:T(8,128)S(1)} %get-tuple-element.45.r_0_), channel_id=1, source_target_pairs={{0,3},{1,2},{2,1},{3,0},{4,7},{5,6},{6,5},{7,4},{8,11},{9,10},{10,... | collective-permute-start | bytes 12296 | tf_op jit(solution)/shard_map/ppermute | solution.py:321
  54.6 1.0 %collective-permute-done.12.r_3_ = f32[8,128]{1,0:T(8,128)S(1)} collective-permute-done((f32[8,128]{1,0:T(8,128)S(1)}, f32[8,128]{1,0:T(8,128)S(1)}, u32[]{:S(2)}, u32[]{:S(2)}) %collective-permute-start.12) | collective-permute-done | bytes 4128 | tf_op jit(solution)/shard_map/ppermute | solution.py:321
  55.7 1.5 %collective-permute-done.11.r_2_ = f32[8,128]{1,0:T(8,128)S(1)} collective-permute-done((f32[8,128]{1,0:T(8,128)S(1)}, f32[8,128]{1,0:T(8,128)S(1)}, u32[]{:S(2)}, u32[]{:S(2)}) %collective-permute-start.11) | collective-permute-done | bytes 4128 | tf_op jit(solution)/shard_map/ppermute | solution.py:321
  57.7 4.0 %sums_first.1 = (bf16[10,288,768]{2,1,0:T(8,128)(2,1)S(1)}, bf16[288,96]{1,0:T(8,128)(2,1)S(1)}, f32[288,256]{1,0:T(8,128)S(1)}, bf16[304,256]{1,0:T(8,128)(2,1)...) custom-call(f32[8,128]{1,0:T(8,128)S(1)} %get-tuple-element.45.r_0_,, ...), custom_call_target="tpu_custom_call", output_to_operand_aliasing={{5}: (9, {}), {6}: (10, {}), {7}: (11, {})} | custom-call | tf_op jit(solution)/shard_map/sums_first/pallas_call | solution.py:345
  61.8 2.5 %sums.3 = (f32[288,256]{1,0:T(8,128)S(1)}, bf16[288,256]{1,0:T(8,128)(2,1)S(1)}, bf16[7680,512]{1,0:T(8,128)(2,1)S(1)}, bf16[7680,512]{1,0:T(8,128)(2,1)S(1)}) custom-call(bf16[10,288,768]{2,1,0:T(8,128)(2,1)S(1)} %get-tuple-element.57.r_0_, bf16[288,96]{1,0:T(8,128)(2,1)S(1)} %get-tuple-element.58.r_1_, ...), custom_call_target="tpu_custom_call", output_to_operand_aliasing={{2}: (4, {}), {3}: (5, {})} | custom-call | tf_op jit(solution)/shard_map/sums/pallas_call | solution.py:345
  64.8 2.5 %sums.4 = (f32[288,256]{1,0:T(8,128)S(1)}, bf16[288,256]{1,0:T(8,128)(2,1)S(1)}, bf16[7680,512]{1,0:T(8,128)(2,1)S(1)}) custom-call(bf16[10,288,768]{2,1,0:T(8,128)(2,1)S(1)} %get-tuple-element.57.r_0_, bf16[288,96]{1,0:T(8,128)(2,1)S(1)} %get-tuple-element.58.r_1_, bf16[7680,512]{1,0:T(8,128)(2,1)S(1)} %get-tuple-element.64.r_2_, ...), custom_call_target="tpu_custom_call", output_to_operand_aliasing={{2}: (4, {})} | custom-call | tf_op jit(solution)/shard_map/sums/pallas_call | solution.py:345
  67.5 2.5 %collective-permute-start.14 = (bf16[304,256]{1,0:T(8,128)(2,1)S(1)}, bf16[304,256]{1,0:T(8,128)(2,1)S(1)}, u32[]{:S(2)}, u32[]{:S(2)}) collective-permute-start(bf16[304,256]{1,0:T(8,128)(2,1)S(1)} %get-tuple-element.56.first), channel_id=1, source_target_pairs={{0,24},{4,28},{8,16},{12,20},{16,8},{20,12},{24,0},{28,4},{1,25},{... | collective-permute-start | bytes 466952 | tf_op jit(solution)/shard_map/ppermute | solution.py:321
  70.2 2.0 %collective-permute-start.18 = (bf16[304,256]{1,0:T(8,128)(2,1)S(1)}, bf16[304,256]{1,0:T(8,128)(2,1)S(1)}, u32[]{:S(2)}, u32[]{:S(2)}) collective-permute-start(bf16[304,256]{1,0:T(8,128)(2,1)S(1)} %pair.3), channel_id=1, source_target_pairs={{0,8},{4,12},{8,0},{12,4},{16,24},{20,28},{24,16},{28,20},{1,9},{5... | collective-permute-start | bytes 466952 | tf_op jit(solution)/shard_map/ppermute | solution.py:321
  72.2 2.5 %sums.5 = (f32[288,256]{1,0:T(8,128)S(1)}, bf16[288,256]{1,0:T(8,128)(2,1)S(1)}) custom-call(bf16[10,288,768]{2,1,0:T(8,128)(2,1)S(1)} %get-tuple-element.57.r_0_, bf16[288,96]{1,0:T(8,128)(2,1)S(1)} %get-tuple-element.58.r_1_, bf16[7680,512]{1,0:T(8,128)(2,1)S(1)} %get-tuple-element.68.r_2_, bf16[96,2048]{1,0:T(8,128)(2,1)S(1)} %get-tuple-element.44.r_12_.r_8_.r_3_), custom_call_target="tpu_custom_call" | custom-call | tf_op jit(solution)/shard_map/sums/pallas_call | solution.py:345
  74.7 1.4 %collective-permute-done.19.r_4_ = bf16[288,256]{1,0:T(8,128)(2,1)S(1)} collective-permute-done((bf16[288,256]{1,0:T(8,128)(2,1)S(1)}, bf16[288,256]{1,0:T(8,128)(2,1)S(1)}, u32[]{:S(2)}, u32[]{:S(2)}) %collective-permute-start.19) | collective-permute-done | bytes 147488 | tf_op jit(solution)/shard_map/ppermute | solution.py:321
  76.3 6.8 %collective-permute-done.16.r_1_ = bf16[304,256]{1,0:T(8,128)(2,1)S(1)} collective-permute-done((bf16[304,256]{1,0:T(8,128)(2,1)S(1)}, bf16[304,256]{1,0:T(8,128)(2,1)S(1)}, u32[]{:S(2)}, u32[]{:S(2)}) %collective-permute-start.16) | collective-permute-done | bytes 155680 | tf_op jit(solution)/shard_map/ppermute | solution.py:321
  83.1 1.0 %finish.1 = (f32[288,256]{1,0:T(8,128)}, f32[8,36]{1,0:T(8,128)}) custom-call(bf16[304,256]{1,0:T(8,128)(2,1)S(1)} %collective-permute-done.14.r_0_, bf16[304,256]{1,0:T(8,128)(2,1)S(1)} %collective-permute-done.16.r_1_, bf16[304,256]{1,0:T(8,128)(2,1)S(1)} %collective-permute-done.18.r_2_, f32[288,256]{1,0:T(8,128)S(1)} %get-tuple-element.69.r_3_, ...), custom_call_target="tpu_custom_call" | custom-call | tf_op jit(solution)/shard_map/finish/pallas_call | solution.py:345
  (44 shorter events, 8.6 us)
Async XLA Ops:
  1.4 1.0 %copy-start.1 = (f32[8,36,256]{2,0,1:T(8,128)S(1)}, f32[8,36,256]{2,0,1:T(8,128)}, u32[]{:S(2)}) copy-start(f32[8,36,256]{2,0,1:T(8,128)} %param.5) | copy-start | bytes 884740
  2.6 11.2 %collective-permute-start.5 = (bf16[304,256]{1,0:T(8,128)(2,1)S(1)}, bf16[304,256]{1,0:T(8,128)(2,1)S(1)}, u32[]{:S(2)}, u32[]{:S(2)}) collective-permute-start(bf16[304,256]{1,0:T(8,128)(2,1)S(1)} %prepare.1.r_0_), channel_id=1, source_target_pairs={{0,24},{4,28},{8,16},{12,20},{16,8},{20,12},{24,0},{28,4},{1,25},{... | collective-permute-start | bytes 466952 | tf_op jit(solution)/shard_map/ppermute | solution.py:321
  7.7 13.2 %collective-permute-start.3 = (bf16[304,256]{1,0:T(8,128)(2,1)S(1)}, bf16[304,256]{1,0:T(8,128)(2,1)S(1)}, u32[]{:S(2)}, u32[]{:S(2)}) collective-permute-start(bf16[304,256]{1,0:T(8,128)(2,1)S(1)} %prepare.1.r_0_), channel_id=1, source_target_pairs={{0,16},{4,20},{8,24},{12,28},{16,0},{20,4},{24,8},{28,12},{1,17},{... | collective-permute-start | bytes 466952 | tf_op jit(solution)/shard_map/ppermute | solution.py:321
  7.7 13.2 %collective-permute-start.1 = (bf16[304,256]{1,0:T(8,128)(2,1)S(1)}, bf16[304,256]{1,0:T(8,128)(2,1)S(1)}, u32[]{:S(2)}, u32[]{:S(2)}) collective-permute-start(bf16[304,256]{1,0:T(8,128)(2,1)S(1)} %prepare.1.r_0_), channel_id=1, source_target_pairs={{0,8},{4,12},{8,0},{12,4},{16,24},{20,28},{24,16},{28,20},{1,9},{5... | collective-permute-start | bytes 466952 | tf_op jit(solution)/shard_map/ppermute | solution.py:321
  8.3 4.8 %collective-permute-start.8 = (bf16[96,512]{1,0:T(8,128)(2,1)}, bf16[96,512]{1,0:T(8,128)(2,1)S(1)}, u32[]{:S(2)}, u32[]{:S(2)}) collective-permute-start(bf16[96,512]{1,0:T(8,128)(2,1)} %r_1_.2), channel_id=1, source_target_pairs={{0,2},{1,3},{2,0},{3,1},{4,6},{5,7},{6,4},{7,5},{8,10},{9,11},{10,... | collective-permute-start | bytes 294920 | tf_op jit(solution)/shard_map/ppermute | solution.py:321
  10.0 11.4 %collective-permute-start.7 = (bf16[96,512]{1,0:T(8,128)(2,1)}, bf16[96,512]{1,0:T(8,128)(2,1)S(1)}, u32[]{:S(2)}, u32[]{:S(2)}) collective-permute-start(bf16[96,512]{1,0:T(8,128)(2,1)} %r_1_.2), channel_id=1, source_target_pairs={{0,1},{1,0},{2,3},{3,2},{4,5},{5,4},{6,7},{7,6},{8,9},{9,8},{10,11... | collective-permute-start | bytes 294920 | tf_op jit(solution)/shard_map/ppermute | solution.py:321
  13.8 24.9 %collective-permute-start = (bf16[304,256]{1,0:T(8,128)(2,1)S(1)}, bf16[304,256]{1,0:T(8,128)(2,1)S(1)}, u32[]{:S(2)}, u32[]{:S(2)}) collective-permute-start(bf16[304,256]{1,0:T(8,128)(2,1)S(1)} %prepare.1.r_0_), channel_id=1, source_target_pairs={{0,4},{4,0},{8,12},{12,8},{16,20},{20,16},{24,28},{28,24},{1,5},{5... | collective-permute-start | bytes 466952 | tf_op jit(solution)/shard_map/ppermute | solution.py:321
  13.8 24.9 %collective-permute-start.6 = (bf16[304,256]{1,0:T(8,128)(2,1)S(1)}, bf16[304,256]{1,0:T(8,128)(2,1)S(1)}, u32[]{:S(2)}, u32[]{:S(2)}) collective-permute-start(bf16[304,256]{1,0:T(8,128)(2,1)S(1)} %collective-permute-done.5.r_6_), channel_id=1, source_target_pairs={{0,4},{4,0},{8,12},{12,8},{16,20},{20,16},{24,28},{28,24},{1,5},{5... | collective-permute-start | bytes 466952 | tf_op jit(solution)/shard_map/ppermute | solution.py:321
  20.9 17.8 %collective-permute-start.4 = (bf16[304,256]{1,0:T(8,128)(2,1)S(1)}, bf16[304,256]{1,0:T(8,128)(2,1)}, u32[]{:S(2)}, u32[]{:S(2)}) collective-permute-start(bf16[304,256]{1,0:T(8,128)(2,1)S(1)} %collective-permute-done.3.r_4_), channel_id=1, source_target_pairs={{0,4},{4,0},{8,12},{12,8},{16,20},{20,16},{24,28},{28,24},{1,5},{5... | collective-permute-start | bytes 466952 | tf_op jit(solution)/shard_map/ppermute | solution.py:321
  20.9 17.8 %collective-permute-start.2 = (bf16[304,256]{1,0:T(8,128)(2,1)S(1)}, bf16[304,256]{1,0:T(8,128)(2,1)}, u32[]{:S(2)}, u32[]{:S(2)}) collective-permute-start(bf16[304,256]{1,0:T(8,128)(2,1)S(1)} %collective-permute-done.1.r_2_), channel_id=1, source_target_pairs={{0,4},{4,0},{8,12},{12,8},{16,20},{20,16},{24,28},{28,24},{1,5},{5... | collective-permute-start | bytes 466952 | tf_op jit(solution)/shard_map/ppermute | solution.py:321
  21.4 5.9 %copy-start.5 = (bf16[96,512]{1,0:T(8,128)(2,1)}, bf16[96,512]{1,0:T(8,128)(2,1)S(1)}, u32[]{:S(2)}) copy-start(bf16[96,512]{1,0:T(8,128)(2,1)S(1)} %collective-permute-done.7.r_2_) | copy-start | bytes 294916
  21.4 5.9 %collective-permute-start.9 = (bf16[96,512]{1,0:T(8,128)(2,1)}, bf16[96,512]{1,0:T(8,128)(2,1)S(1)}, u32[]{:S(2)}, u32[]{:S(2)}) collective-permute-start(bf16[96,512]{1,0:T(8,128)(2,1)} %r_1_.2), channel_id=1, source_target_pairs={{0,3},{1,2},{2,1},{3,0},{4,7},{5,6},{6,5},{7,4},{8,11},{9,10},{10,... | collective-permute-start | bytes 294920 | tf_op jit(solution)/shard_map/ppermute | solution.py:321
  23.9 1.1 %copy-start = (f32[2,88,1024]{2,1,0:T(8,128)S(1)}, f32[2,88,1024]{2,1,0:T(8,128)}, u32[]{:S(2)}) copy-start(f32[2,88,1024]{2,1,0:T(8,128)} %constant.39.clone.r_1_) | copy-start | bytes 2162692
  27.3 0.9 %copy-start.2 = (bf16[96,512]{1,0:T(8,128)(2,1)S(1)}, bf16[96,512]{1,0:T(8,128)(2,1)}, u32[]{:S(2)}) copy-start(bf16[96,512]{1,0:T(8,128)(2,1)} %r_1_.2) | copy-start | bytes 294916
  51.1 4.6 %collective-permute-start.12 = (f32[8,128]{1,0:T(8,128)S(1)}, f32[8,128]{1,0:T(8,128)S(1)}, u32[]{:S(2)}, u32[]{:S(2)}) collective-permute-start(f32[8,128]{1,0:T(8,128)S(1)} %get-tuple-element.45.r_0_), channel_id=1, source_target_pairs={{0,3},{1,2},{2,1},{3,0},{4,7},{5,6},{6,5},{7,4},{8,11},{9,10},{10,... | collective-permute-start | bytes 12296 | tf_op jit(solution)/shard_map/ppermute | solution.py:321
  53.6 3.6 %collective-permute-start.11 = (f32[8,128]{1,0:T(8,128)S(1)}, f32[8,128]{1,0:T(8,128)S(1)}, u32[]{:S(2)}, u32[]{:S(2)}) collective-permute-start(f32[8,128]{1,0:T(8,128)S(1)} %get-tuple-element.45.r_0_), channel_id=1, source_target_pairs={{0,2},{1,3},{2,0},{3,1},{4,6},{5,7},{6,4},{7,5},{8,10},{9,11},{10,... | collective-permute-start | bytes 12296 | tf_op jit(solution)/shard_map/ppermute | solution.py:321
  54.1 3.6 %collective-permute-start.10 = (f32[8,128]{1,0:T(8,128)S(1)}, f32[8,128]{1,0:T(8,128)S(1)}, u32[]{:S(2)}, u32[]{:S(2)}) collective-permute-start(f32[8,128]{1,0:T(8,128)S(1)} %get-tuple-element.45.r_0_), channel_id=1, source_target_pairs={{0,1},{1,0},{2,3},{3,2},{4,5},{5,4},{6,7},{7,6},{8,9},{9,8},{10,11... | collective-permute-start | bytes 12296 | tf_op jit(solution)/shard_map/ppermute | solution.py:321
  61.7 5.7 %collective-permute-start.13 = (bf16[304,256]{1,0:T(8,128)(2,1)S(1)}, bf16[304,256]{1,0:T(8,128)(2,1)S(1)}, u32[]{:S(2)}, u32[]{:S(2)}) collective-permute-start(bf16[304,256]{1,0:T(8,128)(2,1)S(1)} %get-tuple-element.54), channel_id=1, source_target_pairs={{0,4},{4,0},{8,12},{12,8},{16,20},{20,16},{24,28},{28,24},{1,5},{5... | collective-permute-start | bytes 466952 | tf_op jit(solution)/shard_map/ppermute | solution.py:321
  64.3 5.8 %collective-permute-start.15 = (bf16[288,256]{1,0:T(8,128)(2,1)S(1)}, bf16[288,256]{1,0:T(8,128)(2,1)S(1)}, u32[]{:S(2)}, u32[]{:S(2)}) collective-permute-start(bf16[288,256]{1,0:T(8,128)(2,1)S(1)} %get-tuple-element.63), channel_id=1, source_target_pairs={{0,4},{4,0},{8,12},{12,8},{16,20},{20,16},{24,28},{28,24},{1,5},{5... | collective-permute-start | bytes 442376 | tf_op jit(solution)/shard_map/ppermute | solution.py:321
  67.3 2.8 %collective-permute-start.17 = (bf16[288,256]{1,0:T(8,128)(2,1)S(1)}, bf16[288,256]{1,0:T(8,128)(2,1)S(1)}, u32[]{:S(2)}, u32[]{:S(2)}) collective-permute-start(bf16[288,256]{1,0:T(8,128)(2,1)S(1)} %get-tuple-element.67), channel_id=1, source_target_pairs={{0,4},{4,0},{8,12},{12,8},{16,20},{20,16},{24,28},{28,24},{1,5},{5... | collective-permute-start | bytes 442376 | tf_op jit(solution)/shard_map/ppermute | solution.py:321
  67.5 8.8 %collective-permute-start.14 = (bf16[304,256]{1,0:T(8,128)(2,1)S(1)}, bf16[304,256]{1,0:T(8,128)(2,1)S(1)}, u32[]{:S(2)}, u32[]{:S(2)}) collective-permute-start(bf16[304,256]{1,0:T(8,128)(2,1)S(1)} %get-tuple-element.56.first), channel_id=1, source_target_pairs={{0,24},{4,28},{8,16},{12,20},{16,8},{20,12},{24,0},{28,4},{1,25},{... | collective-permute-start | bytes 466952 | tf_op jit(solution)/shard_map/ppermute | solution.py:321
  70.1 13.0 %collective-permute-start.16 = (bf16[304,256]{1,0:T(8,128)(2,1)S(1)}, bf16[304,256]{1,0:T(8,128)(2,1)S(1)}, u32[]{:S(2)}, u32[]{:S(2)}) collective-permute-start(bf16[304,256]{1,0:T(8,128)(2,1)S(1)} %pair.2), channel_id=1, source_target_pairs={{0,16},{4,20},{8,24},{12,28},{16,0},{20,4},{24,8},{28,12},{1,17},{... | collective-permute-start | bytes 466952 | tf_op jit(solution)/shard_map/ppermute | solution.py:321
  70.2 12.9 %collective-permute-start.18 = (bf16[304,256]{1,0:T(8,128)(2,1)S(1)}, bf16[304,256]{1,0:T(8,128)(2,1)S(1)}, u32[]{:S(2)}, u32[]{:S(2)}) collective-permute-start(bf16[304,256]{1,0:T(8,128)(2,1)S(1)} %pair.3), channel_id=1, source_target_pairs={{0,8},{4,12},{8,0},{12,4},{16,24},{20,28},{24,16},{28,20},{1,9},{5... | collective-permute-start | bytes 466952 | tf_op jit(solution)/shard_map/ppermute | solution.py:321
  74.7 1.4 %collective-permute-start.19 = (bf16[288,256]{1,0:T(8,128)(2,1)S(1)}, bf16[288,256]{1,0:T(8,128)(2,1)S(1)}, u32[]{:S(2)}, u32[]{:S(2)}) collective-permute-start(bf16[288,256]{1,0:T(8,128)(2,1)S(1)} %get-tuple-element.70), channel_id=1, source_target_pairs={{0,4},{4,0},{8,12},{12,8},{16,20},{20,16},{24,28},{28,24},{1,5},{5... | collective-permute-start | bytes 442376 | tf_op jit(solution)/shard_map/ppermute | solution.py:321
  (3 other events, 2.4 us)

commit v3 on v2

--- a/solution.py
+++ b/solution.py
@@ -26,15 +26,12 @@
     freq = np.arange(HALF)
     fy = freq // WIN - WIN // 2
     fx = freq % WIN - WIN // 2
-    offset = np.arange(SHIFTS)
+    offset = np.arange(MAIN // 2)
     sy = offset // SHIFT_SIDE - SHIFT_SIDE // 2
     sx = offset % SHIFT_SIDE - SHIFT_SIDE // 2
     turns = sx[:, None] * fx[None, :] + sy[:, None] * fy[None, :]
     theta = (2.0 * math.pi / BOX) * turns
-    pad = -SHIFTS % GROUP
-    cosine = np.pad(np.cos(theta), ((0, pad), (0, 0))).astype(np.float32)
-    sine = np.pad(np.sin(theta), ((0, pad), (0, 0))).astype(np.float32)
-    return cosine, sine
+    return np.stack([np.cos(theta), np.sin(theta)]).astype(np.float32)
 
 
 def contract(x, y, dims):
@@ -77,15 +74,17 @@
 
 def prepare_body(where, refs, noise, message, tall, tail):
     h, width = refs.shape
+    at = pl.multiple_of(jnp.bitwise_and(where[0], HALF // width - 1) * width, 128)
     x = refs[...]
-    w = noise[...]
+    w = noise[:, pl.ds(at, width)]
     message[0:h, :] = (x * w).astype(BF16)
     half = 0.5 * jnp.sum(x * x * w, axis=1, keepdims=True)
     row = column_to_row(half, tall.shape[0], tall)
     message[h : h + TAIL, :] = tail_block(row, width, tail)
 
 
-def table_body(where, tables, cosine, sine, *, width):
+def table_body(where, tables, particles, cosine, sine, kept, *, width):
+    kept[...] = particles[...]
     count = HALF // width
     sign = jnp.where(where[0] < count, 1.0, -1.0).astype(F32)
     for k in range(count):
@@ -106,8 +105,11 @@
     for k in range(2 * pairs):
         at = pl.multiple_of(jnp.bitwise_xor(where[0], k) * width, 128)
         whole[:, k * width : (k + 1) * width] = plain[:, pl.ds(at, width)]
-
-    def move(s, store):
+    rest[...] = whole[...].astype(BF16)
+
+    def one(s, carry):
+        at = pl.multiple_of(2 * s * rows, rows)
+        back = pl.multiple_of((2 * s + 1) * rows, rows)
         c_all = cosine[pl.ds(s, 1), :]
         s_all = sine[pl.ds(s, 1), :]
         for k in range(pairs):
@@ -116,47 +118,55 @@
             s_row = s_all[:, q : q + width]
             a = whole[:, q : q + width]
             b = whole[:, HALF + q : HALF + q + width]
-            store(k, (a * c_row + b * s_row).astype(BF16))
-            store(k + pairs, (b * c_row - a * s_row).astype(BF16))
-
-    def one(s, carry):
-        at = pl.multiple_of(s * rows, rows)
-
-        def store(k, value):
-            outs[k // 2][pl.ds(at, rows), (k % 2) * width : (k % 2 + 1) * width] = value
-
-        move(s, store)
+            ac, bs, bc, sa = a * c_row, b * s_row, b * c_row, a * s_row
+            low = slice((k % 2) * width, (k % 2 + 1) * width)
+            outs[k // 2][pl.ds(at, rows), low] = (ac + bs).astype(BF16)
+            outs[(k + pairs) // 2][pl.ds(at, rows), low] = (bc - sa).astype(BF16)
+            outs[k // 2][pl.ds(back, rows), low] = (ac - bs).astype(BF16)
+            outs[(k + pairs) // 2][pl.ds(back, rows), low] = (bc + sa).astype(BF16)
         return carry
 
-    lax.fori_loop(0, MAIN, one, 0)
-
-    def store_rest(k, value):
-        rest[:, k * width : (k + 1) * width] = value
-
-    for s in range(MAIN, SHIFTS):
-        move(s, store_rest)
-
-
-def score_body(*refs, parts, pairs, length):
-    pieces = refs[:parts]
-    moved = refs[parts : parts + pairs]
-    moved_rest = refs[parts + pairs]
-    weights, weights_rest, tops, stats = refs[parts + pairs + 1 : parts + pairs + 5]
+    lax.fori_loop(0, MAIN // 2, one, 0)
+
+
+def stage_body(*refs, first, others, length, rest_at):
+    mine, sibling, moved, moved_rest = refs[:4]
+    count = 4 if first else 7
+    partial = None if first else refs[4:7]
+    scores, scores_rest, norms = refs[count + others : count + others + 3]
+    weighted = refs[-1]
+    h, span = weighted.shape
+    width = span // 2
+    block = scores.shape[2]
+    row = jnp.zeros((1, length), F32) if first else partial[2][0:1, :]
+    for k, piece in enumerate((mine, sibling)):
+        weighted[:, k * width : (k + 1) * width] = piece[0:h, :]
+        row += row_of_tail(piece[h : h + TAIL, :].astype(F32), width, length)
+    norms[...] = jnp.broadcast_to(row, norms.shape)
+    last = contract(weighted[...], moved_rest[:, rest_at : rest_at + span], ((1,), (1,)))
+    scores_rest[...] = last if first else partial[1][...] + last
+    for i in range(STEPS):
+        x = contract(weighted[...], moved[i * block : (i + 1) * block, :], ((1,), (1,)))
+        scores[i] = x if first else partial[0][i] + x
+
+
+def last_stage_body(*refs, others, length, rest_at):
+    mine, sibling, moved, moved_rest, scores, scores_rest, norms = refs[:7]
+    weights, weights_rest, tops, stats = refs[7 + others : 11 + others]
     weighted, half, even, odd, totals = refs[-5:]
     h, block = even.shape
     rows = moved_rest.shape[0]
-    width = pieces[0].shape[1]
-
-    row = jnp.zeros((1, length), F32)
-    for k in range(parts):
-        weighted[:, k * width : (k + 1) * width] = pieces[k][0:h, :]
-        row += row_of_tail(pieces[k][h : h + TAIL, :].astype(F32), width, length)
+    span = weighted.shape[1]
+    width = span // 2
+    row = norms[0:1, :]
+    for k, piece in enumerate((mine, sibling)):
+        weighted[:, k * width : (k + 1) * width] = piece[0:h, :]
+        row += row_of_tail(piece[h : h + TAIL, :].astype(F32), width, length)
     half[...] = jnp.broadcast_to(row, (128, length)).T[0:h, :]
 
     def multiply(i, target):
-        at = i * block if isinstance(i, int) else pl.multiple_of(i * block, block)
-        x = jnp.concatenate([m[pl.ds(at, block), :] for m in moved], axis=1)
-        target[...] = contract(weighted[...], x, ((1,), (1,)))
+        x = contract(weighted[...], moved[i * block : (i + 1) * block, :], ((1,), (1,)))
+        target[...] = scores[i] + x
 
     def soften(i, source):
         for q in range(0, block, 128):
@@ -169,19 +179,12 @@
             totals[i, :, q : q + 128] = jnp.broadcast_to(total, (8, 128))
 
     multiply(0, even)
-
-    def two(t, carry):
-        multiply(2 * t + 1, odd)
-        soften(2 * t, even)
-        multiply(2 * t + 2, even)
-        soften(2 * t + 1, odd)
-        return carry
-
-    lax.fori_loop(0, STEPS // 2 - 1, two, 0)
-    multiply(STEPS - 1, odd)
-    soften(STEPS - 2, even)
-    last = contract(weighted[...], moved_rest[...], ((1,), (1,))) - half[:, 0:1]
-    soften(STEPS - 1, odd)
+    for i in range(1, STEPS):
+        multiply(i, odd if i % 2 else even)
+        soften(i - 1, even if i % 2 else odd)
+    last = contract(weighted[...], moved_rest[:, rest_at : rest_at + span], ((1,), (1,)))
+    last = scores_rest[...] + last - half[:, 0:1]
+    soften(STEPS - 1, odd if (STEPS - 1) % 2 else even)
 
     best = jnp.max(last, axis=0, keepdims=True)
     last = jnp.exp(last - best)
@@ -212,10 +215,14 @@
     other[0:h, :] = sums[:, width : 2 * width].astype(BF16)
 
 
-def accumulate(sums, probs, probs_rest, moved, moved_rest, rest_at):
+def accumulate(sums, probs, probs_rest, moved, moved_rest, rest_at, ahead=None):
     block = probs.shape[2]
+    if ahead:
+        ahead(0)
     sums[...] = contract(probs_rest[...], moved_rest[:, rest_at : rest_at + sums.shape[1]], ((1,), (0,)))
     for i in range(STEPS):
+        if ahead and i + 1 < STEPS:
+            ahead(i + 1)
         sums[...] += contract(probs[i], moved[i * block : (i + 1) * block, :], ((1,), (0,)))
 
 
@@ -246,14 +253,16 @@
     probs_rest[...] = last_low
     mass[...] = jnp.zeros(mass.shape, F32)
     mass[:, 0:1] = jnp.sum(last, axis=1, keepdims=True)
-    for i in range(STEPS):
+
+    def normalise(i):
         part = mass[...]
         for q in range(0, block, 128):
             prob = weights[i, :, q : q + 128] * scale[i, 0:1, q : q + 128]
             probs[i, :, q : q + 128] = prob.astype(BF16)
             part += prob
         mass[...] = part
-    accumulate(sums, probs, probs_rest, moved, moved_rest, rest_at)
+
+    accumulate(sums, probs, probs_rest, moved, moved_rest, rest_at, normalise)
     split_pair(sums, own, other)
     row = column_to_row(jnp.sum(mass[...], axis=1, keepdims=True), length, tall)
     weight_row[...] = jnp.broadcast_to(row, weight_row.shape)
@@ -348,6 +357,7 @@
                     out_shape=shapes,
                     compiler_params=params,
                     input_output_aliases=aliases or {},
+                    cost_estimate=pl.CostEstimate(flops=1, transcendentals=0, bytes_accessed=1),
                     name=name,
                 )(*args)
 
@@ -356,24 +366,22 @@
         pieces = [particles] + [swap(particles, "cls", cls, k) for k in range(1, cls)]
 
         ref_rows = references.transpose(1, 0, 2).reshape(h, width)
-        slab = lax.dynamic_slice_in_dim(noise_weight, (place % pairs) * width, width)
         (message,) = call(
-            lambda *r: prepare_body(None, *r),
+            prepare_body,
             [shape((h + TAIL, width), BF16)],
             "prepare",
             [pltpu.VMEM((length, 128), F32), pltpu.VMEM((TAIL, width), F32)],
-        )(ref_rows, slab.reshape(1, width))
+        )(where, ref_rows, noise_weight.reshape(1, HALF))
 
         even = [message] + [swap(message, "dom", dom, 2 * k) for k in range(1, pairs)]
-        odd = [swap(m, "dom", dom, 1) for m in even]
-        slices = [m for both in zip(even, odd) for m in both]
-
-        tables = np.stack(phase_tables())
-        angles = call(
+        odd = [swap(message, "dom", dom, 1)]
+
+        tables = phase_tables()
+        *angles, pieces[0] = call(
             lambda *r: table_body(*r, width=width),
-            [shape(tables.shape[1:], F32)] * 2,
+            [shape(tables.shape[1:], F32)] * 2 + [shape(particles.shape, BF16)],
             "tables",
-        )(where, tables)
+        )(where, tables, particles)
 
         *moved, moved_rest = call(
             lambda *r: shift_body(*r, parts=cls, pairs=pairs, width=width),
@@ -383,26 +391,49 @@
             scratch=[pltpu.VMEM((rows, F), F32)] * 2,
         )(where, *pieces, *angles)
 
-        weights, weights_rest, tops, stats, *moved = call(
-            lambda *r: score_body(*r, parts=dom, pairs=pairs, length=length),
-            [
-                shape((STEPS, h, block), F32),
-                shape((h, rows), F32),
-                shape((STEPS + 1, 8, block), F32),
-                shape((8, 128), F32),
-            ]
-            + [pltpu.VMEM((MAIN * rows, 2 * width), BF16)] * pairs,
-            "score",
-            aliases={dom + k: 4 + k for k in range(pairs)},
-            limit=7,
-            scratch=[
-                pltpu.VMEM((h, F), BF16),
-                pltpu.VMEM((h, 128), F32),
-                pltpu.VMEM((h, block), F32),
-                pltpu.VMEM((h, block), F32),
-                pltpu.VMEM((STEPS, 8, block), F32),
-            ],
-        )(*slices, *moved, moved_rest)
+        held = pltpu.VMEM((MAIN * rows, 2 * width), BF16)
+        partial = []
+        for j in range(pairs):
+            last = j == pairs - 1
+            rest = [k for k in range(pairs) if k != j]
+            first_held = 4 if last else 3
+            first_other = 4 + len(partial)
+            aliases = {2: first_held + j}
+            aliases |= {first_other + n: first_held + k for n, k in enumerate(rest)}
+            if partial:
+                aliases |= {4: 0, 5: 1}
+            body = last_stage_body if last else stage_body
+            options = {} if last else {"first": not partial}
+            outs = [pltpu.VMEM((STEPS, h, block), F32), shape((h, rows), F32)]
+            scratch = [pltpu.VMEM((h, 2 * width), BF16)]
+            if last:
+                outs += [shape((STEPS + 1, 8, block), F32), shape((8, 128), F32)]
+                scratch += [
+                    pltpu.VMEM((h, 128), F32),
+                    pltpu.VMEM((h, block), F32),
+                    pltpu.VMEM((h, block), F32),
+                    pltpu.VMEM((STEPS, 8, block), F32),
+                ]
+            else:
+                outs += [shape((8, length), F32)]
+            if not last:
+                if partial:
+                    partial[2], even[j + 1] = lax.optimization_barrier((partial[2], even[j + 1]))
+                else:
+                    moved_rest, even[j + 1] = lax.optimization_barrier((moved_rest, even[j + 1]))
+                odd.append(swap(even[j + 1], "dom", dom, 1))
+            results = call(
+                lambda *r: body(
+                    *r, others=pairs - 1, length=length, rest_at=2 * j * width, **options
+                ),
+                outs + [held] * pairs,
+                "score",
+                scratch,
+                limit=7 if last else 4,
+                aliases=aliases,
+            )(even[j], odd[j], moved[j], moved_rest, *partial, *[moved[k] for k in rest])
+            partial, moved = list(results[:first_held]), results[first_held:]
+        weights, weights_rest, tops, stats = partial
 
         gathered = [stats] + [swap(stats, "cls", cls, k) for k in range(1, cls)]
 
@@ -442,8 +473,13 @@
             [pltpu.VMEM((TAIL, width), F32)],
         )(own, received, weight_row)
         messages.append(swap(first, "dom", dom, 2 * order[0]))
-
-        for k in order[1:]:
+        ready = first
+
+        for n, k in enumerate(order[1:]):
+            if not k:
+                probs_rest, messages[0] = lax.optimization_barrier((probs_rest, messages[0]))
+            elif n:
+                probs_rest, ready = lax.optimization_barrier((probs_rest, ready))
             own, other, *kept = call(
                 lambda *r: sums_body(*r, others=k, rest_at=k * 2 * width),
                 [shape((h, width), F32), shape((h, width), BF16)]
@@ -458,6 +494,7 @@
                     own, received, first
                 )
                 messages.append(swap(summed, "dom", dom, 2 * k))
+                ready = summed
 
         sums, class_weight = call(
             lambda *r: finish_body(*r, count=len(messages)),

time: 84.5 us -> 70.7 us (0.84)
  waiting for transfers between devices: 21.3 us -> 10.1 us
  local copies, waits for them, and re-layouts: 6.16 us -> 3.51 us
    ppermute x20, waiting for transfers between devices: 21.3 us -> 10.1 us  [swap(): return lax.ppermute(x, axis, [(i, i ^ k) for i in range(size)])]
    unnamed x14 -> x8, local copies, waits for them, and re-layouts: 5.4 us -> 3.51 us
    pallas_call x12 -> x15, Pallas kernels: 34.5 us -> 34.1 us  [run(): pl.pallas_call(body, grid_spec=spec, out_shape=shapes, compiler_params=pa...]
  transfers between devices with their start and end apart: 20 -> 20, of which waited for: 9 -> 6; matrix products, arithmetic and copies ran while one was open for 0% -> 0% of each run, Pallas kernels for 20% -> 35%
where the time goes in v3:
time: 70.7 us; the launch traced here: 70.4 us
  Pallas kernels  34.1 us (48%)
  starting transfers between devices  21.9 us (31%)
  waiting for transfers between devices  10.1 us (14%)
  local copies, waits for them, and re-layouts  3.51 us (5%)
  between operations  0.81 us (1%)
    pallas_call x15, Pallas kernels, run(): pl.pallas_call(body, grid_spec=spec, out_shape=shapes, compiler_params=pa...  34.1 us
    ppermute x20, starting transfers between devices, swap(): return lax.ppermute(x, axis, [(i, i ^ k) for i in range(size)])  21.9 us
    ppermute x20, waiting for transfers between devices, swap(): return lax.ppermute(x, axis, [(i, i ^ k) for i in range(size)])  10.1 us
    unnamed x8, local copies, waits for them, and re-layouts  3.51 us
  transfers between devices with their start and end apart: 20, of which 6 were waited for; matrix products, arithmetic and copies ran while one was open for 0% of the time, Pallas kernels for 35%

profile of v3, /device:TPU:0, one launch (start us, length us, event | category | flops | bytes accessed | tf_op | source)
XLA Modules:
  0.0 70.4 jit_solution(5911838568529474666)
XLA Ops:
  0.7 1.0 %copy-done.1 = f32[8,36,256]{2,0,1:T(8,128)S(1)} copy-done((f32[8,36,256]{2,0,1:T(8,128)S(1)}, f32[8,36,256]{2,0,1:T(8,128)}, u32[]{:S(2)}) %copy-start.1) | copy-done | bytes 294936
  3.1 3.1 %collective-permute-start.3 = (bf16[304,256]{1,0:T(8,128)(2,1)S(1)}, bf16[304,256]{1,0:T(8,128)(2,1)S(1)}, u32[]{:S(2)}, u32[]{:S(2)}) collective-permute-start(bf16[304,256]{1,0:T(8,128)(2,1)S(1)} %prepare.1.r_0_), channel_id=1, source_target_pairs={{0,8},{4,12},{8,0},{12,4},{16,24},{20,28},{24,16},{28,20},{1,9},{5... | collective-permute-start | bytes 466952 | tf_op jit(solution)/shard_map/ppermute | solution.py:330
  6.2 1.5 %collective-permute-start = (bf16[96,512]{1,0:T(8,128)(2,1)}, bf16[96,512]{1,0:T(8,128)(2,1)S(1)}, u32[]{:S(2)}, u32[]{:S(2)}) collective-permute-start(bf16[96,512]{1,0:T(8,128)(2,1)} %r_2_.1), channel_id=1, source_target_pairs={{0,1},{1,0},{2,3},{3,2},{4,5},{5,4},{6,7},{7,6},{8,9},{9,8},{10,11... | collective-permute-start | bytes 294920 | tf_op jit(solution)/shard_map/ppermute | solution.py:330
  7.7 1.5 %collective-permute-start.2 = (bf16[96,512]{1,0:T(8,128)(2,1)}, bf16[96,512]{1,0:T(8,128)(2,1)S(1)}, u32[]{:S(2)}, u32[]{:S(2)}) collective-permute-start(bf16[96,512]{1,0:T(8,128)(2,1)} %r_2_.1), channel_id=1, source_target_pairs={{0,3},{1,2},{2,1},{3,0},{4,7},{5,6},{6,5},{7,4},{8,11},{9,10},{10,... | collective-permute-start | bytes 294920 | tf_op jit(solution)/shard_map/ppermute | solution.py:330
  9.7 1.0 %copy-done = f32[2,40,1024]{2,1,0:T(8,128)S(1)} copy-done((f32[2,40,1024]{2,1,0:T(8,128)S(1)}, f32[2,40,1024]{2,1,0:T(8,128)}, u32[]{:S(2)}) %copy-start) | copy-done | bytes 327704
  12.1 2.7 %collective-permute-start.6 = (bf16[304,256]{1,0:T(8,128)(2,1)S(1)}, bf16[304,256]{1,0:T(8,128)(2,1)S(1)}, u32[]{:S(2)}, u32[]{:S(2)}) collective-permute-start(bf16[304,256]{1,0:T(8,128)(2,1)S(1)} %prepare.1.r_0_), channel_id=1, source_target_pairs={{0,16},{4,20},{8,24},{12,28},{16,0},{20,4},{24,8},{28,12},{1,17},{... | collective-permute-start | bytes 466952 | tf_op jit(solution)/shard_map/ppermute | solution.py:330
  14.9 6.6 %shift.1 = (bf16[7680,512]{1,0:T(8,128)(2,1)S(1)}, bf16[7680,512]{1,0:T(8,128)(2,1)S(1)}, bf16[7680,512]{1,0:T(8,128)(2,1)S(1)}, bf16[7680,512]{1,0:T(8,128)(2,1)S(1)}, bf16[96,2048]{1,0:T(8,128)(2,1)S(1)}) custom-call(s32[3]{0:T(128)S(1)} %pad_add_fusion.r_0_.where, bf16[96,512]{1,0:T(8,128)(2,1)S(1)} %get-tuple-element.69.r_1_, ...), custom_call_target="tpu_custom_call" | custom-call | flops 1 | bytes 1 | tf_op jit(solution)/shard_map/shift/pallas_call | solution.py:354
  21.7 2.4 %collective-permute-start.7 = (bf16[304,256]{1,0:T(8,128)(2,1)S(1)}, bf16[304,256]{1,0:T(8,128)(2,1)S(1)}, u32[]{:S(2)}, u32[]{:S(2)}) collective-permute-start(bf16[304,256]{1,0:T(8,128)(2,1)S(1)} %prepare.1.r_0_), channel_id=1, source_target_pairs={{0,24},{4,28},{8,16},{12,20},{16,8},{20,12},{24,0},{28,4},{1,25},{... | collective-permute-start | bytes 466952 | tf_op jit(solution)/shard_map/ppermute | solution.py:330
  24.2 2.5 %score.4 = (f32[10,288,768]{2,1,0:T(8,128)S(1)}, f32[288,96]{1,0:T(8,128)S(1)}, f32[8,512]{1,0:T(8,128)S(1)}, bf16[7680,512]{1,0:T(8,128)(2,1)S(1)}, bf16[7680,5...) custom-call(bf16[304,256]{1,0:T(8,128)(2,1)S(1)} %prepare.1.r_0_, ...), custom_call_target="tpu_custom_call", output_to_operand_aliasing={{3}: (2, {}), {4}: (4, {}), {5}: (5, {}), {6}: (6, {})} | custom-call | flops 1 | bytes 1 | tf_op jit(solution)/shard_map/score/pallas_call | solution.py:354
  27.0 3.6 %score.5 = (f32[10,288,768]{2,1,0:T(8,128)S(1)}, f32[288,96]{1,0:T(8,128)S(1)}, f32[8,512]{1,0:T(8,128)S(1)}, bf16[7680,512]{1,0:T(8,128)(2,1)S(1)}, bf16[7680,5...) custom-call(bf16[304,256]{1,0:T(8,128)(2,1)S(1)} %collective-permute, ...), custom_call_target="tpu_custom_call", output_to_operand_aliasing={{4}: (2, {}), {3}: (7, {}), {5}: (8, {}), {6}: (9, {}), {0}... | custom-call | flops 1 | bytes 1 | tf_op jit(solution)/shard_map/score/pallas_call | solution.py:354
  31.0 3.6 %score.6 = (f32[10,288,768]{2,1,0:T(8,128)S(1)}, f32[288,96]{1,0:T(8,128)S(1)}, f32[8,512]{1,0:T(8,128)S(1)}, bf16[7680,512]{1,0:T(8,128)(2,1)S(1)}, bf16[7680,5...) custom-call(bf16[304,256]{1,0:T(8,128)(2,1)S(1)} %collective-permute, ...), custom_call_target="tpu_custom_call", output_to_operand_aliasing={{5}: (2, {}), {3}: (7, {}), {4}: (8, {}), {6}: (9, {}), {0}... | custom-call | flops 1 | bytes 1 | tf_op jit(solution)/shard_map/score/pallas_call | solution.py:354
  34.6 3.9 %score.7 = (f32[10,288,768]{2,1,0:T(8,128)S(1)}, f32[288,96]{1,0:T(8,128)S(1)}, f32[11,8,768]{2,1,0:T(8,128)S(1)}, f32[8,128]{1,0:T(8,128)S(1)}, bf16[7680,512]{...) custom-call(bf16[304,256]{1,0:T(8,128)(2,1)S(1)} %collective-permute, ...), custom_call_target="tpu_custom_call", output_to_operand_aliasing={{7}: (2, {}), {4}: (7, {}), {5}: (8, {}), {6}: (9, {}), {0}... | custom-call | flops 1 | bytes 1 | tf_op jit(solution)/shard_map/score/pallas_call | solution.py:354
  38.5 1.6 %collective-permute-start.12 = (f32[8,128]{1,0:T(8,128)S(1)}, f32[8,128]{1,0:T(8,128)S(1)}, u32[]{:S(2)}, u32[]{:S(2)}) collective-permute-start(f32[8,128]{1,0:T(8,128)S(1)} %get-tuple-element.104.r_0_), channel_id=1, source_target_pairs={{0,3},{1,2},{2,1},{3,0},{4,7},{5,6},{6,5},{7,4},{8,11},{9,10},{10,... | collective-permute-start | bytes 12296 | tf_op jit(solution)/shard_map/ppermute | solution.py:330
  40.0 1.3 %collective-permute-start.11 = (f32[8,128]{1,0:T(8,128)S(1)}, f32[8,128]{1,0:T(8,128)S(1)}, u32[]{:S(2)}, u32[]{:S(2)}) collective-permute-start(f32[8,128]{1,0:T(8,128)S(1)} %get-tuple-element.104.r_0_), channel_id=1, source_target_pairs={{0,2},{1,3},{2,0},{3,1},{4,6},{5,7},{6,4},{7,5},{8,10},{9,11},{10,... | collective-permute-start | bytes 12296 | tf_op jit(solution)/shard_map/ppermute | solution.py:330
  42.0 1.0 %collective-permute-done.12.r_3_ = f32[8,128]{1,0:T(8,128)S(1)} collective-permute-done((f32[8,128]{1,0:T(8,128)S(1)}, f32[8,128]{1,0:T(8,128)S(1)}, u32[]{:S(2)}, u32[]{:S(2)}) %collective-permute-start.12) | collective-permute-done | bytes 4128 | tf_op jit(solution)/shard_map/ppermute | solution.py:330
  43.7 1.3 %collective-permute-done.10.r_1_ = f32[8,128]{1,0:T(8,128)S(1)} collective-permute-done((f32[8,128]{1,0:T(8,128)S(1)}, f32[8,128]{1,0:T(8,128)S(1)}, u32[]{:S(2)}, u32[]{:S(2)}) %collective-permute-start.10) | collective-permute-done | bytes 4128 | tf_op jit(solution)/shard_map/ppermute | solution.py:330
  45.0 3.9 %sums_first.1 = (bf16[10,288,768]{2,1,0:T(8,128)(2,1)S(1)}, bf16[288,96]{1,0:T(8,128)(2,1)S(1)}, f32[288,256]{1,0:T(8,128)S(1)}, bf16[304,256]{1,0:T(8,128)(2,1)...) custom-call(f32[8,128]{1,0:T(8,128)S(1)} %get-tuple-element.104.r_0_, ...), custom_call_target="tpu_custom_call", output_to_operand_aliasing={{5}: (9, {}), {6}: (10, {}), {7}: (11, {})} | custom-call | flops 1 | bytes 1 | tf_op jit(solution)/shard_map/sums_first/pallas_call | solution.py:354
  49.0 2.5 %sums.3 = (f32[288,256]{1,0:T(8,128)S(1)}, bf16[288,256]{1,0:T(8,128)(2,1)S(1)}, bf16[7680,512]{1,0:T(8,128)(2,1)S(1)}, bf16[7680,512]{1,0:T(8,128)(2,1)S(1)}) custom-call(bf16[10,288,768]{2,1,0:T(8,128)(2,1)S(1)} %get-tuple-element.113.r_0_, bf16[288,96]{1,0:T(8,128)(2,1)S(1)} %get-tuple-element.129.r_1_, ...), custom_call_target="tpu_custom_call", output_to_operand_aliasing={{2}: (4, {}), {3}: (5, {})} | custom-call | flops 1 | bytes 1 | tf_op jit(solution)/shard_map/sums/pallas_call | solution.py:354
  52.1 1.6 %collective-permute-start.15 = (bf16[304,256]{1,0:T(8,128)(2,1)S(1)}, bf16[304,256]{1,0:T(8,128)(2,1)S(1)}, u32[]{:S(2)}, u32[]{:S(2)}) collective-permute-start(bf16[304,256]{1,0:T(8,128)(2,1)S(1)} %get-tuple-element.122.first), channel_id=1, source_target_pairs={{0,24},{4,28},{8,16},{12,20},{16,8},{20,12},{24,0},{28,4},{1,25},{... | collective-permute-start | bytes 466952 | tf_op jit(solution)/shard_map/ppermute | solution.py:330
  53.7 2.5 %sums.4 = (f32[288,256]{1,0:T(8,128)S(1)}, bf16[288,256]{1,0:T(8,128)(2,1)S(1)}, bf16[7680,512]{1,0:T(8,128)(2,1)S(1)}) custom-call(bf16[10,288,768]{2,1,0:T(8,128)(2,1)S(1)} %get-tuple-element.113.r_0_, bf16[288,96]{1,0:T(8,128)(2,1)S(1)} %get-tuple-element.129.r_1_, ...), custom_call_target="tpu_custom_call", output_to_operand_aliasing={{2}: (4, {})} | custom-call | flops 1 | bytes 1 | tf_op jit(solution)/shard_map/sums/pallas_call | solution.py:354
  56.3 2.7 %collective-permute-start.16 = (bf16[304,256]{1,0:T(8,128)(2,1)S(1)}, bf16[304,256]{1,0:T(8,128)(2,1)S(1)}, u32[]{:S(2)}, u32[]{:S(2)}) collective-permute-start(bf16[304,256]{1,0:T(8,128)(2,1)S(1)} %pair.2), channel_id=1, source_target_pairs={{0,16},{4,20},{8,24},{12,28},{16,0},{20,4},{24,8},{28,12},{1,17},{... | collective-permute-start | bytes 466952 | tf_op jit(solution)/shard_map/ppermute | solution.py:330
  60.0 2.5 %sums.5 = (f32[288,256]{1,0:T(8,128)S(1)}, bf16[288,256]{1,0:T(8,128)(2,1)S(1)}) custom-call(bf16[10,288,768]{2,1,0:T(8,128)(2,1)S(1)} %get-tuple-element.113.r_0_, bf16[288,96]{1,0:T(8,128)(2,1)S(1)} %get-tuple-element.129.r_1_, bf16[7680,512]{1,0:T(8,128)(2,1)S(1)} %get-tuple-element.130.r_2_, bf16[96,2048]{1,0:T(8,128)(2,1)S(1)} %get-tuple-element.75.r_3_.r_8_), custom_call_target="tpu_custom_call" | custom-call | flops 1 | bytes 1 | tf_op jit(solution)/shard_map/sums/pallas_call | solution.py:354
  62.6 6.8 %collective-permute-done.16.r_1_ = bf16[304,256]{1,0:T(8,128)(2,1)S(1)} collective-permute-done((bf16[304,256]{1,0:T(8,128)(2,1)S(1)}, bf16[304,256]{1,0:T(8,128)(2,1)S(1)}, u32[]{:S(2)}, u32[]{:S(2)}) %collective-permute-start.16) | collective-permute-done | bytes 155680 | tf_op jit(solution)/shard_map/ppermute | solution.py:330
  69.4 1.0 %finish.1 = (f32[288,256]{1,0:T(8,128)}, f32[8,36]{1,0:T(8,128)}) custom-call(bf16[304,256]{1,0:T(8,128)(2,1)S(1)} %collective-permute-done.15.r_0_, bf16[304,256]{1,0:T(8,128)(2,1)S(1)} %collective-permute-done.16.r_1_, bf16[304,256]{1,0:T(8,128)(2,1)S(1)} %collective-permute-done.18.r_2_, f32[288,256]{1,0:T(8,128)S(1)} %get-tuple-element.131.r_3_, ...), custom_call_target="tpu_custom_call" | custom-call | flops 1 | bytes 1 | tf_op jit(solution)/shard_map/finish/pallas_call | solution.py:354
  (40 shorter events, 7.6 us)
Async XLA Ops:
  0.7 1.0 %copy-start.1 = (f32[8,36,256]{2,0,1:T(8,128)S(1)}, f32[8,36,256]{2,0,1:T(8,128)}, u32[]{:S(2)}) copy-start(f32[8,36,256]{2,0,1:T(8,128)} %param.5) | copy-start | bytes 884740
  1.7 0.7 copy-start.3
  3.1 18.4 %collective-permute-start.3 = (bf16[304,256]{1,0:T(8,128)(2,1)S(1)}, bf16[304,256]{1,0:T(8,128)(2,1)S(1)}, u32[]{:S(2)}, u32[]{:S(2)}) collective-permute-start(bf16[304,256]{1,0:T(8,128)(2,1)S(1)} %prepare.1.r_0_), channel_id=1, source_target_pairs={{0,8},{4,12},{8,0},{12,4},{16,24},{20,28},{24,16},{28,20},{1,9},{5... | collective-permute-start | bytes 466952 | tf_op jit(solution)/shard_map/ppermute | solution.py:330
  6.2 5.9 %collective-permute-start = (bf16[96,512]{1,0:T(8,128)(2,1)}, bf16[96,512]{1,0:T(8,128)(2,1)S(1)}, u32[]{:S(2)}, u32[]{:S(2)}) collective-permute-start(bf16[96,512]{1,0:T(8,128)(2,1)} %r_2_.1), channel_id=1, source_target_pairs={{0,1},{1,0},{2,3},{3,2},{4,5},{5,4},{6,7},{7,6},{8,9},{9,8},{10,11... | collective-permute-start | bytes 294920 | tf_op jit(solution)/shard_map/ppermute | solution.py:330
  7.7 7.1 %collective-permute-start.2 = (bf16[96,512]{1,0:T(8,128)(2,1)}, bf16[96,512]{1,0:T(8,128)(2,1)S(1)}, u32[]{:S(2)}, u32[]{:S(2)}) collective-permute-start(bf16[96,512]{1,0:T(8,128)(2,1)} %r_2_.1), channel_id=1, source_target_pairs={{0,3},{1,2},{2,1},{3,0},{4,7},{5,6},{6,5},{7,4},{8,11},{9,10},{10,... | collective-permute-start | bytes 294920 | tf_op jit(solution)/shard_map/ppermute | solution.py:330
  9.2 5.7 %collective-permute-start.1 = (bf16[96,512]{1,0:T(8,128)(2,1)}, bf16[96,512]{1,0:T(8,128)(2,1)S(1)}, u32[]{:S(2)}, u32[]{:S(2)}) collective-permute-start(bf16[96,512]{1,0:T(8,128)(2,1)} %r_2_.1), channel_id=1, source_target_pairs={{0,2},{1,3},{2,0},{3,1},{4,6},{5,7},{6,4},{7,5},{8,10},{9,11},{10,... | collective-permute-start | bytes 294920 | tf_op jit(solution)/shard_map/ppermute | solution.py:330
  9.7 14.5 %collective-permute-start.5 = (bf16[304,256]{1,0:T(8,128)(2,1)S(1)}, bf16[304,256]{1,0:T(8,128)(2,1)S(1)}, u32[]{:S(2)}, u32[]{:S(2)}) collective-permute-start(bf16[304,256]{1,0:T(8,128)(2,1)S(1)} %prepare.1.r_0_), channel_id=1, source_target_pairs={{0,4},{4,0},{8,12},{12,8},{16,20},{20,16},{24,28},{28,24},{1,5},{5... | collective-permute-start | bytes 466952 | tf_op jit(solution)/shard_map/ppermute | solution.py:330
  9.7 1.0 %copy-start = (f32[2,40,1024]{2,1,0:T(8,128)S(1)}, f32[2,40,1024]{2,1,0:T(8,128)}, u32[]{:S(2)}) copy-start(f32[2,40,1024]{2,1,0:T(8,128)} %constant.24.clone.r_1_) | copy-start | bytes 983044
  10.6 0.9 %copy-start.2 = (bf16[96,512]{1,0:T(8,128)(2,1)S(1)}, bf16[96,512]{1,0:T(8,128)(2,1)}, u32[]{:S(2)}) copy-start(bf16[96,512]{1,0:T(8,128)(2,1)} %r_2_.1) | copy-start | bytes 294916
  12.1 14.6 %collective-permute-start.6 = (bf16[304,256]{1,0:T(8,128)(2,1)S(1)}, bf16[304,256]{1,0:T(8,128)(2,1)S(1)}, u32[]{:S(2)}, u32[]{:S(2)}) collective-permute-start(bf16[304,256]{1,0:T(8,128)(2,1)S(1)} %prepare.1.r_0_), channel_id=1, source_target_pairs={{0,16},{4,20},{8,24},{12,28},{16,0},{20,4},{24,8},{28,12},{1,17},{... | collective-permute-start | bytes 466952 | tf_op jit(solution)/shard_map/ppermute | solution.py:330
  21.6 5.4 %collective-permute-start.4 = (bf16[304,256]{1,0:T(8,128)(2,1)S(1)}, bf16[304,256]{1,0:T(8,128)(2,1)S(1)}, u32[]{:S(2)}, u32[]{:S(2)}) collective-permute-start(bf16[304,256]{1,0:T(8,128)(2,1)S(1)} %collective-permute-done.3.r_0_), channel_id=1, source_target_pairs={{0,4},{4,0},{8,12},{12,8},{16,20},{20,16},{24,28},{28,24},{1,5},{5... | collective-permute-start | bytes 466952 | tf_op jit(solution)/shard_map/ppermute | solution.py:330
  21.7 8.8 %collective-permute-start.7 = (bf16[304,256]{1,0:T(8,128)(2,1)S(1)}, bf16[304,256]{1,0:T(8,128)(2,1)S(1)}, u32[]{:S(2)}, u32[]{:S(2)}) collective-permute-start(bf16[304,256]{1,0:T(8,128)(2,1)S(1)} %prepare.1.r_0_), channel_id=1, source_target_pairs={{0,24},{4,28},{8,16},{12,20},{16,8},{20,12},{24,0},{28,4},{1,25},{... | collective-permute-start | bytes 466952 | tf_op jit(solution)/shard_map/ppermute | solution.py:330
  26.7 4.3 %collective-permute-start.9 = (bf16[304,256]{1,0:T(8,128)(2,1)S(1)}, bf16[304,256]{1,0:T(8,128)(2,1)S(1)}, u32[]{:S(2)}, u32[]{:S(2)}) collective-permute-start(bf16[304,256]{1,0:T(8,128)(2,1)S(1)} %collective-permute-done.6.r_0_), channel_id=1, source_target_pairs={{0,4},{4,0},{8,12},{12,8},{16,20},{20,16},{24,28},{28,24},{1,5},{5... | collective-permute-start | bytes 466952 | tf_op jit(solution)/shard_map/ppermute | solution.py:330
  30.6 4.0 %collective-permute-start.8 = (bf16[304,256]{1,0:T(8,128)(2,1)S(1)}, bf16[304,256]{1,0:T(8,128)(2,1)S(1)}, u32[]{:S(2)}, u32[]{:S(2)}) collective-permute-start(bf16[304,256]{1,0:T(8,128)(2,1)S(1)} %collective-permute-done.7.r_0_), channel_id=1, source_target_pairs={{0,4},{4,0},{8,12},{12,8},{16,20},{20,16},{24,28},{28,24},{1,5},{5... | collective-permute-start | bytes 466952 | tf_op jit(solution)/shard_map/ppermute | solution.py:330
  38.5 4.6 %collective-permute-start.12 = (f32[8,128]{1,0:T(8,128)S(1)}, f32[8,128]{1,0:T(8,128)S(1)}, u32[]{:S(2)}, u32[]{:S(2)}) collective-permute-start(f32[8,128]{1,0:T(8,128)S(1)} %get-tuple-element.104.r_0_), channel_id=1, source_target_pairs={{0,3},{1,2},{2,1},{3,0},{4,7},{5,6},{6,5},{7,4},{8,11},{9,10},{10,... | collective-permute-start | bytes 12296 | tf_op jit(solution)/shard_map/ppermute | solution.py:330
  40.0 3.6 %collective-permute-start.11 = (f32[8,128]{1,0:T(8,128)S(1)}, f32[8,128]{1,0:T(8,128)S(1)}, u32[]{:S(2)}, u32[]{:S(2)}) collective-permute-start(f32[8,128]{1,0:T(8,128)S(1)} %get-tuple-element.104.r_0_), channel_id=1, source_target_pairs={{0,2},{1,3},{2,0},{3,1},{4,6},{5,7},{6,4},{7,5},{8,10},{9,11},{10,... | collective-permute-start | bytes 12296 | tf_op jit(solution)/shard_map/ppermute | solution.py:330
  41.4 3.6 %collective-permute-start.10 = (f32[8,128]{1,0:T(8,128)S(1)}, f32[8,128]{1,0:T(8,128)S(1)}, u32[]{:S(2)}, u32[]{:S(2)}) collective-permute-start(f32[8,128]{1,0:T(8,128)S(1)} %get-tuple-element.104.r_0_), channel_id=1, source_target_pairs={{0,1},{1,0},{2,3},{3,2},{4,5},{5,4},{6,7},{7,6},{8,9},{9,8},{10,11... | collective-permute-start | bytes 12296 | tf_op jit(solution)/shard_map/ppermute | solution.py:330
  48.9 3.1 %collective-permute-start.14 = (bf16[304,256]{1,0:T(8,128)(2,1)S(1)}, bf16[304,256]{1,0:T(8,128)(2,1)S(1)}, u32[]{:S(2)}, u32[]{:S(2)}) collective-permute-start(bf16[304,256]{1,0:T(8,128)(2,1)S(1)} %get-tuple-element.120), channel_id=1, source_target_pairs={{0,4},{4,0},{8,12},{12,8},{16,20},{20,16},{24,28},{28,24},{1,5},{5... | collective-permute-start | bytes 466952 | tf_op jit(solution)/shard_map/ppermute | solution.py:330
  51.5 2.2 %collective-permute-start.13 = (bf16[288,256]{1,0:T(8,128)(2,1)S(1)}, bf16[288,256]{1,0:T(8,128)(2,1)S(1)}, u32[]{:S(2)}, u32[]{:S(2)}) collective-permute-start(bf16[288,256]{1,0:T(8,128)(2,1)S(1)} %get-tuple-element.118), channel_id=1, source_target_pairs={{0,4},{4,0},{8,12},{12,8},{16,20},{20,16},{24,28},{28,24},{1,5},{5... | collective-permute-start | bytes 442376 | tf_op jit(solution)/shard_map/ppermute | solution.py:330
  52.1 7.9 %collective-permute-start.15 = (bf16[304,256]{1,0:T(8,128)(2,1)S(1)}, bf16[304,256]{1,0:T(8,128)(2,1)S(1)}, u32[]{:S(2)}, u32[]{:S(2)}) collective-permute-start(bf16[304,256]{1,0:T(8,128)(2,1)S(1)} %get-tuple-element.122.first), channel_id=1, source_target_pairs={{0,24},{4,28},{8,16},{12,20},{16,8},{20,12},{24,0},{28,4},{1,25},{... | collective-permute-start | bytes 466952 | tf_op jit(solution)/shard_map/ppermute | solution.py:330
  56.2 2.8 %collective-permute-start.17 = (bf16[288,256]{1,0:T(8,128)(2,1)S(1)}, bf16[288,256]{1,0:T(8,128)(2,1)S(1)}, u32[]{:S(2)}, u32[]{:S(2)}) collective-permute-start(bf16[288,256]{1,0:T(8,128)(2,1)S(1)} %get-tuple-element.128), channel_id=1, source_target_pairs={{0,4},{4,0},{8,12},{12,8},{16,20},{20,16},{24,28},{28,24},{1,5},{5... | collective-permute-start | bytes 442376 | tf_op jit(solution)/shard_map/ppermute | solution.py:330
  56.3 13.1 %collective-permute-start.16 = (bf16[304,256]{1,0:T(8,128)(2,1)S(1)}, bf16[304,256]{1,0:T(8,128)(2,1)S(1)}, u32[]{:S(2)}, u32[]{:S(2)}) collective-permute-start(bf16[304,256]{1,0:T(8,128)(2,1)S(1)} %pair.2), channel_id=1, source_target_pairs={{0,16},{4,20},{8,24},{12,28},{16,0},{20,4},{24,8},{28,12},{1,17},{... | collective-permute-start | bytes 466952 | tf_op jit(solution)/shard_map/ppermute | solution.py:330
  59.1 10.3 %collective-permute-start.18 = (bf16[304,256]{1,0:T(8,128)(2,1)S(1)}, bf16[304,256]{1,0:T(8,128)(2,1)S(1)}, u32[]{:S(2)}, u32[]{:S(2)}) collective-permute-start(bf16[304,256]{1,0:T(8,128)(2,1)S(1)} %pair.3), channel_id=1, source_target_pairs={{0,8},{4,12},{8,0},{12,4},{16,24},{20,28},{24,16},{28,20},{1,9},{5... | collective-permute-start | bytes 466952 | tf_op jit(solution)/shard_map/ppermute | solution.py:330
  62.5 6.9 %collective-permute-start.19 = (bf16[288,256]{1,0:T(8,128)(2,1)S(1)}, bf16[288,256]{1,0:T(8,128)(2,1)S(1)}, u32[]{:S(2)}, u32[]{:S(2)}) collective-permute-start(bf16[288,256]{1,0:T(8,128)(2,1)S(1)} %get-tuple-element.132), channel_id=1, source_target_pairs={{0,4},{4,0},{8,12},{12,8},{16,20},{20,16},{24,28},{28,24},{1,5},{5... | collective-permute-start | bytes 442376 | tf_op jit(solution)/shard_map/ppermute | solution.py:330

commit v4 on v3

--- a/solution.py
+++ b/solution.py
@@ -72,25 +72,33 @@
     return jnp.concatenate(pieces, axis=1) if per > 1 else pieces[0]
 
 
-def prepare_body(where, refs, noise, message, tall, tail):
-    h, width = refs.shape
-    at = pl.multiple_of(jnp.bitwise_and(where[0], HALF // width - 1) * width, 128)
-    x = refs[...]
+def begin_body(where, *refs, width):
+    sources = refs[:4]
+    message, cosine, sine, kept, x_ref, noise, tables, tall, tail, arrived = refs[4:]
+    copies = [
+        pltpu.make_async_copy(source, target, arrived.at[n])
+        for n, (source, target) in enumerate(zip(sources, (x_ref, noise, tables, kept)))
+    ]
+    for copy in copies:
+        copy.start()
+    count = HALF // width
+    at = pl.multiple_of(jnp.bitwise_and(where[0], count - 1) * width, 128)
+    h = x_ref.shape[0]
+    copies[0].wait()
+    copies[1].wait()
+    x = x_ref[...]
     w = noise[:, pl.ds(at, width)]
     message[0:h, :] = (x * w).astype(BF16)
     half = 0.5 * jnp.sum(x * x * w, axis=1, keepdims=True)
     row = column_to_row(half, tall.shape[0], tall)
     message[h : h + TAIL, :] = tail_block(row, width, tail)
-
-
-def table_body(where, tables, particles, cosine, sine, kept, *, width):
-    kept[...] = particles[...]
-    count = HALF // width
+    copies[2].wait()
     sign = jnp.where(where[0] < count, 1.0, -1.0).astype(F32)
     for k in range(count):
         at = pl.multiple_of(jnp.bitwise_and(jnp.bitwise_xor(where[0], k), count - 1) * width, 128)
         cosine[:, k * width : (k + 1) * width] = tables[0, :, pl.ds(at, width)]
         sine[:, k * width : (k + 1) * width] = tables[1, :, pl.ds(at, width)] * sign
+    copies[3].wait()
 
 
 def shift_body(where, *refs, parts, pairs, width):
@@ -129,44 +137,49 @@
     lax.fori_loop(0, MAIN // 2, one, 0)
 
 
-def stage_body(*refs, first, others, length, rest_at):
-    mine, sibling, moved, moved_rest = refs[:4]
-    count = 4 if first else 7
-    partial = None if first else refs[4:7]
-    scores, scores_rest, norms = refs[count + others : count + others + 3]
+def load_slabs(slabs, weighted, row, length):
+    h = weighted.shape[0]
+    width = slabs[0].shape[1]
+    for k, slab in enumerate(slabs):
+        weighted[:, k * width : (k + 1) * width] = slab[0:h, :]
+        row += row_of_tail(slab[h : h + TAIL, :].astype(F32), width, length)
+    return row
+
+
+def stage_body(*refs, first, count, others, length, rest_at):
+    slabs, moved, moved_rest = refs[: 2 * count], refs[2 * count : 3 * count], refs[3 * count]
+    at = 3 * count + 1
+    partial = None if first else refs[at : at + 3]
+    at += (0 if first else 3) + others
+    scores, scores_rest, norms = refs[at : at + 3]
     weighted = refs[-1]
-    h, span = weighted.shape
-    width = span // 2
+    span = weighted.shape[1]
     block = scores.shape[2]
     row = jnp.zeros((1, length), F32) if first else partial[2][0:1, :]
-    for k, piece in enumerate((mine, sibling)):
-        weighted[:, k * width : (k + 1) * width] = piece[0:h, :]
-        row += row_of_tail(piece[h : h + TAIL, :].astype(F32), width, length)
-    norms[...] = jnp.broadcast_to(row, norms.shape)
+    norms[...] = jnp.broadcast_to(load_slabs(slabs, weighted, row, length), norms.shape)
     last = contract(weighted[...], moved_rest[:, rest_at : rest_at + span], ((1,), (1,)))
     scores_rest[...] = last if first else partial[1][...] + last
     for i in range(STEPS):
-        x = contract(weighted[...], moved[i * block : (i + 1) * block, :], ((1,), (1,)))
+        x = jnp.concatenate([m[i * block : (i + 1) * block, :] for m in moved], axis=1)
+        x = contract(weighted[...], x, ((1,), (1,)))
         scores[i] = x if first else partial[0][i] + x
 
 
-def last_stage_body(*refs, others, length, rest_at):
-    mine, sibling, moved, moved_rest, scores, scores_rest, norms = refs[:7]
-    weights, weights_rest, tops, stats = refs[7 + others : 11 + others]
+def last_stage_body(*refs, count, others, length, rest_at):
+    slabs, moved, moved_rest = refs[: 2 * count], refs[2 * count : 3 * count], refs[3 * count]
+    scores, scores_rest, norms = refs[3 * count + 1 : 3 * count + 4]
+    at = 3 * count + 4 + others
+    weights, weights_rest, tops, stats = refs[at : at + 4]
     weighted, half, even, odd, totals = refs[-5:]
     h, block = even.shape
     rows = moved_rest.shape[0]
     span = weighted.shape[1]
-    width = span // 2
-    row = norms[0:1, :]
-    for k, piece in enumerate((mine, sibling)):
-        weighted[:, k * width : (k + 1) * width] = piece[0:h, :]
-        row += row_of_tail(piece[h : h + TAIL, :].astype(F32), width, length)
+    row = load_slabs(slabs, weighted, norms[0:1, :], length)
     half[...] = jnp.broadcast_to(row, (128, length)).T[0:h, :]
 
     def multiply(i, target):
-        x = contract(weighted[...], moved[i * block : (i + 1) * block, :], ((1,), (1,)))
-        target[...] = scores[i] + x
+        x = jnp.concatenate([m[i * block : (i + 1) * block, :] for m in moved], axis=1)
+        target[...] = scores[i] + contract(weighted[...], x, ((1,), (1,)))
 
     def soften(i, source):
         for q in range(0, block, 128):
@@ -285,10 +298,18 @@
     message[h : h + TAIL, :] = tail_block(row, width, tail)
 
 
-def pair_body(own, received, first, message):
-    h = own.shape[0]
-    message[0:h, :] = (own[...] + received[...].astype(F32)).astype(BF16)
-    message[h : h + TAIL, :] = first[h : h + TAIL, :]
+def pair_body(own, received, chip_row, *refs):
+    arrived = refs[:-2]
+    message, tail = refs[-2:]
+    h, width = own.shape
+    length = chip_row.shape[1]
+    x = own[...] + received[...].astype(F32)
+    row = chip_row[0:1, :]
+    for m in arrived:
+        x += m[0:h, :].astype(F32)
+        row += row_of_tail(m[h : h + TAIL, :].astype(F32), width, length)
+    message[0:h, :] = x.astype(BF16)
+    message[h : h + TAIL, :] = tail_block(row, width, tail)
 
 
 def finish_body(*refs, count):
@@ -339,10 +360,10 @@
         place = lax.axis_index("dom")
         where = jnp.stack([place, place % 2, lax.axis_index("cls")]).astype(jnp.int32)
 
-        def call(body, shapes, name, scratch=(), limit=2, aliases=None):
+        def call(body, shapes, name, scratch=(), limit=2, aliases=None, inputs=VMEM, flops=1):
             def run(*args):
                 scalars = args[0] is where
-                specs = [VMEM] * (len(args) - scalars)
+                specs = [inputs] * (len(args) - scalars)
                 spec = pltpu.PrefetchScalarGridSpec(
                     num_scalar_prefetch=int(scalars),
                     grid=(),
@@ -357,7 +378,7 @@
                     out_shape=shapes,
                     compiler_params=params,
                     input_output_aliases=aliases or {},
-                    cost_estimate=pl.CostEstimate(flops=1, transcendentals=0, bytes_accessed=1),
+                    cost_estimate=pl.CostEstimate(flops=flops, transcendentals=0, bytes_accessed=1),
                     name=name,
                 )(*args)
 
@@ -365,47 +386,60 @@
 
         pieces = [particles] + [swap(particles, "cls", cls, k) for k in range(1, cls)]
 
+        tables = phase_tables()
         ref_rows = references.transpose(1, 0, 2).reshape(h, width)
-        (message,) = call(
-            prepare_body,
-            [shape((h + TAIL, width), BF16)],
-            "prepare",
-            [pltpu.VMEM((length, 128), F32), pltpu.VMEM((TAIL, width), F32)],
-        )(where, ref_rows, noise_weight.reshape(1, HALF))
+        message, *angles, pieces[0] = call(
+            lambda *r: begin_body(*r, width=width),
+            [shape((h + TAIL, width), BF16)]
+            + [shape(tables.shape[1:], F32)] * 2
+            + [shape(particles.shape, BF16)],
+            "begin",
+            [
+                pltpu.VMEM((h, width), F32),
+                pltpu.VMEM((1, HALF), F32),
+                pltpu.VMEM(tables.shape, F32),
+                pltpu.VMEM((length, 128), F32),
+                pltpu.VMEM((TAIL, width), F32),
+                pltpu.SemaphoreType.DMA((4,)),
+            ],
+            inputs=pl.BlockSpec(memory_space=pltpu.HBM),
+        )(
+            where,
+            *[
+                pltpu.with_memory_space_constraint(x, pltpu.HBM)
+                for x in (ref_rows, noise_weight.reshape(1, HALF), jnp.asarray(tables), particles)
+            ],
+        )
 
         even = [message] + [swap(message, "dom", dom, 2 * k) for k in range(1, pairs)]
         odd = [swap(message, "dom", dom, 1)]
-
-        tables = phase_tables()
-        *angles, pieces[0] = call(
-            lambda *r: table_body(*r, width=width),
-            [shape(tables.shape[1:], F32)] * 2 + [shape(particles.shape, BF16)],
-            "tables",
-        )(where, tables, particles)
 
         *moved, moved_rest = call(
             lambda *r: shift_body(*r, parts=cls, pairs=pairs, width=width),
             [pltpu.VMEM((MAIN * rows, 2 * width), BF16)] * pairs + [shape((rows, F), BF16)],
             "shift",
-            limit=4,
+            flops=10**10,
+            limit=2,
             scratch=[pltpu.VMEM((rows, F), F32)] * 2,
         )(where, *pieces, *angles)
 
         held = pltpu.VMEM((MAIN * rows, 2 * width), BF16)
         partial = []
-        for j in range(pairs):
-            last = j == pairs - 1
-            rest = [k for k in range(pairs) if k != j]
+        stages = [[0]] + [list(range(1 << t, 2 << t)) for t in range((pairs - 1).bit_length())]
+        for n, stage in enumerate(stages):
+            last = stage[-1] == pairs - 1
+            count = len(stage)
+            rest = [k for k in range(pairs) if k not in stage]
             first_held = 4 if last else 3
-            first_other = 4 + len(partial)
-            aliases = {2: first_held + j}
-            aliases |= {first_other + n: first_held + k for n, k in enumerate(rest)}
+            after = 3 * count + 1 + len(partial)
+            aliases = {2 * count + m: first_held + k for m, k in enumerate(stage)}
+            aliases |= {after + m: first_held + k for m, k in enumerate(rest)}
             if partial:
-                aliases |= {4: 0, 5: 1}
+                aliases |= {3 * count + 1: 0, 3 * count + 2: 1}
             body = last_stage_body if last else stage_body
             options = {} if last else {"first": not partial}
             outs = [pltpu.VMEM((STEPS, h, block), F32), shape((h, rows), F32)]
-            scratch = [pltpu.VMEM((h, 2 * width), BF16)]
+            scratch = [pltpu.VMEM((h, 2 * width * count), BF16)]
             if last:
                 outs += [shape((STEPS + 1, 8, block), F32), shape((8, 128), F32)]
                 scratch += [
@@ -416,30 +450,46 @@
                 ]
             else:
                 outs += [shape((8, length), F32)]
-            if not last:
-                if partial:
-                    partial[2], even[j + 1] = lax.optimization_barrier((partial[2], even[j + 1]))
-                else:
-                    moved_rest, even[j + 1] = lax.optimization_barrier((moved_rest, even[j + 1]))
-                odd.append(swap(even[j + 1], "dom", dom, 1))
+                for k in stages[n + 1]:
+                    if partial:
+                        partial[2], even[k] = lax.optimization_barrier((partial[2], even[k]))
+                    else:
+                        moved_rest, even[k] = lax.optimization_barrier((moved_rest, even[k]))
+                    odd.append(swap(even[k], "dom", dom, 1))
             results = call(
                 lambda *r: body(
-                    *r, others=pairs - 1, length=length, rest_at=2 * j * width, **options
+                    *r,
+                    count=count,
+                    others=len(rest),
+                    length=length,
+                    rest_at=2 * stage[0] * width,
+                    **options,
                 ),
                 outs + [held] * pairs,
                 "score",
                 scratch,
-                limit=7 if last else 4,
+                limit=6 if last else 6,
                 aliases=aliases,
-            )(even[j], odd[j], moved[j], moved_rest, *partial, *[moved[k] for k in rest])
+            )(
+                *[m for k in stage for m in (even[k], odd[k])],
+                *[moved[k] for k in stage],
+                moved_rest,
+                *partial,
+                *[moved[k] for k in rest],
+            )
             partial, moved = list(results[:first_held]), results[first_held:]
         weights, weights_rest, tops, stats = partial
 
         gathered = [stats] + [swap(stats, "cls", cls, k) for k in range(1, cls)]
 
         accumulator = pltpu.VMEM((h, 2 * width), F32)
-        order = list(range(pairs - 1, -1, -1))
-        messages = []
+        order = sorted(range(1, pairs), key=lambda k: (k & -k, -k)) + [0]
+        sent = {}
+
+        def children(k):
+            low = k & -k or pairs
+            return [sent[k | 1 << t] for t in range(low.bit_length() - 1)]
+
         probs, probs_rest, own, other, weight_row, *kept = call(
             lambda *r: first_sums_body(
                 *r, groups=cls, others=pairs - 1, length=length, rest_at=order[0] * 2 * width
@@ -451,10 +501,10 @@
                 shape((h + TAIL, width), BF16),
                 shape((8, length), F32),
             ]
-            + [pltpu.VMEM((MAIN * rows, 2 * width), BF16)] * (pairs - 1),
+            + [held] * (pairs - 1),
             "sums_first",
             aliases={cls + 5 + k: 5 + k for k in range(pairs - 1)},
-            limit=4,
+            limit=2,
             scratch=[
                 accumulator,
                 pltpu.VMEM((8, block), F32),
@@ -464,7 +514,15 @@
                 pltpu.VMEM((length, 128), F32),
                 pltpu.VMEM((TAIL, width), F32),
             ],
-        )(*gathered, weights, weights_rest, tops, moved[order[0]], moved_rest, *moved[:-1])
+        )(
+            *gathered,
+            weights,
+            weights_rest,
+            tops,
+            moved[order[0]],
+            moved_rest,
+            *[moved[k] for k in order[1:]],
+        )
         received = swap(other, "dom", dom, 1)
         first, chip_row = call(
             first_pair_body,
@@ -472,35 +530,36 @@
             "pair_first",
             [pltpu.VMEM((TAIL, width), F32)],
         )(own, received, weight_row)
-        messages.append(swap(first, "dom", dom, 2 * order[0]))
+        sent[order[0]] = swap(first, "dom", dom, 2 * (order[0] & -order[0]))
         ready = first
 
         for n, k in enumerate(order[1:]):
-            if not k:
-                probs_rest, messages[0] = lax.optimization_barrier((probs_rest, messages[0]))
-            elif n:
+            if n:
                 probs_rest, ready = lax.optimization_barrier((probs_rest, ready))
+            others = pairs - 2 - n
             own, other, *kept = call(
-                lambda *r: sums_body(*r, others=k, rest_at=k * 2 * width),
-                [shape((h, width), F32), shape((h, width), BF16)]
-                + [pltpu.VMEM((MAIN * rows, 2 * width), BF16)] * k,
+                lambda *r: sums_body(*r, others=others, rest_at=k * 2 * width),
+                [shape((h, width), F32), shape((h, width), BF16)] + [held] * others,
                 "sums",
                 [accumulator],
-                aliases={4 + j: 2 + j for j in range(k)},
-            )(probs, probs_rest, kept[k], moved_rest, *kept[:k])
+                aliases={4 + j: 2 + j for j in range(others)},
+            )(probs, probs_rest, kept[0], moved_rest, *kept[1:])
             received = swap(other, "dom", dom, 1)
             if k:
-                (summed,) = call(pair_body, [shape((h + TAIL, width), BF16)], "pair")(
-                    own, received, first
-                )
-                messages.append(swap(summed, "dom", dom, 2 * k))
-                ready = summed
-
+                (ready,) = call(
+                    pair_body,
+                    [shape((h + TAIL, width), BF16)],
+                    "pair",
+                    [pltpu.VMEM((TAIL, width), F32)],
+                )(own, received, chip_row, *children(k))
+                sent[k] = swap(ready, "dom", dom, 2 * (k & -k))
+
+        arrived = children(0)
         sums, class_weight = call(
-            lambda *r: finish_body(*r, count=len(messages)),
+            lambda *r: finish_body(*r, count=len(arrived)),
             [shape((h, width), F32), shape((classes, rotations), F32)],
             "finish",
-        )(*messages, own, received, chip_row)
+        )(*arrived, own, received, chip_row)
         return sums.reshape(rotations, classes, width).transpose(1, 0, 2), class_weight
 
     return on_device

time: 70.7 us -> 65.4 us (0.925)
  local copies, waits for them, and re-layouts: 3.51 us -> 0 us
  starting transfers between devices: 21.9 us -> 18.5 us
  waiting for transfers between devices: 10.1 us -> 12.5 us
    unnamed x8 -> x0, local copies, waits for them, and re-layouts: 3.51 us -> none
    ppermute x20, starting transfers between devices: 21.9 us -> 18.5 us  [swap(): return lax.ppermute(x, axis, [(i, i ^ k) for i in range(size)])]
    ppermute x20, waiting for transfers between devices: 10.1 us -> 12.5 us  [swap(): return lax.ppermute(x, axis, [(i, i ^ k) for i in range(size)])]
    pallas_call x15 -> x13, Pallas kernels: 34.1 us -> 33.4 us  [run(): pl.pallas_call(body, grid_spec=spec, out_shape=shapes, compiler_params=pa...]
  transfers between devices with their start and end apart: 20 -> 20, of which waited for: 6 -> 9; matrix products, arithmetic and copies ran while one was open for 0% -> 0% of each run, Pallas kernels for 35% -> 34%
where the time goes in v4:
time: 65.4 us; the launch traced here: 65.3 us
  Pallas kernels  33.4 us (51%)
  starting transfers between devices  18.5 us (28%)
  waiting for transfers between devices  12.5 us (19%)
  between operations  0.76 us (1%)
    pallas_call x13, Pallas kernels, run(): pl.pallas_call(body, grid_spec=spec, out_shape=shapes, compiler_params=pa...  33.4 us
    ppermute x20, starting transfers between devices, swap(): return lax.ppermute(x, axis, [(i, i ^ k) for i in range(size)])  18.5 us
    ppermute x20, waiting for transfers between devices, swap(): return lax.ppermute(x, axis, [(i, i ^ k) for i in range(size)])  12.5 us
  transfers between devices with their start and end apart: 20, of which 9 were waited for; matrix products, arithmetic and copies ran while one was open for 0% of the time, Pallas kernels for 34%

profile of v4, /device:TPU:0, one launch (start us, length us, event | category | flops | bytes accessed | tf_op | source)
XLA Modules:
  0.0 65.3 jit_solution(13924708917077369602)
XLA Ops:
  0.6 3.0 %collective-permute-start.1 = (bf16[96,512]{1,0:T(8,128)(2,1)}, bf16[96,512]{1,0:T(8,128)(2,1)S(1)}, u32[]{:S(2)}, u32[]{:S(2)}) collective-permute-start(bf16[96,512]{1,0:T(8,128)(2,1)} %r_4_.1), channel_id=1, source_target_pairs={{0,1},{1,0},{2,3},{3,2},{4,5},{5,4},{6,7},{7,6},{8,9},{9,8},{10,11... | collective-permute-start | bytes 294920 | tf_op jit(solution)/shard_map/ppermute | solution.py:351
  3.6 1.5 %collective-permute-start.3 = (bf16[96,512]{1,0:T(8,128)(2,1)}, bf16[96,512]{1,0:T(8,128)(2,1)S(1)}, u32[]{:S(2)}, u32[]{:S(2)}) collective-permute-start(bf16[96,512]{1,0:T(8,128)(2,1)} %r_4_.1), channel_id=1, source_target_pairs={{0,3},{1,2},{2,1},{3,0},{4,7},{5,6},{6,5},{7,4},{8,11},{9,10},{10,... | collective-permute-start | bytes 294920 | tf_op jit(solution)/shard_map/ppermute | solution.py:351
  5.3 1.8 %begin.1 = (bf16[304,256]{1,0:T(8,128)(2,1)S(1)}, f32[40,1024]{1,0:T(8,128)S(1)}, f32[40,1024]{1,0:T(8,128)S(1)}, bf16[96,512]{1,0:T(8,128)(2,1)S(1)}) custom-call(s32[3]{0:T(128)S(1)} %pad_add_fusion.r_0_, f32[288,256]{1,0:T(8,128)} %bitcast.10, f32[1,1024]{1,0:T(1,128)} %bitcast.11, f32[2,40,1024]{2,1,0:T(8,128)} %constant.24.clone.r_3_, bf16[96,512]{1,0:T(8,128)(2,1)} %r_4_.1), custom_call_target="tpu_custom_call" | custom-call | flops 1 | bytes 1 | tf_op jit(solution)/shard_map/begin/pallas_call | solution.py:375
  7.0 4.1 %collective-permute-start.7 = (bf16[304,256]{1,0:T(8,128)(2,1)S(1)}, bf16[304,256]{1,0:T(8,128)(2,1)S(1)}, u32[]{:S(2)}, u32[]{:S(2)}) collective-permute-start(bf16[304,256]{1,0:T(8,128)(2,1)S(1)} %get-tuple-element.62.r_0_), channel_id=1, source_target_pairs={{0,24},{4,28},{8,16},{12,20},{16,8},{20,12},{24,0},{28,4},{1,25},{... | collective-permute-start | bytes 466952 | tf_op jit(solution)/shard_map/ppermute | solution.py:351
  11.2 0.6 collective-permute-start.4
  11.8 6.6 %shift.1 = (bf16[7680,512]{1,0:T(8,128)(2,1)S(1)}, bf16[7680,512]{1,0:T(8,128)(2,1)S(1)}, bf16[7680,512]{1,0:T(8,128)(2,1)S(1)}, bf16[7680,512]{1,0:T(8,128)(2,1)S(1)}, bf16[96,2048]{1,0:T(8,128)(2,1)S(1)}) custom-call(s32[3]{0:T(128)S(1)} %pad_add_fusion.r_0_, bf16[96,512]{1,0:T(8,128)(2,1)S(1)} %get-tuple-element.63.r_1_, ...), custom_call_target="tpu_custom_call" | custom-call | flops 10000000000 | bytes 1 | tf_op jit(solution)/shard_map/shift/pallas_call | solution.py:375
  18.5 1.8 %collective-permute-done.4.r_0_ = bf16[304,256]{1,0:T(8,128)(2,1)S(1)} collective-permute-done((bf16[304,256]{1,0:T(8,128)(2,1)S(1)}, bf16[304,256]{1,0:T(8,128)(2,1)S(1)}, u32[]{:S(2)}, u32[]{:S(2)}) %collective-permute-start.4) | collective-permute-done | bytes 155680 | tf_op jit(solution)/shard_map/ppermute | solution.py:351
  20.3 2.5 %score.3 = (f32[10,288,768]{2,1,0:T(8,128)S(1)}, f32[288,96]{1,0:T(8,128)S(1)}, f32[8,512]{1,0:T(8,128)S(1)}, bf16[7680,512]{1,0:T(8,128)(2,1)S(1)}, bf16[7680,5...) custom-call(bf16[304,256]{1,0:T(8,128)(2,1)S(1)} %get-tuple-element., ...), custom_call_target="tpu_custom_call", output_to_operand_aliasing={{3}: (2, {}), {4}: (4, {}), {5}: (5, {}), {6}: (6, {})} | custom-call | flops 1 | bytes 1 | tf_op jit(solution)/shard_map/score/pallas_call | solution.py:375
  22.8 0.6 collective-permute-done.5.r_0_
  24.0 3.6 %score.4 = (f32[10,288,768]{2,1,0:T(8,128)S(1)}, f32[288,96]{1,0:T(8,128)S(1)}, f32[8,512]{1,0:T(8,128)S(1)}, bf16[7680,512]{1,0:T(8,128)(2,1)S(1)}, bf16[7680,5...) custom-call(bf16[304,256]{1,0:T(8,128)(2,1)S(1)} %collective-permute, ...), custom_call_target="tpu_custom_call", output_to_operand_aliasing={{4}: (2, {}), {3}: (7, {}), {5}: (8, {}), {6}: (9, {}), {0}... | custom-call | flops 1 | bytes 1 | tf_op jit(solution)/shard_map/score/pallas_call | solution.py:375
  27.6 6.0 %score.5 = (f32[10,288,768]{2,1,0:T(8,128)S(1)}, f32[288,96]{1,0:T(8,128)S(1)}, f32[11,8,768]{2,1,0:T(8,128)S(1)}, f32[8,128]{1,0:T(8,128)S(1)}, bf16[7680,512]{...) custom-call(bf16[304,256]{1,0:T(8,128)(2,1)S(1)} %collective-permute, ...), custom_call_target="tpu_custom_call", output_to_operand_aliasing={{6}: (4, {}), {7}: (5, {}), {4}: (10, {}), {5}: (11, {}), {... | custom-call | flops 1 | bytes 1 | tf_op jit(solution)/shard_map/score/pallas_call | solution.py:375
  33.7 2.5 %collective-permute-start.12 = (f32[8,128]{1,0:T(8,128)S(1)}, f32[8,128]{1,0:T(8,128)S(1)}, u32[]{:S(2)}, u32[]{:S(2)}) collective-permute-start(f32[8,128]{1,0:T(8,128)S(1)} %get-tuple-element.91.r_0_), channel_id=1, source_target_pairs={{0,3},{1,2},{2,1},{3,0},{4,7},{5,6},{6,5},{7,4},{8,11},{9,10},{10,... | collective-permute-start | bytes 12296 | tf_op jit(solution)/shard_map/ppermute | solution.py:351
  37.2 1.0 %collective-permute-done.12.r_3_ = f32[8,128]{1,0:T(8,128)S(1)} collective-permute-done((f32[8,128]{1,0:T(8,128)S(1)}, f32[8,128]{1,0:T(8,128)S(1)}, u32[]{:S(2)}, u32[]{:S(2)}) %collective-permute-start.12) | collective-permute-done | bytes 4128 | tf_op jit(solution)/shard_map/ppermute | solution.py:351
  38.2 1.5 %collective-permute-done.11.r_2_ = f32[8,128]{1,0:T(8,128)S(1)} collective-permute-done((f32[8,128]{1,0:T(8,128)S(1)}, f32[8,128]{1,0:T(8,128)S(1)}, u32[]{:S(2)}, u32[]{:S(2)}) %collective-permute-start.11) | collective-permute-done | bytes 4128 | tf_op jit(solution)/shard_map/ppermute | solution.py:351
  40.3 4.1 %sums_first.1 = (bf16[10,288,768]{2,1,0:T(8,128)(2,1)S(1)}, bf16[288,96]{1,0:T(8,128)(2,1)S(1)}, f32[288,256]{1,0:T(8,128)S(1)}, bf16[304,256]{1,0:T(8,128)(2,1)...) custom-call(f32[8,128]{1,0:T(8,128)S(1)} %get-tuple-element.91.r_0_,, ...), custom_call_target="tpu_custom_call", output_to_operand_aliasing={{5}: (9, {}), {6}: (10, {}), {7}: (11, {})} | custom-call | flops 1 | bytes 1 | tf_op jit(solution)/shard_map/sums_first/pallas_call | solution.py:375
  44.5 2.5 %sums.3 = (f32[288,256]{1,0:T(8,128)S(1)}, bf16[288,256]{1,0:T(8,128)(2,1)S(1)}, bf16[7680,512]{1,0:T(8,128)(2,1)S(1)}, bf16[7680,512]{1,0:T(8,128)(2,1)S(1)}) custom-call(bf16[10,288,768]{2,1,0:T(8,128)(2,1)S(1)} %get-tuple-element.99.r_0_, bf16[288,96]{1,0:T(8,128)(2,1)S(1)} %get-tuple-element.116.r_1_, ...), custom_call_target="tpu_custom_call", output_to_operand_aliasing={{2}: (4, {}), {3}: (5, {})} | custom-call | flops 1 | bytes 1 | tf_op jit(solution)/shard_map/sums/pallas_call | solution.py:375
  47.7 2.1 %collective-permute-start.17 = (bf16[304,256]{1,0:T(8,128)(2,1)S(1)}, bf16[304,256]{1,0:T(8,128)(2,1)S(1)}, u32[]{:S(2)}, u32[]{:S(2)}) collective-permute-start(bf16[304,256]{1,0:T(8,128)(2,1)S(1)} %get-tuple-element.115), channel_id=1, source_target_pairs={{0,8},{4,12},{8,0},{12,4},{16,24},{20,28},{24,16},{28,20},{1,9},{5... | collective-permute-start | bytes 466952 | tf_op jit(solution)/shard_map/ppermute | solution.py:351
  49.8 2.5 %sums.4 = (f32[288,256]{1,0:T(8,128)S(1)}, bf16[288,256]{1,0:T(8,128)(2,1)S(1)}, bf16[7680,512]{1,0:T(8,128)(2,1)S(1)}) custom-call(bf16[10,288,768]{2,1,0:T(8,128)(2,1)S(1)} %get-tuple-element.99.r_0_, bf16[288,96]{1,0:T(8,128)(2,1)S(1)} %get-tuple-element.116.r_1_, bf16[7680,512]{1,0:T(8,128)(2,1)S(1)} %get-tuple-element.111.r_2_, ...), custom_call_target="tpu_custom_call", output_to_operand_aliasing={{2}: (4, {})} | custom-call | flops 1 | bytes 1 | tf_op jit(solution)/shard_map/sums/pallas_call | solution.py:375
  52.4 1.2 %collective-permute-start.15 = (bf16[304,256]{1,0:T(8,128)(2,1)S(1)}, bf16[304,256]{1,0:T(8,128)(2,1)S(1)}, u32[]{:S(2)}, u32[]{:S(2)}) collective-permute-start(bf16[304,256]{1,0:T(8,128)(2,1)S(1)} %pair.2), channel_id=1, source_target_pairs={{0,8},{4,12},{8,0},{12,4},{16,24},{20,28},{24,16},{28,20},{1,9},{5... | collective-permute-start | bytes 466952 | tf_op jit(solution)/shard_map/ppermute | solution.py:351
  54.0 1.1 %collective-permute-start.18 = (bf16[304,256]{1,0:T(8,128)(2,1)S(1)}, bf16[304,256]{1,0:T(8,128)(2,1)S(1)}, u32[]{:S(2)}, u32[]{:S(2)}) collective-permute-start(bf16[304,256]{1,0:T(8,128)(2,1)S(1)} %pair.3), channel_id=1, source_target_pairs={{0,16},{4,20},{8,24},{12,28},{16,0},{20,4},{24,8},{28,12},{1,17},{... | collective-permute-start | bytes 466952 | tf_op jit(solution)/shard_map/ppermute | solution.py:351
  55.1 2.5 %sums.5 = (f32[288,256]{1,0:T(8,128)S(1)}, bf16[288,256]{1,0:T(8,128)(2,1)S(1)}) custom-call(bf16[10,288,768]{2,1,0:T(8,128)(2,1)S(1)} %get-tuple-element.99.r_0_, bf16[288,96]{1,0:T(8,128)(2,1)S(1)} %get-tuple-element.116.r_1_, bf16[7680,512]{1,0:T(8,128)(2,1)S(1)} %get-tuple-element.117.r_2_, bf16[96,2048]{1,0:T(8,128)(2,1)S(1)} %get-tuple-element.68.r_3_.r_6_.r_8_), custom_call_target="tpu_custom_call" | custom-call | flops 1 | bytes 1 | tf_op jit(solution)/shard_map/sums/pallas_call | solution.py:375
  57.7 2.9 %collective-permute-done.15.r_0_ = bf16[304,256]{1,0:T(8,128)(2,1)S(1)} collective-permute-done((bf16[304,256]{1,0:T(8,128)(2,1)S(1)}, bf16[304,256]{1,0:T(8,128)(2,1)S(1)}, u32[]{:S(2)}, u32[]{:S(2)}) %collective-permute-start.15) | collective-permute-done | bytes 155680 | tf_op jit(solution)/shard_map/ppermute | solution.py:351
  60.6 3.6 %collective-permute-done.18.r_1_ = bf16[304,256]{1,0:T(8,128)(2,1)S(1)} collective-permute-done((bf16[304,256]{1,0:T(8,128)(2,1)S(1)}, bf16[304,256]{1,0:T(8,128)(2,1)S(1)}, u32[]{:S(2)}, u32[]{:S(2)}) %collective-permute-start.18) | collective-permute-done | bytes 155680 | tf_op jit(solution)/shard_map/ppermute | solution.py:351
  64.3 1.0 %finish.1 = (f32[288,256]{1,0:T(8,128)}, f32[8,36]{1,0:T(8,128)}) custom-call(bf16[304,256]{1,0:T(8,128)(2,1)S(1)} %collective-permute-done.15.r_0_, bf16[304,256]{1,0:T(8,128)(2,1)S(1)} %collective-permute-done.18.r_1_, f32[288,256]{1,0:T(8,128)S(1)} %get-tuple-element.118.r_2_, bf16[288,256]{1,0:T(8,128)(2,1)S(1)} %collective-permute-done.19.r_3_, ...), custom_call_target="tpu_custom_call" | custom-call | flops 1 | bytes 1 | tf_op jit(solution)/shard_map/finish/pallas_call | solution.py:375
  (30 shorter events, 3.6 us)
Async XLA Ops:
  0.6 10.5 %collective-permute-start.1 = (bf16[96,512]{1,0:T(8,128)(2,1)}, bf16[96,512]{1,0:T(8,128)(2,1)S(1)}, u32[]{:S(2)}, u32[]{:S(2)}) collective-permute-start(bf16[96,512]{1,0:T(8,128)(2,1)} %r_4_.1), channel_id=1, source_target_pairs={{0,1},{1,0},{2,3},{3,2},{4,5},{5,4},{6,7},{7,6},{8,9},{9,8},{10,11... | collective-permute-start | bytes 294920 | tf_op jit(solution)/shard_map/ppermute | solution.py:351
  3.6 8.2 %collective-permute-start.3 = (bf16[96,512]{1,0:T(8,128)(2,1)}, bf16[96,512]{1,0:T(8,128)(2,1)S(1)}, u32[]{:S(2)}, u32[]{:S(2)}) collective-permute-start(bf16[96,512]{1,0:T(8,128)(2,1)} %r_4_.1), channel_id=1, source_target_pairs={{0,3},{1,2},{2,1},{3,0},{4,7},{5,6},{6,5},{7,4},{8,11},{9,10},{10,... | collective-permute-start | bytes 294920 | tf_op jit(solution)/shard_map/ppermute | solution.py:351
  5.1 6.7 %collective-permute-start.2 = (bf16[96,512]{1,0:T(8,128)(2,1)}, bf16[96,512]{1,0:T(8,128)(2,1)S(1)}, u32[]{:S(2)}, u32[]{:S(2)}) collective-permute-start(bf16[96,512]{1,0:T(8,128)(2,1)} %r_4_.1), channel_id=1, source_target_pairs={{0,2},{1,3},{2,0},{3,1},{4,6},{5,7},{6,4},{7,5},{8,10},{9,11},{10,... | collective-permute-start | bytes 294920 | tf_op jit(solution)/shard_map/ppermute | solution.py:351
  7.0 16.5 %collective-permute-start.7 = (bf16[304,256]{1,0:T(8,128)(2,1)S(1)}, bf16[304,256]{1,0:T(8,128)(2,1)S(1)}, u32[]{:S(2)}, u32[]{:S(2)}) collective-permute-start(bf16[304,256]{1,0:T(8,128)(2,1)S(1)} %get-tuple-element.62.r_0_), channel_id=1, source_target_pairs={{0,24},{4,28},{8,16},{12,20},{16,8},{20,12},{24,0},{28,4},{1,25},{... | collective-permute-start | bytes 466952 | tf_op jit(solution)/shard_map/ppermute | solution.py:351
  11.2 12.3 %collective-permute-start.5 = (bf16[304,256]{1,0:T(8,128)(2,1)S(1)}, bf16[304,256]{1,0:T(8,128)(2,1)S(1)}, u32[]{:S(2)}, u32[]{:S(2)}) collective-permute-start(bf16[304,256]{1,0:T(8,128)(2,1)S(1)} %get-tuple-element.62.r_0_), channel_id=1, source_target_pairs={{0,16},{4,20},{8,24},{12,28},{16,0},{20,4},{24,8},{28,12},{1,17},{... | collective-permute-start | bytes 466952 | tf_op jit(solution)/shard_map/ppermute | solution.py:351
  11.2 9.2 %collective-permute-start.4 = (bf16[304,256]{1,0:T(8,128)(2,1)S(1)}, bf16[304,256]{1,0:T(8,128)(2,1)S(1)}, u32[]{:S(2)}, u32[]{:S(2)}) collective-permute-start(bf16[304,256]{1,0:T(8,128)(2,1)S(1)} %get-tuple-element.62.r_0_), channel_id=1, source_target_pairs={{0,8},{4,12},{8,0},{12,4},{16,24},{20,28},{24,16},{28,20},{1,9},{5... | collective-permute-start | bytes 466952 | tf_op jit(solution)/shard_map/ppermute | solution.py:351
  11.8 8.5 %collective-permute-start = (bf16[304,256]{1,0:T(8,128)(2,1)S(1)}, bf16[304,256]{1,0:T(8,128)(2,1)S(1)}, u32[]{:S(2)}, u32[]{:S(2)}) collective-permute-start(bf16[304,256]{1,0:T(8,128)(2,1)S(1)} %get-tuple-element.62.r_0_), channel_id=1, source_target_pairs={{0,4},{4,0},{8,12},{12,8},{16,20},{20,16},{24,28},{28,24},{1,5},{5... | collective-permute-start | bytes 466952 | tf_op jit(solution)/shard_map/ppermute | solution.py:351
  20.3 3.7 %collective-permute-start.9 = (bf16[304,256]{1,0:T(8,128)(2,1)S(1)}, bf16[304,256]{1,0:T(8,128)(2,1)S(1)}, u32[]{:S(2)}, u32[]{:S(2)}) collective-permute-start(bf16[304,256]{1,0:T(8,128)(2,1)S(1)} %collective-permute-done.4.r_0_), channel_id=1, source_target_pairs={{0,4},{4,0},{8,12},{12,8},{16,20},{20,16},{24,28},{28,24},{1,5},{5... | collective-permute-start | bytes 466952 | tf_op jit(solution)/shard_map/ppermute | solution.py:351
  23.5 4.1 %collective-permute-start.8 = (bf16[304,256]{1,0:T(8,128)(2,1)S(1)}, bf16[304,256]{1,0:T(8,128)(2,1)S(1)}, u32[]{:S(2)}, u32[]{:S(2)}) collective-permute-start(bf16[304,256]{1,0:T(8,128)(2,1)S(1)} %collective-permute-done.7.r_2_), channel_id=1, source_target_pairs={{0,4},{4,0},{8,12},{12,8},{16,20},{20,16},{24,28},{28,24},{1,5},{5... | collective-permute-start | bytes 466952 | tf_op jit(solution)/shard_map/ppermute | solution.py:351
  23.5 4.1 %collective-permute-start.6 = (bf16[304,256]{1,0:T(8,128)(2,1)S(1)}, bf16[304,256]{1,0:T(8,128)(2,1)S(1)}, u32[]{:S(2)}, u32[]{:S(2)}) collective-permute-start(bf16[304,256]{1,0:T(8,128)(2,1)S(1)} %collective-permute-done.5.r_0_), channel_id=1, source_target_pairs={{0,4},{4,0},{8,12},{12,8},{16,20},{20,16},{24,28},{28,24},{1,5},{5... | collective-permute-start | bytes 466952 | tf_op jit(solution)/shard_map/ppermute | solution.py:351
  33.7 4.6 %collective-permute-start.12 = (f32[8,128]{1,0:T(8,128)S(1)}, f32[8,128]{1,0:T(8,128)S(1)}, u32[]{:S(2)}, u32[]{:S(2)}) collective-permute-start(f32[8,128]{1,0:T(8,128)S(1)} %get-tuple-element.91.r_0_), channel_id=1, source_target_pairs={{0,3},{1,2},{2,1},{3,0},{4,7},{5,6},{6,5},{7,4},{8,11},{9,10},{10,... | collective-permute-start | bytes 12296 | tf_op jit(solution)/shard_map/ppermute | solution.py:351
  36.2 3.6 %collective-permute-start.11 = (f32[8,128]{1,0:T(8,128)S(1)}, f32[8,128]{1,0:T(8,128)S(1)}, u32[]{:S(2)}, u32[]{:S(2)}) collective-permute-start(f32[8,128]{1,0:T(8,128)S(1)} %get-tuple-element.91.r_0_), channel_id=1, source_target_pairs={{0,2},{1,3},{2,0},{3,1},{4,6},{5,7},{6,4},{7,5},{8,10},{9,11},{10,... | collective-permute-start | bytes 12296 | tf_op jit(solution)/shard_map/ppermute | solution.py:351
  36.7 3.6 %collective-permute-start.10 = (f32[8,128]{1,0:T(8,128)S(1)}, f32[8,128]{1,0:T(8,128)S(1)}, u32[]{:S(2)}, u32[]{:S(2)}) collective-permute-start(f32[8,128]{1,0:T(8,128)S(1)} %get-tuple-element.91.r_0_), channel_id=1, source_target_pairs={{0,1},{1,0},{2,3},{3,2},{4,5},{5,4},{6,7},{7,6},{8,9},{9,8},{10,11... | collective-permute-start | bytes 12296 | tf_op jit(solution)/shard_map/ppermute | solution.py:351
  44.5 3.1 %collective-permute-start.14 = (bf16[304,256]{1,0:T(8,128)(2,1)S(1)}, bf16[304,256]{1,0:T(8,128)(2,1)S(1)}, u32[]{:S(2)}, u32[]{:S(2)}) collective-permute-start(bf16[304,256]{1,0:T(8,128)(2,1)S(1)} %get-tuple-element.107), channel_id=1, source_target_pairs={{0,4},{4,0},{8,12},{12,8},{16,20},{20,16},{24,28},{28,24},{1,5},{5... | collective-permute-start | bytes 466952 | tf_op jit(solution)/shard_map/ppermute | solution.py:351
  47.0 2.7 %collective-permute-start.13 = (bf16[288,256]{1,0:T(8,128)(2,1)S(1)}, bf16[288,256]{1,0:T(8,128)(2,1)S(1)}, u32[]{:S(2)}, u32[]{:S(2)}) collective-permute-start(bf16[288,256]{1,0:T(8,128)(2,1)S(1)} %get-tuple-element.105), channel_id=1, source_target_pairs={{0,4},{4,0},{8,12},{12,8},{16,20},{20,16},{24,28},{28,24},{1,5},{5... | collective-permute-start | bytes 442376 | tf_op jit(solution)/shard_map/ppermute | solution.py:351
  47.7 6.3 %collective-permute-start.17 = (bf16[304,256]{1,0:T(8,128)(2,1)S(1)}, bf16[304,256]{1,0:T(8,128)(2,1)S(1)}, u32[]{:S(2)}, u32[]{:S(2)}) collective-permute-start(bf16[304,256]{1,0:T(8,128)(2,1)S(1)} %get-tuple-element.115), channel_id=1, source_target_pairs={{0,8},{4,12},{8,0},{12,4},{16,24},{20,28},{24,16},{28,20},{1,9},{5... | collective-permute-start | bytes 466952 | tf_op jit(solution)/shard_map/ppermute | solution.py:351
  52.3 1.4 %collective-permute-start.16 = (bf16[288,256]{1,0:T(8,128)(2,1)S(1)}, bf16[288,256]{1,0:T(8,128)(2,1)S(1)}, u32[]{:S(2)}, u32[]{:S(2)}) collective-permute-start(bf16[288,256]{1,0:T(8,128)(2,1)S(1)} %get-tuple-element.114), channel_id=1, source_target_pairs={{0,4},{4,0},{8,12},{12,8},{16,20},{20,16},{24,28},{28,24},{1,5},{5... | collective-permute-start | bytes 442376 | tf_op jit(solution)/shard_map/ppermute | solution.py:351
  52.4 8.3 %collective-permute-start.15 = (bf16[304,256]{1,0:T(8,128)(2,1)S(1)}, bf16[304,256]{1,0:T(8,128)(2,1)S(1)}, u32[]{:S(2)}, u32[]{:S(2)}) collective-permute-start(bf16[304,256]{1,0:T(8,128)(2,1)S(1)} %pair.2), channel_id=1, source_target_pairs={{0,8},{4,12},{8,0},{12,4},{16,24},{20,28},{24,16},{28,20},{1,9},{5... | collective-permute-start | bytes 466952 | tf_op jit(solution)/shard_map/ppermute | solution.py:351
  54.0 10.2 %collective-permute-start.18 = (bf16[304,256]{1,0:T(8,128)(2,1)S(1)}, bf16[304,256]{1,0:T(8,128)(2,1)S(1)}, u32[]{:S(2)}, u32[]{:S(2)}) collective-permute-start(bf16[304,256]{1,0:T(8,128)(2,1)S(1)} %pair.3), channel_id=1, source_target_pairs={{0,16},{4,20},{8,24},{12,28},{16,0},{20,4},{24,8},{28,12},{1,17},{... | collective-permute-start | bytes 466952 | tf_op jit(solution)/shard_map/ppermute | solution.py:351
  57.6 3.0 %collective-permute-start.19 = (bf16[288,256]{1,0:T(8,128)(2,1)S(1)}, bf16[288,256]{1,0:T(8,128)(2,1)S(1)}, u32[]{:S(2)}, u32[]{:S(2)}) collective-permute-start(bf16[288,256]{1,0:T(8,128)(2,1)S(1)} %get-tuple-element.119), channel_id=1, source_target_pairs={{0,4},{4,0},{8,12},{12,8},{16,20},{20,16},{24,28},{28,24},{1,5},{5... | collective-permute-start | bytes 442376 | tf_op jit(solution)/shard_map/ppermute | solution.py:351

commit v5 on v4

--- a/solution.py
+++ b/solution.py
@@ -17,7 +17,7 @@
 GROUP = 8
 MAIN = SHIFTS // GROUP * GROUP
 STEPS = MAIN // GROUP
-TAIL = 16
+TAIL = 8
 F32 = jnp.float32
 BF16 = jnp.bfloat16
 
@@ -234,9 +234,9 @@
         ahead(0)
     sums[...] = contract(probs_rest[...], moved_rest[:, rest_at : rest_at + sums.shape[1]], ((1,), (0,)))
     for i in range(STEPS):
+        sums[...] += contract(probs[i], moved[i * block : (i + 1) * block, :], ((1,), (0,)))
         if ahead and i + 1 < STEPS:
             ahead(i + 1)
-        sums[...] += contract(probs[i], moved[i * block : (i + 1) * block, :], ((1,), (0,)))
 
 
 def first_sums_body(*refs, groups, others, length, rest_at):
@@ -411,7 +411,10 @@
             ],
         )
 
-        even = [message] + [swap(message, "dom", dom, 2 * k) for k in range(1, pairs)]
+        even = [message] + [None] * (pairs - 1)
+        for k in range(1, pairs):
+            if not k & (k - 1):
+                even[k] = swap(message, "dom", dom, 2 * k)
         odd = [swap(message, "dom", dom, 1)]
 
         *moved, moved_rest = call(
@@ -422,6 +425,12 @@
             limit=2,
             scratch=[pltpu.VMEM((rows, F), F32)] * 2,
         )(where, *pieces, *angles)
+
+        for k in range(1, pairs):
+            if k & (k - 1):
+                source = k & (k - 1)
+                moved_rest, even[source] = lax.optimization_barrier((moved_rest, even[source]))
+                even[k] = swap(even[source], "dom", dom, 2 * (k & -k))
 
         held = pltpu.VMEM((MAIN * rows, 2 * width), BF16)
         partial = []
@@ -450,12 +459,17 @@
                 ]
             else:
                 outs += [shape((8, length), F32)]
-                for k in stages[n + 1]:
+                for k in sorted(stages[n + 1] if n == 0 else [j for j in stages[n + 1] if not j & (j - 1)]):
                     if partial:
                         partial[2], even[k] = lax.optimization_barrier((partial[2], even[k]))
                     else:
                         moved_rest, even[k] = lax.optimization_barrier((moved_rest, even[k]))
                     odd.append(swap(even[k], "dom", dom, 1))
+            if n > 1:
+                for k in stage:
+                    if k & (k - 1):
+                        partial[2], even[k] = lax.optimization_barrier((partial[2], even[k]))
+                        odd.append(swap(even[k], "dom", dom, 1))
             results = call(
                 lambda *r: body(
                     *r,

time: 65.4 us -> 64.6 us (0.988)
  waiting for transfers between devices: 12.5 us -> 9.19 us
  starting transfers between devices: 18.5 us -> 20.8 us
    ppermute x20, waiting for transfers between devices: 12.5 us -> 9.19 us  [swap(): return lax.ppermute(x, axis, [(i, i ^ k) for i in range(size)])]
    ppermute x20, starting transfers between devices: 18.5 us -> 20.8 us  [swap(): return lax.ppermute(x, axis, [(i, i ^ k) for i in range(size)])]
  transfers between devices with their start and end apart: 20 -> 20, of which waited for: 9 -> 8; matrix products, arithmetic and copies ran while one was open for 0% -> 0% of each run, Pallas kernels for 34% -> 35%
where the time goes in v5:
time: 64.6 us; the launch traced here: 64.4 us
  Pallas kernels  33.6 us (52%)
  starting transfers between devices  20.8 us (32%)
  waiting for transfers between devices  9.19 us (14%)
  between operations  0.78 us (1%)
    pallas_call x13, Pallas kernels, run(): pl.pallas_call(body, grid_spec=spec, out_shape=shapes, compiler_params=pa...  33.6 us
    ppermute x20, starting transfers between devices, swap(): return lax.ppermute(x, axis, [(i, i ^ k) for i in range(size)])  20.8 us
    ppermute x20, waiting for transfers between devices, swap(): return lax.ppermute(x, axis, [(i, i ^ k) for i in range(size)])  9.19 us
  transfers between devices with their start and end apart: 20, of which 8 were waited for; matrix products, arithmetic and copies ran while one was open for 0% of the time, Pallas kernels for 35%

profile of v5, /device:TPU:0, one launch (start us, length us, event | category | flops | bytes accessed | tf_op | source)
XLA Modules:
  0.0 64.4 jit_solution(753515778163790981)
XLA Ops:
  0.6 3.0 %collective-permute-start.1 = (bf16[96,512]{1,0:T(8,128)(2,1)}, bf16[96,512]{1,0:T(8,128)(2,1)S(1)}, u32[]{:S(2)}, u32[]{:S(2)}) collective-permute-start(bf16[96,512]{1,0:T(8,128)(2,1)} %r_4_.1), channel_id=1, source_target_pairs={{0,1},{1,0},{2,3},{3,2},{4,5},{5,4},{6,7},{7,6},{8,9},{9,8},{10,11... | collective-permute-start | bytes 294920 | tf_op jit(solution)/shard_map/ppermute | solution.py:351
  3.6 1.5 %collective-permute-start.3 = (bf16[96,512]{1,0:T(8,128)(2,1)}, bf16[96,512]{1,0:T(8,128)(2,1)S(1)}, u32[]{:S(2)}, u32[]{:S(2)}) collective-permute-start(bf16[96,512]{1,0:T(8,128)(2,1)} %r_4_.1), channel_id=1, source_target_pairs={{0,3},{1,2},{2,1},{3,0},{4,7},{5,6},{6,5},{7,4},{8,11},{9,10},{10,... | collective-permute-start | bytes 294920 | tf_op jit(solution)/shard_map/ppermute | solution.py:351
  5.3 1.8 %begin.1 = (bf16[296,256]{1,0:T(8,128)(2,1)S(1)}, f32[40,1024]{1,0:T(8,128)S(1)}, f32[40,1024]{1,0:T(8,128)S(1)}, bf16[96,512]{1,0:T(8,128)(2,1)S(1)}) custom-call(s32[3]{0:T(128)S(1)} %pad_add_fusion.r_0_, f32[288,256]{1,0:T(8,128)} %bitcast.10, f32[1,1024]{1,0:T(1,128)} %bitcast.11, f32[2,40,1024]{2,1,0:T(8,128)} %constant.24.clone.r_3_, bf16[96,512]{1,0:T(8,128)(2,1)} %r_4_.1), custom_call_target="tpu_custom_call" | custom-call | flops 1 | bytes 1 | tf_op jit(solution)/shard_map/begin/pallas_call | solution.py:375
  7.0 2.1 %collective-permute-start.5 = (bf16[296,256]{1,0:T(8,128)(2,1)S(1)}, bf16[296,256]{1,0:T(8,128)(2,1)S(1)}, u32[]{:S(2)}, u32[]{:S(2)}) collective-permute-start(bf16[296,256]{1,0:T(8,128)(2,1)S(1)} %get-tuple-element.64.r_0_), channel_id=1, source_target_pairs={{0,8},{4,12},{8,0},{12,4},{16,24},{20,28},{24,16},{28,20},{1,9},{5... | collective-permute-start | bytes 454664 | tf_op jit(solution)/shard_map/ppermute | solution.py:351
  9.1 2.6 %collective-permute-start.4 = (bf16[296,256]{1,0:T(8,128)(2,1)S(1)}, bf16[296,256]{1,0:T(8,128)(2,1)S(1)}, u32[]{:S(2)}, u32[]{:S(2)}) collective-permute-start(bf16[296,256]{1,0:T(8,128)(2,1)S(1)} %get-tuple-element.64.r_0_), channel_id=1, source_target_pairs={{0,16},{4,20},{8,24},{12,28},{16,0},{20,4},{24,8},{28,12},{1,17},{... | collective-permute-start | bytes 454664 | tf_op jit(solution)/shard_map/ppermute | solution.py:351
  11.7 6.6 %shift.1 = (bf16[7680,512]{1,0:T(8,128)(2,1)S(1)}, bf16[7680,512]{1,0:T(8,128)(2,1)S(1)}, bf16[7680,512]{1,0:T(8,128)(2,1)S(1)}, bf16[7680,512]{1,0:T(8,128)(2,1)S(1)}, bf16[96,2048]{1,0:T(8,128)(2,1)S(1)}) custom-call(s32[3]{0:T(128)S(1)} %pad_add_fusion.r_0_, bf16[96,512]{1,0:T(8,128)(2,1)S(1)} %get-tuple-element.65.r_1_, ...), custom_call_target="tpu_custom_call" | custom-call | flops 10000000000 | bytes 1 | tf_op jit(solution)/shard_map/shift/pallas_call | solution.py:375
  19.0 0.7 %collective-permute-start.8 = (bf16[296,256]{1,0:T(8,128)(2,1)S(1)}, bf16[296,256]{1,0:T(8,128)(2,1)S(1)}, u32[]{:S(2)}, u32[]{:S(2)}) collective-permute-start(bf16[296,256]{1,0:T(8,128)(2,1)S(1)} %collective-permute-done.4.r_0_), channel_id=1, source_target_pairs={{0,8},{4,12},{8,0},{12,4},{16,24},{20,28},{24,16},{28,20},{1,9},{5... | collective-permute-start | bytes 454664 | tf_op jit(solution)/shard_map/ppermute | solution.py:351
  19.7 2.5 %score.3 = (f32[10,288,768]{2,1,0:T(8,128)S(1)}, f32[288,96]{1,0:T(8,128)S(1)}, f32[8,512]{1,0:T(8,128)S(1)}, bf16[7680,512]{1,0:T(8,128)(2,1)S(1)}, bf16[7680,5...) custom-call(bf16[296,256]{1,0:T(8,128)(2,1)S(1)} %get-tuple-element., ...), custom_call_target="tpu_custom_call", output_to_operand_aliasing={{3}: (2, {}), {4}: (4, {}), {5}: (5, {}), {6}: (6, {})} | custom-call | flops 1 | bytes 1 | tf_op jit(solution)/shard_map/score/pallas_call | solution.py:375
  22.4 3.6 %score.4 = (f32[10,288,768]{2,1,0:T(8,128)S(1)}, f32[288,96]{1,0:T(8,128)S(1)}, f32[8,512]{1,0:T(8,128)S(1)}, bf16[7680,512]{1,0:T(8,128)(2,1)S(1)}, bf16[7680,5...) custom-call(bf16[296,256]{1,0:T(8,128)(2,1)S(1)} %collective-permute, ...), custom_call_target="tpu_custom_call", output_to_operand_aliasing={{4}: (2, {}), {3}: (7, {}), {5}: (8, {}), {6}: (9, {}), {0}... | custom-call | flops 1 | bytes 1 | tf_op jit(solution)/shard_map/score/pallas_call | solution.py:375
  26.5 1.0 %collective-permute-done.9.r_3_ = bf16[296,256]{1,0:T(8,128)(2,1)S(1)} collective-permute-done((bf16[296,256]{1,0:T(8,128)(2,1)S(1)}, bf16[296,256]{1,0:T(8,128)(2,1)S(1)}, u32[]{:S(2)}, u32[]{:S(2)}) %collective-permute-start.9) | collective-permute-done | bytes 151584 | tf_op jit(solution)/shard_map/ppermute | solution.py:351
  27.5 6.2 %score.5 = (f32[10,288,768]{2,1,0:T(8,128)S(1)}, f32[288,96]{1,0:T(8,128)S(1)}, f32[11,8,768]{2,1,0:T(8,128)S(1)}, f32[8,128]{1,0:T(8,128)S(1)}, bf16[7680,512]{...) custom-call(bf16[296,256]{1,0:T(8,128)(2,1)S(1)} %collective-permute, ...), custom_call_target="tpu_custom_call", output_to_operand_aliasing={{6}: (4, {}), {7}: (5, {}), {4}: (10, {}), {5}: (11, {}), {... | custom-call | flops 1 | bytes 1 | tf_op jit(solution)/shard_map/score/pallas_call | solution.py:375
  33.7 2.3 %collective-permute-start.12 = (f32[8,128]{1,0:T(8,128)S(1)}, f32[8,128]{1,0:T(8,128)S(1)}, u32[]{:S(2)}, u32[]{:S(2)}) collective-permute-start(f32[8,128]{1,0:T(8,128)S(1)} %get-tuple-element.95.r_0_), channel_id=1, source_target_pairs={{0,3},{1,2},{2,1},{3,0},{4,7},{5,6},{6,5},{7,4},{8,11},{9,10},{10,... | collective-permute-start | bytes 12296 | tf_op jit(solution)/shard_map/ppermute | solution.py:351
  37.2 1.0 %collective-permute-done.12.r_3_ = f32[8,128]{1,0:T(8,128)S(1)} collective-permute-done((f32[8,128]{1,0:T(8,128)S(1)}, f32[8,128]{1,0:T(8,128)S(1)}, u32[]{:S(2)}, u32[]{:S(2)}) %collective-permute-start.12) | collective-permute-done | bytes 4128 | tf_op jit(solution)/shard_map/ppermute | solution.py:351
  38.3 1.3 %collective-permute-done.11.r_2_ = f32[8,128]{1,0:T(8,128)S(1)} collective-permute-done((f32[8,128]{1,0:T(8,128)S(1)}, f32[8,128]{1,0:T(8,128)S(1)}, u32[]{:S(2)}, u32[]{:S(2)}) %collective-permute-start.11) | collective-permute-done | bytes 4128 | tf_op jit(solution)/shard_map/ppermute | solution.py:351
  40.2 4.1 %sums_first.1 = (bf16[10,288,768]{2,1,0:T(8,128)(2,1)S(1)}, bf16[288,96]{1,0:T(8,128)(2,1)S(1)}, f32[288,256]{1,0:T(8,128)S(1)}, bf16[296,256]{1,0:T(8,128)(2,1)...) custom-call(f32[8,128]{1,0:T(8,128)S(1)} %get-tuple-element.95.r_0_,, ...), custom_call_target="tpu_custom_call", output_to_operand_aliasing={{5}: (9, {}), {6}: (10, {}), {7}: (11, {})} | custom-call | flops 1 | bytes 1 | tf_op jit(solution)/shard_map/sums_first/pallas_call | solution.py:375
  44.4 2.5 %sums.3 = (f32[288,256]{1,0:T(8,128)S(1)}, bf16[288,256]{1,0:T(8,128)(2,1)S(1)}, bf16[7680,512]{1,0:T(8,128)(2,1)S(1)}, bf16[7680,512]{1,0:T(8,128)(2,1)S(1)}) custom-call(bf16[10,288,768]{2,1,0:T(8,128)(2,1)S(1)} %get-tuple-element.103.r_0_, bf16[288,96]{1,0:T(8,128)(2,1)S(1)} %get-tuple-element.120.r_1_, ...), custom_call_target="tpu_custom_call", output_to_operand_aliasing={{2}: (4, {}), {3}: (5, {})} | custom-call | flops 1 | bytes 1 | tf_op jit(solution)/shard_map/sums/pallas_call | solution.py:375
  47.6 1.5 %collective-permute-start.17 = (bf16[296,256]{1,0:T(8,128)(2,1)S(1)}, bf16[296,256]{1,0:T(8,128)(2,1)S(1)}, u32[]{:S(2)}, u32[]{:S(2)}) collective-permute-start(bf16[296,256]{1,0:T(8,128)(2,1)S(1)} %get-tuple-element.119), channel_id=1, source_target_pairs={{0,8},{4,12},{8,0},{12,4},{16,24},{20,28},{24,16},{28,20},{1,9},{5... | collective-permute-start | bytes 454664 | tf_op jit(solution)/shard_map/ppermute | solution.py:351
  49.2 2.5 %sums.4 = (f32[288,256]{1,0:T(8,128)S(1)}, bf16[288,256]{1,0:T(8,128)(2,1)S(1)}, bf16[7680,512]{1,0:T(8,128)(2,1)S(1)}) custom-call(bf16[10,288,768]{2,1,0:T(8,128)(2,1)S(1)} %get-tuple-element.103.r_0_, bf16[288,96]{1,0:T(8,128)(2,1)S(1)} %get-tuple-element.120.r_1_, ...), custom_call_target="tpu_custom_call", output_to_operand_aliasing={{2}: (4, {})} | custom-call | flops 1 | bytes 1 | tf_op jit(solution)/shard_map/sums/pallas_call | solution.py:375
  51.7 1.2 %collective-permute-start.15 = (bf16[296,256]{1,0:T(8,128)(2,1)S(1)}, bf16[296,256]{1,0:T(8,128)(2,1)S(1)}, u32[]{:S(2)}, u32[]{:S(2)}) collective-permute-start(bf16[296,256]{1,0:T(8,128)(2,1)S(1)} %pair.2), channel_id=1, source_target_pairs={{0,8},{4,12},{8,0},{12,4},{16,24},{20,28},{24,16},{28,20},{1,9},{5... | collective-permute-start | bytes 454664 | tf_op jit(solution)/shard_map/ppermute | solution.py:351
  53.6 2.7 %collective-permute-start.18 = (bf16[296,256]{1,0:T(8,128)(2,1)S(1)}, bf16[296,256]{1,0:T(8,128)(2,1)S(1)}, u32[]{:S(2)}, u32[]{:S(2)}) collective-permute-start(bf16[296,256]{1,0:T(8,128)(2,1)S(1)} %pair.3), channel_id=1, source_target_pairs={{0,16},{4,20},{8,24},{12,28},{16,0},{20,4},{24,8},{28,12},{1,17},{... | collective-permute-start | bytes 454664 | tf_op jit(solution)/shard_map/ppermute | solution.py:351
  56.3 2.5 %sums.5 = (f32[288,256]{1,0:T(8,128)S(1)}, bf16[288,256]{1,0:T(8,128)(2,1)S(1)}) custom-call(bf16[10,288,768]{2,1,0:T(8,128)(2,1)S(1)} %get-tuple-element.103.r_0_, bf16[288,96]{1,0:T(8,128)(2,1)S(1)} %get-tuple-element.120.r_1_, bf16[7680,512]{1,0:T(8,128)(2,1)S(1)} %get-tuple-element.121.r_2_, bf16[96,2048]{1,0:T(8,128)(2,1)S(1)} %get-tuple-element.71.r_3_.r_6_.r_8_), custom_call_target="tpu_custom_call" | custom-call | flops 1 | bytes 1 | tf_op jit(solution)/shard_map/sums/pallas_call | solution.py:375
  58.9 1.9 %collective-permute-done.15.r_0_ = bf16[296,256]{1,0:T(8,128)(2,1)S(1)} collective-permute-done((bf16[296,256]{1,0:T(8,128)(2,1)S(1)}, bf16[296,256]{1,0:T(8,128)(2,1)S(1)}, u32[]{:S(2)}, u32[]{:S(2)}) %collective-permute-start.15) | collective-permute-done | bytes 151584 | tf_op jit(solution)/shard_map/ppermute | solution.py:351
  60.8 2.7 %collective-permute-done.18.r_1_ = bf16[296,256]{1,0:T(8,128)(2,1)S(1)} collective-permute-done((bf16[296,256]{1,0:T(8,128)(2,1)S(1)}, bf16[296,256]{1,0:T(8,128)(2,1)S(1)}, u32[]{:S(2)}, u32[]{:S(2)}) %collective-permute-start.18) | collective-permute-done | bytes 151584 | tf_op jit(solution)/shard_map/ppermute | solution.py:351
  63.4 1.0 %finish.1 = (f32[288,256]{1,0:T(8,128)}, f32[8,36]{1,0:T(8,128)}) custom-call(bf16[296,256]{1,0:T(8,128)(2,1)S(1)} %collective-permute-done.15.r_0_, bf16[296,256]{1,0:T(8,128)(2,1)S(1)} %collective-permute-done.18.r_1_, f32[288,256]{1,0:T(8,128)S(1)} %get-tuple-element.122.r_2_, bf16[288,256]{1,0:T(8,128)(2,1)S(1)} %collective-permute-done.19.r_3_, ...), custom_call_target="tpu_custom_call" | custom-call | flops 1 | bytes 1 | tf_op jit(solution)/shard_map/finish/pallas_call | solution.py:375
  (30 shorter events, 4.9 us)
Async XLA Ops:
  0.6 11.1 %collective-permute-start.1 = (bf16[96,512]{1,0:T(8,128)(2,1)}, bf16[96,512]{1,0:T(8,128)(2,1)S(1)}, u32[]{:S(2)}, u32[]{:S(2)}) collective-permute-start(bf16[96,512]{1,0:T(8,128)(2,1)} %r_4_.1), channel_id=1, source_target_pairs={{0,1},{1,0},{2,3},{3,2},{4,5},{5,4},{6,7},{7,6},{8,9},{9,8},{10,11... | collective-permute-start | bytes 294920 | tf_op jit(solution)/shard_map/ppermute | solution.py:351
  3.6 8.1 %collective-permute-start.3 = (bf16[96,512]{1,0:T(8,128)(2,1)}, bf16[96,512]{1,0:T(8,128)(2,1)S(1)}, u32[]{:S(2)}, u32[]{:S(2)}) collective-permute-start(bf16[96,512]{1,0:T(8,128)(2,1)} %r_4_.1), channel_id=1, source_target_pairs={{0,3},{1,2},{2,1},{3,0},{4,7},{5,6},{6,5},{7,4},{8,11},{9,10},{10,... | collective-permute-start | bytes 294920 | tf_op jit(solution)/shard_map/ppermute | solution.py:351
  5.1 6.6 %collective-permute-start.2 = (bf16[96,512]{1,0:T(8,128)(2,1)}, bf16[96,512]{1,0:T(8,128)(2,1)S(1)}, u32[]{:S(2)}, u32[]{:S(2)}) collective-permute-start(bf16[96,512]{1,0:T(8,128)(2,1)} %r_4_.1), channel_id=1, source_target_pairs={{0,2},{1,3},{2,0},{3,1},{4,6},{5,7},{6,4},{7,5},{8,10},{9,11},{10,... | collective-permute-start | bytes 294920 | tf_op jit(solution)/shard_map/ppermute | solution.py:351
  7.0 11.4 %collective-permute-start.5 = (bf16[296,256]{1,0:T(8,128)(2,1)S(1)}, bf16[296,256]{1,0:T(8,128)(2,1)S(1)}, u32[]{:S(2)}, u32[]{:S(2)}) collective-permute-start(bf16[296,256]{1,0:T(8,128)(2,1)S(1)} %get-tuple-element.64.r_0_), channel_id=1, source_target_pairs={{0,8},{4,12},{8,0},{12,4},{16,24},{20,28},{24,16},{28,20},{1,9},{5... | collective-permute-start | bytes 454664 | tf_op jit(solution)/shard_map/ppermute | solution.py:351
  9.1 9.3 %collective-permute-start.4 = (bf16[296,256]{1,0:T(8,128)(2,1)S(1)}, bf16[296,256]{1,0:T(8,128)(2,1)S(1)}, u32[]{:S(2)}, u32[]{:S(2)}) collective-permute-start(bf16[296,256]{1,0:T(8,128)(2,1)S(1)} %get-tuple-element.64.r_0_), channel_id=1, source_target_pairs={{0,16},{4,20},{8,24},{12,28},{16,0},{20,4},{24,8},{28,12},{1,17},{... | collective-permute-start | bytes 454664 | tf_op jit(solution)/shard_map/ppermute | solution.py:351
  11.7 7.9 %collective-permute-start = (bf16[296,256]{1,0:T(8,128)(2,1)S(1)}, bf16[296,256]{1,0:T(8,128)(2,1)S(1)}, u32[]{:S(2)}, u32[]{:S(2)}) collective-permute-start(bf16[296,256]{1,0:T(8,128)(2,1)S(1)} %get-tuple-element.64.r_0_), channel_id=1, source_target_pairs={{0,4},{4,0},{8,12},{12,8},{16,20},{20,16},{24,28},{28,24},{1,5},{5... | collective-permute-start | bytes 454664 | tf_op jit(solution)/shard_map/ppermute | solution.py:351
  18.4 4.0 %collective-permute-start.7 = (bf16[296,256]{1,0:T(8,128)(2,1)S(1)}, bf16[296,256]{1,0:T(8,128)(2,1)S(1)}, u32[]{:S(2)}, u32[]{:S(2)}) collective-permute-start(bf16[296,256]{1,0:T(8,128)(2,1)S(1)} %collective-permute-done.5.r_0_), channel_id=1, source_target_pairs={{0,4},{4,0},{8,12},{12,8},{16,20},{20,16},{24,28},{28,24},{1,5},{5... | collective-permute-start | bytes 454664 | tf_op jit(solution)/shard_map/ppermute | solution.py:351
  19.0 7.1 %collective-permute-start.8 = (bf16[296,256]{1,0:T(8,128)(2,1)S(1)}, bf16[296,256]{1,0:T(8,128)(2,1)S(1)}, u32[]{:S(2)}, u32[]{:S(2)}) collective-permute-start(bf16[296,256]{1,0:T(8,128)(2,1)S(1)} %collective-permute-done.4.r_0_), channel_id=1, source_target_pairs={{0,8},{4,12},{8,0},{12,4},{16,24},{20,28},{24,16},{28,20},{1,9},{5... | collective-permute-start | bytes 454664 | tf_op jit(solution)/shard_map/ppermute | solution.py:351
  22.2 4.3 %collective-permute-start.6 = (bf16[296,256]{1,0:T(8,128)(2,1)S(1)}, bf16[296,256]{1,0:T(8,128)(2,1)S(1)}, u32[]{:S(2)}, u32[]{:S(2)}) collective-permute-start(bf16[296,256]{1,0:T(8,128)(2,1)S(1)} %collective-permute-done.4.r_0_), channel_id=1, source_target_pairs={{0,4},{4,0},{8,12},{12,8},{16,20},{20,16},{24,28},{28,24},{1,5},{5... | collective-permute-start | bytes 454664 | tf_op jit(solution)/shard_map/ppermute | solution.py:351
  26.1 1.4 %collective-permute-start.9 = (bf16[296,256]{1,0:T(8,128)(2,1)S(1)}, bf16[296,256]{1,0:T(8,128)(2,1)S(1)}, u32[]{:S(2)}, u32[]{:S(2)}) collective-permute-start(bf16[296,256]{1,0:T(8,128)(2,1)S(1)} %collective-permute-done.8.r_2_), channel_id=1, source_target_pairs={{0,4},{4,0},{8,12},{12,8},{16,20},{20,16},{24,28},{28,24},{1,5},{5... | collective-permute-start | bytes 454664 | tf_op jit(solution)/shard_map/ppermute | solution.py:351
  33.7 4.6 %collective-permute-start.12 = (f32[8,128]{1,0:T(8,128)S(1)}, f32[8,128]{1,0:T(8,128)S(1)}, u32[]{:S(2)}, u32[]{:S(2)}) collective-permute-start(f32[8,128]{1,0:T(8,128)S(1)} %get-tuple-element.95.r_0_), channel_id=1, source_target_pairs={{0,3},{1,2},{2,1},{3,0},{4,7},{5,6},{6,5},{7,4},{8,11},{9,10},{10,... | collective-permute-start | bytes 12296 | tf_op jit(solution)/shard_map/ppermute | solution.py:351
  36.0 3.6 %collective-permute-start.11 = (f32[8,128]{1,0:T(8,128)S(1)}, f32[8,128]{1,0:T(8,128)S(1)}, u32[]{:S(2)}, u32[]{:S(2)}) collective-permute-start(f32[8,128]{1,0:T(8,128)S(1)} %get-tuple-element.95.r_0_), channel_id=1, source_target_pairs={{0,2},{1,3},{2,0},{3,1},{4,6},{5,7},{6,4},{7,5},{8,10},{9,11},{10,... | collective-permute-start | bytes 12296 | tf_op jit(solution)/shard_map/ppermute | solution.py:351
  36.6 3.6 %collective-permute-start.10 = (f32[8,128]{1,0:T(8,128)S(1)}, f32[8,128]{1,0:T(8,128)S(1)}, u32[]{:S(2)}, u32[]{:S(2)}) collective-permute-start(f32[8,128]{1,0:T(8,128)S(1)} %get-tuple-element.95.r_0_), channel_id=1, source_target_pairs={{0,1},{1,0},{2,3},{3,2},{4,5},{5,4},{6,7},{7,6},{8,9},{9,8},{10,11... | collective-permute-start | bytes 12296 | tf_op jit(solution)/shard_map/ppermute | solution.py:351
  44.4 3.1 %collective-permute-start.14 = (bf16[296,256]{1,0:T(8,128)(2,1)S(1)}, bf16[296,256]{1,0:T(8,128)(2,1)S(1)}, u32[]{:S(2)}, u32[]{:S(2)}) collective-permute-start(bf16[296,256]{1,0:T(8,128)(2,1)S(1)} %get-tuple-element.111), channel_id=1, source_target_pairs={{0,4},{4,0},{8,12},{12,8},{16,20},{20,16},{24,28},{28,24},{1,5},{5... | collective-permute-start | bytes 454664 | tf_op jit(solution)/shard_map/ppermute | solution.py:351
  46.9 2.1 %collective-permute-start.13 = (bf16[288,256]{1,0:T(8,128)(2,1)S(1)}, bf16[288,256]{1,0:T(8,128)(2,1)S(1)}, u32[]{:S(2)}, u32[]{:S(2)}) collective-permute-start(bf16[288,256]{1,0:T(8,128)(2,1)S(1)} %get-tuple-element.109), channel_id=1, source_target_pairs={{0,4},{4,0},{8,12},{12,8},{16,20},{20,16},{24,28},{28,24},{1,5},{5... | collective-permute-start | bytes 442376 | tf_op jit(solution)/shard_map/ppermute | solution.py:351
  47.6 5.9 %collective-permute-start.17 = (bf16[296,256]{1,0:T(8,128)(2,1)S(1)}, bf16[296,256]{1,0:T(8,128)(2,1)S(1)}, u32[]{:S(2)}, u32[]{:S(2)}) collective-permute-start(bf16[296,256]{1,0:T(8,128)(2,1)S(1)} %get-tuple-element.119), channel_id=1, source_target_pairs={{0,8},{4,12},{8,0},{12,4},{16,24},{20,28},{24,16},{28,20},{1,9},{5... | collective-permute-start | bytes 454664 | tf_op jit(solution)/shard_map/ppermute | solution.py:351
  51.7 1.4 %collective-permute-start.16 = (bf16[288,256]{1,0:T(8,128)(2,1)S(1)}, bf16[288,256]{1,0:T(8,128)(2,1)S(1)}, u32[]{:S(2)}, u32[]{:S(2)}) collective-permute-start(bf16[288,256]{1,0:T(8,128)(2,1)S(1)} %get-tuple-element.118), channel_id=1, source_target_pairs={{0,4},{4,0},{8,12},{12,8},{16,20},{20,16},{24,28},{28,24},{1,5},{5... | collective-permute-start | bytes 442376 | tf_op jit(solution)/shard_map/ppermute | solution.py:351
  51.7 9.0 %collective-permute-start.15 = (bf16[296,256]{1,0:T(8,128)(2,1)S(1)}, bf16[296,256]{1,0:T(8,128)(2,1)S(1)}, u32[]{:S(2)}, u32[]{:S(2)}) collective-permute-start(bf16[296,256]{1,0:T(8,128)(2,1)S(1)} %pair.2), channel_id=1, source_target_pairs={{0,8},{4,12},{8,0},{12,4},{16,24},{20,28},{24,16},{28,20},{1,9},{5... | collective-permute-start | bytes 454664 | tf_op jit(solution)/shard_map/ppermute | solution.py:351
  53.6 9.8 %collective-permute-start.18 = (bf16[296,256]{1,0:T(8,128)(2,1)S(1)}, bf16[296,256]{1,0:T(8,128)(2,1)S(1)}, u32[]{:S(2)}, u32[]{:S(2)}) collective-permute-start(bf16[296,256]{1,0:T(8,128)(2,1)S(1)} %pair.3), channel_id=1, source_target_pairs={{0,16},{4,20},{8,24},{12,28},{16,0},{20,4},{24,8},{28,12},{1,17},{... | collective-permute-start | bytes 454664 | tf_op jit(solution)/shard_map/ppermute | solution.py:351
  58.8 2.0 %collective-permute-start.19 = (bf16[288,256]{1,0:T(8,128)(2,1)S(1)}, bf16[288,256]{1,0:T(8,128)(2,1)S(1)}, u32[]{:S(2)}, u32[]{:S(2)}) collective-permute-start(bf16[288,256]{1,0:T(8,128)(2,1)S(1)} %get-tuple-element.123), channel_id=1, source_target_pairs={{0,4},{4,0},{8,12},{12,8},{16,20},{20,16},{24,28},{28,24},{1,5},{5... | collective-permute-start | bytes 442376 | tf_op jit(solution)/shard_map/ppermute | solution.py:351

commit v6 on v5

--- a/solution.py
+++ b/solution.py
@@ -72,7 +72,8 @@
     return jnp.concatenate(pieces, axis=1) if per > 1 else pieces[0]
 
 
-def begin_body(where, *refs, width):
+def begin_body(*refs, width):
+    place = lax.axis_index("dom")
     sources = refs[:4]
     message, cosine, sine, kept, x_ref, noise, tables, tall, tail, arrived = refs[4:]
     copies = [
@@ -82,7 +83,7 @@
     for copy in copies:
         copy.start()
     count = HALF // width
-    at = pl.multiple_of(jnp.bitwise_and(where[0], count - 1) * width, 128)
+    at = pl.multiple_of(jnp.bitwise_and(place, count - 1) * width, 128)
     h = x_ref.shape[0]
     copies[0].wait()
     copies[1].wait()
@@ -93,25 +94,27 @@
     row = column_to_row(half, tall.shape[0], tall)
     message[h : h + TAIL, :] = tail_block(row, width, tail)
     copies[2].wait()
-    sign = jnp.where(where[0] < count, 1.0, -1.0).astype(F32)
+    sign = jnp.where(place < count, 1.0, -1.0).astype(F32)
     for k in range(count):
-        at = pl.multiple_of(jnp.bitwise_and(jnp.bitwise_xor(where[0], k), count - 1) * width, 128)
+        at = pl.multiple_of(jnp.bitwise_and(jnp.bitwise_xor(place, k), count - 1) * width, 128)
         cosine[:, k * width : (k + 1) * width] = tables[0, :, pl.ds(at, width)]
         sine[:, k * width : (k + 1) * width] = tables[1, :, pl.ds(at, width)] * sign
     copies[3].wait()
 
 
-def shift_body(where, *refs, parts, pairs, width):
+def shift_body(*refs, parts, pairs, width):
     pieces = refs[:parts]
     cosine, sine = refs[parts : parts + 2]
     outs = refs[parts + 2 : parts + 2 + pairs]
     rest, plain, whole = refs[parts + 2 + pairs :]
     rows, part_width = pieces[0].shape
+    place = lax.axis_index("dom")
+    column = lax.axis_index("cls")
     for k in range(parts):
-        at = pl.multiple_of(jnp.bitwise_xor(where[2], k) * part_width, 128)
+        at = pl.multiple_of(jnp.bitwise_xor(column, k) * part_width, 128)
         plain[:, pl.ds(at, part_width)] = pieces[k][...].astype(F32)
     for k in range(2 * pairs):
-        at = pl.multiple_of(jnp.bitwise_xor(where[0], k) * width, 128)
+        at = pl.multiple_of(jnp.bitwise_xor(place, k) * width, 128)
         whole[:, k * width : (k + 1) * width] = plain[:, pl.ds(at, width)]
     rest[...] = whole[...].astype(BF16)
 
@@ -357,15 +360,12 @@
         length = -(-h // width) * width
         block = GROUP * rows
         shape = jax.ShapeDtypeStruct
-        place = lax.axis_index("dom")
-        where = jnp.stack([place, place % 2, lax.axis_index("cls")]).astype(jnp.int32)
 
         def call(body, shapes, name, scratch=(), limit=2, aliases=None, inputs=VMEM, flops=1):
             def run(*args):
-                scalars = args[0] is where
-                specs = [inputs] * (len(args) - scalars)
+                specs = [inputs] * len(args)
                 spec = pltpu.PrefetchScalarGridSpec(
-                    num_scalar_prefetch=int(scalars),
+                    num_scalar_prefetch=0,
                     grid=(),
                     in_specs=specs,
                     out_specs=[VMEM] * len(shapes),
@@ -404,7 +404,6 @@
             ],
             inputs=pl.BlockSpec(memory_space=pltpu.HBM),
         )(
-            where,
             *[
                 pltpu.with_memory_space_constraint(x, pltpu.HBM)
                 for x in (ref_rows, noise_weight.reshape(1, HALF), jnp.asarray(tables), particles)
@@ -424,7 +423,7 @@
             flops=10**10,
             limit=2,
             scratch=[pltpu.VMEM((rows, F), F32)] * 2,
-        )(where, *pieces, *angles)
+        )(*pieces, *angles)
 
         for k in range(1, pairs):
             if k & (k - 1):

time: 64.6 us -> 63.7 us (0.986)
  Pallas kernels: 33.6 us -> 32.5 us
    pallas_call x13, Pallas kernels: 33.6 us -> 32.5 us  [run(): pl.pallas_call(body, grid_spec=spec, out_shape=shapes, compiler_params=pa...]
  transfers between devices with their start and end apart: 20 -> 20, of which waited for: 8 -> 9; matrix products, arithmetic and copies ran while one was open for 0% -> 0% of each run, Pallas kernels for 35% -> 33%
where the time goes in v6:
time: 63.7 us; the launch traced here: 63.5 us
  Pallas kernels  32.5 us (51%)
  starting transfers between devices  20.7 us (32%)
  waiting for transfers between devices  9.57 us (15%)
  between operations  0.76 us (1%)
    pallas_call x13, Pallas kernels, run(): pl.pallas_call(body, grid_spec=spec, out_shape=shapes, compiler_params=pa...  32.5 us
    ppermute x20, starting transfers between devices, swap(): return lax.ppermute(x, axis, [(i, i ^ k) for i in range(size)])  20.7 us
    ppermute x20, waiting for transfers between devices, swap(): return lax.ppermute(x, axis, [(i, i ^ k) for i in range(size)])  9.57 us
  transfers between devices with their start and end apart: 20, of which 9 were waited for; matrix products, arithmetic and copies ran while one was open for 0% of the time, Pallas kernels for 33%

profile of v6, /device:TPU:0, one launch (start us, length us, event | category | flops | bytes accessed | tf_op | source)
XLA Modules:
  0.0 63.5 jit_solution(7639709257849951851)
XLA Ops:
  0.6 3.0 %collective-permute-start.1 = (bf16[96,512]{1,0:T(8,128)(2,1)}, bf16[96,512]{1,0:T(8,128)(2,1)S(1)}, u32[]{:S(2)}, u32[]{:S(2)}) collective-permute-start(bf16[96,512]{1,0:T(8,128)(2,1)} %r_3_.1), channel_id=1, source_target_pairs={{0,1},{1,0},{2,3},{3,2},{4,5},{5,4},{6,7},{7,6},{8,9},{9,8},{10,11... | collective-permute-start | bytes 294920 | tf_op jit(solution)/shard_map/ppermute | solution.py:354
  3.6 1.5 %collective-permute-start.3 = (bf16[96,512]{1,0:T(8,128)(2,1)}, bf16[96,512]{1,0:T(8,128)(2,1)S(1)}, u32[]{:S(2)}, u32[]{:S(2)}) collective-permute-start(bf16[96,512]{1,0:T(8,128)(2,1)} %r_3_.1), channel_id=1, source_target_pairs={{0,3},{1,2},{2,1},{3,0},{4,7},{5,6},{6,5},{7,4},{8,11},{9,10},{10,... | collective-permute-start | bytes 294920 | tf_op jit(solution)/shard_map/ppermute | solution.py:354
  5.2 1.2 %begin.1 = (bf16[296,256]{1,0:T(8,128)(2,1)S(1)}, f32[40,1024]{1,0:T(8,128)S(1)}, f32[40,1024]{1,0:T(8,128)S(1)}, bf16[96,512]{1,0:T(8,128)(2,1)S(1)}) custom-call(f32[288,256]{1,0:T(8,128)} %bitcast.7, f32[1,1024]{1,0:T(1,128)} %bitcast.8, f32[2,40,1024]{2,1,0:T(8,128)} %constant.2.clone.r_2_, bf16[96,512]{1,0:T(8,128)(2,1)} %r_3_.1), custom_call_target="tpu_custom_call" | custom-call | flops 1 | bytes 1 | tf_op jit(solution)/shard_map/begin/pallas_call | solution.py:375
  6.4 2.1 %collective-permute-start.5 = (bf16[296,256]{1,0:T(8,128)(2,1)S(1)}, bf16[296,256]{1,0:T(8,128)(2,1)S(1)}, u32[]{:S(2)}, u32[]{:S(2)}) collective-permute-start(bf16[296,256]{1,0:T(8,128)(2,1)S(1)} %get-tuple-element.64.r_0_), channel_id=1, source_target_pairs={{0,8},{4,12},{8,0},{12,4},{16,24},{20,28},{24,16},{28,20},{1,9},{5... | collective-permute-start | bytes 454664 | tf_op jit(solution)/shard_map/ppermute | solution.py:354
  8.5 2.6 %collective-permute-start.4 = (bf16[296,256]{1,0:T(8,128)(2,1)S(1)}, bf16[296,256]{1,0:T(8,128)(2,1)S(1)}, u32[]{:S(2)}, u32[]{:S(2)}) collective-permute-start(bf16[296,256]{1,0:T(8,128)(2,1)S(1)} %get-tuple-element.64.r_0_), channel_id=1, source_target_pairs={{0,16},{4,20},{8,24},{12,28},{16,0},{20,4},{24,8},{28,12},{1,17},{... | collective-permute-start | bytes 454664 | tf_op jit(solution)/shard_map/ppermute | solution.py:354
  11.3 6.1 %shift.1 = (bf16[7680,512]{1,0:T(8,128)(2,1)S(1)}, bf16[7680,512]{1,0:T(8,128)(2,1)S(1)}, bf16[7680,512]{1,0:T(8,128)(2,1)S(1)}, bf16[7680,512]{1,0:T(8,128)(2,1)S(1)}, bf16[96,2048]{1,0:T(8,128)(2,1)S(1)}) custom-call(bf16[96,512]{1,0:T(8,128)(2,1)S(1)} %get-tuple-element.65.r_0_, bf16[96,512]{1,0:T(8,128)(2,1)S(1)} %collective-permute-done.1.r_1_, ...), custom_call_target="tpu_custom_call" | custom-call | flops 10000000000 | bytes 1 | tf_op jit(solution)/shard_map/shift/pallas_call | solution.py:375
  17.8 1.3 %collective-permute-start.8 = (bf16[296,256]{1,0:T(8,128)(2,1)S(1)}, bf16[296,256]{1,0:T(8,128)(2,1)S(1)}, u32[]{:S(2)}, u32[]{:S(2)}) collective-permute-start(bf16[296,256]{1,0:T(8,128)(2,1)S(1)} %collective-permute-done.4.r_0_), channel_id=1, source_target_pairs={{0,8},{4,12},{8,0},{12,4},{16,24},{20,28},{24,16},{28,20},{1,9},{5... | collective-permute-start | bytes 454664 | tf_op jit(solution)/shard_map/ppermute | solution.py:354
  19.1 2.5 %score.3 = (f32[10,288,768]{2,1,0:T(8,128)S(1)}, f32[288,96]{1,0:T(8,128)S(1)}, f32[8,512]{1,0:T(8,128)S(1)}, bf16[7680,512]{1,0:T(8,128)(2,1)S(1)}, bf16[7680,5...) custom-call(bf16[296,256]{1,0:T(8,128)(2,1)S(1)} %get-tuple-element., ...), custom_call_target="tpu_custom_call", output_to_operand_aliasing={{3}: (2, {}), {4}: (4, {}), {5}: (5, {}), {6}: (6, {})} | custom-call | flops 1 | bytes 1 | tf_op jit(solution)/shard_map/score/pallas_call | solution.py:375
  21.9 3.6 %score.4 = (f32[10,288,768]{2,1,0:T(8,128)S(1)}, f32[288,96]{1,0:T(8,128)S(1)}, f32[8,512]{1,0:T(8,128)S(1)}, bf16[7680,512]{1,0:T(8,128)(2,1)S(1)}, bf16[7680,5...) custom-call(bf16[296,256]{1,0:T(8,128)(2,1)S(1)} %collective-permute, ...), custom_call_target="tpu_custom_call", output_to_operand_aliasing={{4}: (2, {}), {3}: (7, {}), {5}: (8, {}), {6}: (9, {}), {0}... | custom-call | flops 1 | bytes 1 | tf_op jit(solution)/shard_map/score/pallas_call | solution.py:375
  25.9 1.0 %collective-permute-done.9.r_3_ = bf16[296,256]{1,0:T(8,128)(2,1)S(1)} collective-permute-done((bf16[296,256]{1,0:T(8,128)(2,1)S(1)}, bf16[296,256]{1,0:T(8,128)(2,1)S(1)}, u32[]{:S(2)}, u32[]{:S(2)}) %collective-permute-start.9) | collective-permute-done | bytes 151584 | tf_op jit(solution)/shard_map/ppermute | solution.py:354
  27.0 6.2 %score.5 = (f32[10,288,768]{2,1,0:T(8,128)S(1)}, f32[288,96]{1,0:T(8,128)S(1)}, f32[11,8,768]{2,1,0:T(8,128)S(1)}, f32[8,128]{1,0:T(8,128)S(1)}, bf16[7680,512]{...) custom-call(bf16[296,256]{1,0:T(8,128)(2,1)S(1)} %collective-permute, ...), custom_call_target="tpu_custom_call", output_to_operand_aliasing={{6}: (4, {}), {7}: (5, {}), {4}: (10, {}), {5}: (11, {}), {... | custom-call | flops 1 | bytes 1 | tf_op jit(solution)/shard_map/score/pallas_call | solution.py:375
  33.1 1.7 %collective-permute-start.12 = (f32[8,128]{1,0:T(8,128)S(1)}, f32[8,128]{1,0:T(8,128)S(1)}, u32[]{:S(2)}, u32[]{:S(2)}) collective-permute-start(f32[8,128]{1,0:T(8,128)S(1)} %get-tuple-element.95.r_0_), channel_id=1, source_target_pairs={{0,3},{1,2},{2,1},{3,0},{4,7},{5,6},{6,5},{7,4},{8,11},{9,10},{10,... | collective-permute-start | bytes 12296 | tf_op jit(solution)/shard_map/ppermute | solution.py:354
  34.8 1.2 %collective-permute-start.11 = (f32[8,128]{1,0:T(8,128)S(1)}, f32[8,128]{1,0:T(8,128)S(1)}, u32[]{:S(2)}, u32[]{:S(2)}) collective-permute-start(f32[8,128]{1,0:T(8,128)S(1)} %get-tuple-element.95.r_0_), channel_id=1, source_target_pairs={{0,2},{1,3},{2,0},{3,1},{4,6},{5,7},{6,4},{7,5},{8,10},{9,11},{10,... | collective-permute-start | bytes 12296 | tf_op jit(solution)/shard_map/ppermute | solution.py:354
  36.7 1.0 %collective-permute-done.12.r_3_ = f32[8,128]{1,0:T(8,128)S(1)} collective-permute-done((f32[8,128]{1,0:T(8,128)S(1)}, f32[8,128]{1,0:T(8,128)S(1)}, u32[]{:S(2)}, u32[]{:S(2)}) %collective-permute-start.12) | collective-permute-done | bytes 4128 | tf_op jit(solution)/shard_map/ppermute | solution.py:354
  38.4 1.2 %collective-permute-done.10.r_1_ = f32[8,128]{1,0:T(8,128)S(1)} collective-permute-done((f32[8,128]{1,0:T(8,128)S(1)}, f32[8,128]{1,0:T(8,128)S(1)}, u32[]{:S(2)}, u32[]{:S(2)}) %collective-permute-start.10) | collective-permute-done | bytes 4128 | tf_op jit(solution)/shard_map/ppermute | solution.py:354
  39.7 4.1 %sums_first.1 = (bf16[10,288,768]{2,1,0:T(8,128)(2,1)S(1)}, bf16[288,96]{1,0:T(8,128)(2,1)S(1)}, f32[288,256]{1,0:T(8,128)S(1)}, bf16[296,256]{1,0:T(8,128)(2,1)...) custom-call(f32[8,128]{1,0:T(8,128)S(1)} %get-tuple-element.95.r_0_,, ...), custom_call_target="tpu_custom_call", output_to_operand_aliasing={{5}: (9, {}), {6}: (10, {}), {7}: (11, {})} | custom-call | flops 1 | bytes 1 | tf_op jit(solution)/shard_map/sums_first/pallas_call | solution.py:375
  43.9 2.5 %sums.3 = (f32[288,256]{1,0:T(8,128)S(1)}, bf16[288,256]{1,0:T(8,128)(2,1)S(1)}, bf16[7680,512]{1,0:T(8,128)(2,1)S(1)}, bf16[7680,512]{1,0:T(8,128)(2,1)S(1)}) custom-call(bf16[10,288,768]{2,1,0:T(8,128)(2,1)S(1)} %get-tuple-element.103.r_0_, bf16[288,96]{1,0:T(8,128)(2,1)S(1)} %get-tuple-element.120.r_1_, ...), custom_call_target="tpu_custom_call", output_to_operand_aliasing={{2}: (4, {}), {3}: (5, {})} | custom-call | flops 1 | bytes 1 | tf_op jit(solution)/shard_map/sums/pallas_call | solution.py:375
  48.0 2.5 %sums.4 = (f32[288,256]{1,0:T(8,128)S(1)}, bf16[288,256]{1,0:T(8,128)(2,1)S(1)}, bf16[7680,512]{1,0:T(8,128)(2,1)S(1)}) custom-call(bf16[10,288,768]{2,1,0:T(8,128)(2,1)S(1)} %get-tuple-element.103.r_0_, bf16[288,96]{1,0:T(8,128)(2,1)S(1)} %get-tuple-element.120.r_1_, ...), custom_call_target="tpu_custom_call", output_to_operand_aliasing={{2}: (4, {})} | custom-call | flops 1 | bytes 1 | tf_op jit(solution)/shard_map/sums/pallas_call | solution.py:375
  52.0 1.0 %collective-permute-done.17.refs_0_ = bf16[296,256]{1,0:T(8,128)(2,1)S(1)} collective-permute-done((bf16[296,256]{1,0:T(8,128)(2,1)S(1)}, bf16[296,256]{1,0:T(8,128)(2,1)S(1)}, u32[]{:S(2)}, u32[]{:S(2)}) %collective-permute-start.17) | collective-permute-done | bytes 151584 | tf_op jit(solution)/shard_map/ppermute | solution.py:354
  53.1 2.7 %collective-permute-start.18 = (bf16[296,256]{1,0:T(8,128)(2,1)S(1)}, bf16[296,256]{1,0:T(8,128)(2,1)S(1)}, u32[]{:S(2)}, u32[]{:S(2)}) collective-permute-start(bf16[296,256]{1,0:T(8,128)(2,1)S(1)} %pair.3), channel_id=1, source_target_pairs={{0,16},{4,20},{8,24},{12,28},{16,0},{20,4},{24,8},{28,12},{1,17},{... | collective-permute-start | bytes 454664 | tf_op jit(solution)/shard_map/ppermute | solution.py:354
  55.7 2.5 %sums.5 = (f32[288,256]{1,0:T(8,128)S(1)}, bf16[288,256]{1,0:T(8,128)(2,1)S(1)}) custom-call(bf16[10,288,768]{2,1,0:T(8,128)(2,1)S(1)} %get-tuple-element.103.r_0_, bf16[288,96]{1,0:T(8,128)(2,1)S(1)} %get-tuple-element.120.r_1_, bf16[7680,512]{1,0:T(8,128)(2,1)S(1)} %get-tuple-element.121.r_2_, bf16[96,2048]{1,0:T(8,128)(2,1)S(1)} %get-tuple-element.71.r_3_.r_6_.r_8_), custom_call_target="tpu_custom_call" | custom-call | flops 1 | bytes 1 | tf_op jit(solution)/shard_map/sums/pallas_call | solution.py:375
  58.3 1.7 %collective-permute-done.15.r_0_ = bf16[296,256]{1,0:T(8,128)(2,1)S(1)} collective-permute-done((bf16[296,256]{1,0:T(8,128)(2,1)S(1)}, bf16[296,256]{1,0:T(8,128)(2,1)S(1)}, u32[]{:S(2)}, u32[]{:S(2)}) %collective-permute-start.15) | collective-permute-done | bytes 151584 | tf_op jit(solution)/shard_map/ppermute | solution.py:354
  60.0 2.5 %collective-permute-done.18.r_1_ = bf16[296,256]{1,0:T(8,128)(2,1)S(1)} collective-permute-done((bf16[296,256]{1,0:T(8,128)(2,1)S(1)}, bf16[296,256]{1,0:T(8,128)(2,1)S(1)}, u32[]{:S(2)}, u32[]{:S(2)}) %collective-permute-start.18) | collective-permute-done | bytes 151584 | tf_op jit(solution)/shard_map/ppermute | solution.py:354
  62.5 1.0 %finish.1 = (f32[288,256]{1,0:T(8,128)}, f32[8,36]{1,0:T(8,128)}) custom-call(bf16[296,256]{1,0:T(8,128)(2,1)S(1)} %collective-permute-done.15.r_0_, bf16[296,256]{1,0:T(8,128)(2,1)S(1)} %collective-permute-done.18.r_1_, f32[288,256]{1,0:T(8,128)S(1)} %get-tuple-element.122.r_2_, bf16[288,256]{1,0:T(8,128)(2,1)S(1)} %collective-permute-done.19.r_3_, ...), custom_call_target="tpu_custom_call" | custom-call | flops 1 | bytes 1 | tf_op jit(solution)/shard_map/finish/pallas_call | solution.py:375
  (29 shorter events, 6.0 us)
Async XLA Ops:
  0.6 10.5 %collective-permute-start.1 = (bf16[96,512]{1,0:T(8,128)(2,1)}, bf16[96,512]{1,0:T(8,128)(2,1)S(1)}, u32[]{:S(2)}, u32[]{:S(2)}) collective-permute-start(bf16[96,512]{1,0:T(8,128)(2,1)} %r_3_.1), channel_id=1, source_target_pairs={{0,1},{1,0},{2,3},{3,2},{4,5},{5,4},{6,7},{7,6},{8,9},{9,8},{10,11... | collective-permute-start | bytes 294920 | tf_op jit(solution)/shard_map/ppermute | solution.py:354
  3.6 7.5 %collective-permute-start.3 = (bf16[96,512]{1,0:T(8,128)(2,1)}, bf16[96,512]{1,0:T(8,128)(2,1)S(1)}, u32[]{:S(2)}, u32[]{:S(2)}) collective-permute-start(bf16[96,512]{1,0:T(8,128)(2,1)} %r_3_.1), channel_id=1, source_target_pairs={{0,3},{1,2},{2,1},{3,0},{4,7},{5,6},{6,5},{7,4},{8,11},{9,10},{10,... | collective-permute-start | bytes 294920 | tf_op jit(solution)/shard_map/ppermute | solution.py:354
  5.1 6.1 %collective-permute-start.2 = (bf16[96,512]{1,0:T(8,128)(2,1)}, bf16[96,512]{1,0:T(8,128)(2,1)S(1)}, u32[]{:S(2)}, u32[]{:S(2)}) collective-permute-start(bf16[96,512]{1,0:T(8,128)(2,1)} %r_3_.1), channel_id=1, source_target_pairs={{0,2},{1,3},{2,0},{3,1},{4,6},{5,7},{6,4},{7,5},{8,10},{9,11},{10,... | collective-permute-start | bytes 294920 | tf_op jit(solution)/shard_map/ppermute | solution.py:354
  6.4 11.0 %collective-permute-start.5 = (bf16[296,256]{1,0:T(8,128)(2,1)S(1)}, bf16[296,256]{1,0:T(8,128)(2,1)S(1)}, u32[]{:S(2)}, u32[]{:S(2)}) collective-permute-start(bf16[296,256]{1,0:T(8,128)(2,1)S(1)} %get-tuple-element.64.r_0_), channel_id=1, source_target_pairs={{0,8},{4,12},{8,0},{12,4},{16,24},{20,28},{24,16},{28,20},{1,9},{5... | collective-permute-start | bytes 454664 | tf_op jit(solution)/shard_map/ppermute | solution.py:354
  8.5 8.9 %collective-permute-start.4 = (bf16[296,256]{1,0:T(8,128)(2,1)S(1)}, bf16[296,256]{1,0:T(8,128)(2,1)S(1)}, u32[]{:S(2)}, u32[]{:S(2)}) collective-permute-start(bf16[296,256]{1,0:T(8,128)(2,1)S(1)} %get-tuple-element.64.r_0_), channel_id=1, source_target_pairs={{0,16},{4,20},{8,24},{12,28},{16,0},{20,4},{24,8},{28,12},{1,17},{... | collective-permute-start | bytes 454664 | tf_op jit(solution)/shard_map/ppermute | solution.py:354
  11.1 8.0 %collective-permute-start = (bf16[296,256]{1,0:T(8,128)(2,1)S(1)}, bf16[296,256]{1,0:T(8,128)(2,1)S(1)}, u32[]{:S(2)}, u32[]{:S(2)}) collective-permute-start(bf16[296,256]{1,0:T(8,128)(2,1)S(1)} %get-tuple-element.64.r_0_), channel_id=1, source_target_pairs={{0,4},{4,0},{8,12},{12,8},{16,20},{20,16},{24,28},{28,24},{1,5},{5... | collective-permute-start | bytes 454664 | tf_op jit(solution)/shard_map/ppermute | solution.py:354
  17.4 4.5 %collective-permute-start.7 = (bf16[296,256]{1,0:T(8,128)(2,1)S(1)}, bf16[296,256]{1,0:T(8,128)(2,1)S(1)}, u32[]{:S(2)}, u32[]{:S(2)}) collective-permute-start(bf16[296,256]{1,0:T(8,128)(2,1)S(1)} %collective-permute-done.5.r_0_), channel_id=1, source_target_pairs={{0,4},{4,0},{8,12},{12,8},{16,20},{20,16},{24,28},{28,24},{1,5},{5... | collective-permute-start | bytes 454664 | tf_op jit(solution)/shard_map/ppermute | solution.py:354
  17.8 7.7 %collective-permute-start.8 = (bf16[296,256]{1,0:T(8,128)(2,1)S(1)}, bf16[296,256]{1,0:T(8,128)(2,1)S(1)}, u32[]{:S(2)}, u32[]{:S(2)}) collective-permute-start(bf16[296,256]{1,0:T(8,128)(2,1)S(1)} %collective-permute-done.4.r_0_), channel_id=1, source_target_pairs={{0,8},{4,12},{8,0},{12,4},{16,24},{20,28},{24,16},{28,20},{1,9},{5... | collective-permute-start | bytes 454664 | tf_op jit(solution)/shard_map/ppermute | solution.py:354
  21.6 4.3 %collective-permute-start.6 = (bf16[296,256]{1,0:T(8,128)(2,1)S(1)}, bf16[296,256]{1,0:T(8,128)(2,1)S(1)}, u32[]{:S(2)}, u32[]{:S(2)}) collective-permute-start(bf16[296,256]{1,0:T(8,128)(2,1)S(1)} %collective-permute-done.4.r_0_), channel_id=1, source_target_pairs={{0,4},{4,0},{8,12},{12,8},{16,20},{20,16},{24,28},{28,24},{1,5},{5... | collective-permute-start | bytes 454664 | tf_op jit(solution)/shard_map/ppermute | solution.py:354
  25.5 1.4 %collective-permute-start.9 = (bf16[296,256]{1,0:T(8,128)(2,1)S(1)}, bf16[296,256]{1,0:T(8,128)(2,1)S(1)}, u32[]{:S(2)}, u32[]{:S(2)}) collective-permute-start(bf16[296,256]{1,0:T(8,128)(2,1)S(1)} %collective-permute-done.8.r_2_), channel_id=1, source_target_pairs={{0,4},{4,0},{8,12},{12,8},{16,20},{20,16},{24,28},{28,24},{1,5},{5... | collective-permute-start | bytes 454664 | tf_op jit(solution)/shard_map/ppermute | solution.py:354
  33.1 4.6 %collective-permute-start.12 = (f32[8,128]{1,0:T(8,128)S(1)}, f32[8,128]{1,0:T(8,128)S(1)}, u32[]{:S(2)}, u32[]{:S(2)}) collective-permute-start(f32[8,128]{1,0:T(8,128)S(1)} %get-tuple-element.95.r_0_), channel_id=1, source_target_pairs={{0,3},{1,2},{2,1},{3,0},{4,7},{5,6},{6,5},{7,4},{8,11},{9,10},{10,... | collective-permute-start | bytes 12296 | tf_op jit(solution)/shard_map/ppermute | solution.py:354
  34.8 3.6 %collective-permute-start.11 = (f32[8,128]{1,0:T(8,128)S(1)}, f32[8,128]{1,0:T(8,128)S(1)}, u32[]{:S(2)}, u32[]{:S(2)}) collective-permute-start(f32[8,128]{1,0:T(8,128)S(1)} %get-tuple-element.95.r_0_), channel_id=1, source_target_pairs={{0,2},{1,3},{2,0},{3,1},{4,6},{5,7},{6,4},{7,5},{8,10},{9,11},{10,... | collective-permute-start | bytes 12296 | tf_op jit(solution)/shard_map/ppermute | solution.py:354
  36.1 3.6 %collective-permute-start.10 = (f32[8,128]{1,0:T(8,128)S(1)}, f32[8,128]{1,0:T(8,128)S(1)}, u32[]{:S(2)}, u32[]{:S(2)}) collective-permute-start(f32[8,128]{1,0:T(8,128)S(1)} %get-tuple-element.95.r_0_), channel_id=1, source_target_pairs={{0,1},{1,0},{2,3},{3,2},{4,5},{5,4},{6,7},{7,6},{8,9},{9,8},{10,11... | collective-permute-start | bytes 12296 | tf_op jit(solution)/shard_map/ppermute | solution.py:354
  43.8 3.1 %collective-permute-start.14 = (bf16[296,256]{1,0:T(8,128)(2,1)S(1)}, bf16[296,256]{1,0:T(8,128)(2,1)S(1)}, u32[]{:S(2)}, u32[]{:S(2)}) collective-permute-start(bf16[296,256]{1,0:T(8,128)(2,1)S(1)} %get-tuple-element.111), channel_id=1, source_target_pairs={{0,4},{4,0},{8,12},{12,8},{16,20},{20,16},{24,28},{28,24},{1,5},{5... | collective-permute-start | bytes 454664 | tf_op jit(solution)/shard_map/ppermute | solution.py:354
  46.4 1.6 %collective-permute-start.13 = (bf16[288,256]{1,0:T(8,128)(2,1)S(1)}, bf16[288,256]{1,0:T(8,128)(2,1)S(1)}, u32[]{:S(2)}, u32[]{:S(2)}) collective-permute-start(bf16[288,256]{1,0:T(8,128)(2,1)S(1)} %get-tuple-element.109), channel_id=1, source_target_pairs={{0,4},{4,0},{8,12},{12,8},{16,20},{20,16},{24,28},{28,24},{1,5},{5... | collective-permute-start | bytes 442376 | tf_op jit(solution)/shard_map/ppermute | solution.py:354
  47.0 5.9 %collective-permute-start.17 = (bf16[296,256]{1,0:T(8,128)(2,1)S(1)}, bf16[296,256]{1,0:T(8,128)(2,1)S(1)}, u32[]{:S(2)}, u32[]{:S(2)}) collective-permute-start(bf16[296,256]{1,0:T(8,128)(2,1)S(1)} %get-tuple-element.119), channel_id=1, source_target_pairs={{0,8},{4,12},{8,0},{12,4},{16,24},{20,28},{24,16},{28,20},{1,9},{5... | collective-permute-start | bytes 454664 | tf_op jit(solution)/shard_map/ppermute | solution.py:354
  50.5 1.4 %collective-permute-start.16 = (bf16[288,256]{1,0:T(8,128)(2,1)S(1)}, bf16[288,256]{1,0:T(8,128)(2,1)S(1)}, u32[]{:S(2)}, u32[]{:S(2)}) collective-permute-start(bf16[288,256]{1,0:T(8,128)(2,1)S(1)} %get-tuple-element.118), channel_id=1, source_target_pairs={{0,4},{4,0},{8,12},{12,8},{16,20},{20,16},{24,28},{28,24},{1,5},{5... | collective-permute-start | bytes 442376 | tf_op jit(solution)/shard_map/ppermute | solution.py:354
  51.0 9.0 %collective-permute-start.15 = (bf16[296,256]{1,0:T(8,128)(2,1)S(1)}, bf16[296,256]{1,0:T(8,128)(2,1)S(1)}, u32[]{:S(2)}, u32[]{:S(2)}) collective-permute-start(bf16[296,256]{1,0:T(8,128)(2,1)S(1)} %pair.2), channel_id=1, source_target_pairs={{0,8},{4,12},{8,0},{12,4},{16,24},{20,28},{24,16},{28,20},{1,9},{5... | collective-permute-start | bytes 454664 | tf_op jit(solution)/shard_map/ppermute | solution.py:354
  53.1 9.5 %collective-permute-start.18 = (bf16[296,256]{1,0:T(8,128)(2,1)S(1)}, bf16[296,256]{1,0:T(8,128)(2,1)S(1)}, u32[]{:S(2)}, u32[]{:S(2)}) collective-permute-start(bf16[296,256]{1,0:T(8,128)(2,1)S(1)} %pair.3), channel_id=1, source_target_pairs={{0,16},{4,20},{8,24},{12,28},{16,0},{20,4},{24,8},{28,12},{1,17},{... | collective-permute-start | bytes 454664 | tf_op jit(solution)/shard_map/ppermute | solution.py:354
  58.2 1.8 %collective-permute-start.19 = (bf16[288,256]{1,0:T(8,128)(2,1)S(1)}, bf16[288,256]{1,0:T(8,128)(2,1)S(1)}, u32[]{:S(2)}, u32[]{:S(2)}) collective-permute-start(bf16[288,256]{1,0:T(8,128)(2,1)S(1)} %get-tuple-element.123), channel_id=1, source_target_pairs={{0,4},{4,0},{8,12},{12,8},{16,20},{20,16},{24,28},{28,24},{1,5},{5... | collective-permute-start | bytes 442376 | tf_op jit(solution)/shard_map/ppermute | solution.py:354

commit v7 on v6

--- a/solution.py
+++ b/solution.py
@@ -330,18 +330,16 @@
     shape = (classes, length)
     at = lax.broadcasted_iota(jnp.int32, shape, 1)
     mine = at - at // classes * classes == lax.broadcasted_iota(jnp.int32, shape, 0)
-    spread_out = jnp.where(mine, jnp.broadcast_to(row, shape), 0.0)
-    shape = (length, rotations)
-    pick = lax.broadcasted_iota(jnp.int32, shape, 0) // classes == lax.broadcasted_iota(
-        jnp.int32, shape, 1
-    )
-    class_weight[...] = lax.dot_general(
-        spread_out,
-        pick.astype(F32),
-        (((1,), (0,)), ((), ())),
-        precision=lax.Precision.HIGHEST,
-        preferred_element_type=F32,
-    )
+    pick = lax.broadcasted_iota(jnp.int32, (length, rotations), 0) // classes
+    pick = pick == lax.broadcasted_iota(jnp.int32, (length, rotations), 1)
+    pick = pick.astype(F32).astype(BF16)
+    high, mid, low = [
+        contract(
+            jnp.where(mine, jnp.broadcast_to(part, shape), 0.0).astype(BF16), pick, ((1,), (0,))
+        )
+        for part in spread(row)
+    ]
+    class_weight[...] = (low + mid) + high
 
 
 VMEM = pl.BlockSpec(memory_space=pltpu.VMEM)

time: 63.7 us -> 63.6 us (level)
  no operation moved by 1% of the time
where the time goes in v7:
time: 63.6 us; the launch traced here: 63.5 us
  Pallas kernels  32.4 us (51%)
  starting transfers between devices  20.7 us (33%)
  waiting for transfers between devices  9.57 us (15%)
  between operations  0.76 us (1%)
    pallas_call x13, Pallas kernels, run(): pl.pallas_call(body, grid_spec=spec, out_shape=shapes, compiler_params=pa...  32.4 us
    ppermute x20, starting transfers between devices, swap(): return lax.ppermute(x, axis, [(i, i ^ k) for i in range(size)])  20.7 us
    ppermute x20, waiting for transfers between devices, swap(): return lax.ppermute(x, axis, [(i, i ^ k) for i in range(size)])  9.57 us
  transfers between devices with their start and end apart: 20, of which 9 were waited for; matrix products, arithmetic and copies ran while one was open for 0% of the time, Pallas kernels for 33%

profile of v7, /device:TPU:0, one launch (start us, length us, event | category | flops | bytes accessed | tf_op | source)
XLA Modules:
  0.0 63.5 jit_solution(13969316901452164885)
XLA Ops:
  0.6 3.0 %collective-permute-start.1 = (bf16[96,512]{1,0:T(8,128)(2,1)}, bf16[96,512]{1,0:T(8,128)(2,1)S(1)}, u32[]{:S(2)}, u32[]{:S(2)}) collective-permute-start(bf16[96,512]{1,0:T(8,128)(2,1)} %r_3_.1), channel_id=1, source_target_pairs={{0,1},{1,0},{2,3},{3,2},{4,5},{5,4},{6,7},{7,6},{8,9},{9,8},{10,11... | collective-permute-start | bytes 294920 | tf_op jit(solution)/shard_map/ppermute | solution.py:352
  3.6 1.5 %collective-permute-start.3 = (bf16[96,512]{1,0:T(8,128)(2,1)}, bf16[96,512]{1,0:T(8,128)(2,1)S(1)}, u32[]{:S(2)}, u32[]{:S(2)}) collective-permute-start(bf16[96,512]{1,0:T(8,128)(2,1)} %r_3_.1), channel_id=1, source_target_pairs={{0,3},{1,2},{2,1},{3,0},{4,7},{5,6},{6,5},{7,4},{8,11},{9,10},{10,... | collective-permute-start | bytes 294920 | tf_op jit(solution)/shard_map/ppermute | solution.py:352
  5.2 1.2 %begin.1 = (bf16[296,256]{1,0:T(8,128)(2,1)S(1)}, f32[40,1024]{1,0:T(8,128)S(1)}, f32[40,1024]{1,0:T(8,128)S(1)}, bf16[96,512]{1,0:T(8,128)(2,1)S(1)}) custom-call(f32[288,256]{1,0:T(8,128)} %bitcast.7, f32[1,1024]{1,0:T(1,128)} %bitcast.8, f32[2,40,1024]{2,1,0:T(8,128)} %constant.2.clone.r_2_, bf16[96,512]{1,0:T(8,128)(2,1)} %r_3_.1), custom_call_target="tpu_custom_call" | custom-call | flops 1 | bytes 1 | tf_op jit(solution)/shard_map/begin/pallas_call | solution.py:373
  6.4 2.1 %collective-permute-start.5 = (bf16[296,256]{1,0:T(8,128)(2,1)S(1)}, bf16[296,256]{1,0:T(8,128)(2,1)S(1)}, u32[]{:S(2)}, u32[]{:S(2)}) collective-permute-start(bf16[296,256]{1,0:T(8,128)(2,1)S(1)} %get-tuple-element.64.r_0_), channel_id=1, source_target_pairs={{0,8},{4,12},{8,0},{12,4},{16,24},{20,28},{24,16},{28,20},{1,9},{5... | collective-permute-start | bytes 454664 | tf_op jit(solution)/shard_map/ppermute | solution.py:352
  8.5 2.6 %collective-permute-start.4 = (bf16[296,256]{1,0:T(8,128)(2,1)S(1)}, bf16[296,256]{1,0:T(8,128)(2,1)S(1)}, u32[]{:S(2)}, u32[]{:S(2)}) collective-permute-start(bf16[296,256]{1,0:T(8,128)(2,1)S(1)} %get-tuple-element.64.r_0_), channel_id=1, source_target_pairs={{0,16},{4,20},{8,24},{12,28},{16,0},{20,4},{24,8},{28,12},{1,17},{... | collective-permute-start | bytes 454664 | tf_op jit(solution)/shard_map/ppermute | solution.py:352
  11.3 6.1 %shift.1 = (bf16[7680,512]{1,0:T(8,128)(2,1)S(1)}, bf16[7680,512]{1,0:T(8,128)(2,1)S(1)}, bf16[7680,512]{1,0:T(8,128)(2,1)S(1)}, bf16[7680,512]{1,0:T(8,128)(2,1)S(1)}, bf16[96,2048]{1,0:T(8,128)(2,1)S(1)}) custom-call(bf16[96,512]{1,0:T(8,128)(2,1)S(1)} %get-tuple-element.65.r_0_, bf16[96,512]{1,0:T(8,128)(2,1)S(1)} %collective-permute-done.1.r_1_, ...), custom_call_target="tpu_custom_call" | custom-call | flops 10000000000 | bytes 1 | tf_op jit(solution)/shard_map/shift/pallas_call | solution.py:373
  17.8 1.3 %collective-permute-start.8 = (bf16[296,256]{1,0:T(8,128)(2,1)S(1)}, bf16[296,256]{1,0:T(8,128)(2,1)S(1)}, u32[]{:S(2)}, u32[]{:S(2)}) collective-permute-start(bf16[296,256]{1,0:T(8,128)(2,1)S(1)} %collective-permute-done.4.r_0_), channel_id=1, source_target_pairs={{0,8},{4,12},{8,0},{12,4},{16,24},{20,28},{24,16},{28,20},{1,9},{5... | collective-permute-start | bytes 454664 | tf_op jit(solution)/shard_map/ppermute | solution.py:352
  19.1 2.5 %score.3 = (f32[10,288,768]{2,1,0:T(8,128)S(1)}, f32[288,96]{1,0:T(8,128)S(1)}, f32[8,512]{1,0:T(8,128)S(1)}, bf16[7680,512]{1,0:T(8,128)(2,1)S(1)}, bf16[7680,5...) custom-call(bf16[296,256]{1,0:T(8,128)(2,1)S(1)} %get-tuple-element., ...), custom_call_target="tpu_custom_call", output_to_operand_aliasing={{3}: (2, {}), {4}: (4, {}), {5}: (5, {}), {6}: (6, {})} | custom-call | flops 1 | bytes 1 | tf_op jit(solution)/shard_map/score/pallas_call | solution.py:373
  21.9 3.6 %score.4 = (f32[10,288,768]{2,1,0:T(8,128)S(1)}, f32[288,96]{1,0:T(8,128)S(1)}, f32[8,512]{1,0:T(8,128)S(1)}, bf16[7680,512]{1,0:T(8,128)(2,1)S(1)}, bf16[7680,5...) custom-call(bf16[296,256]{1,0:T(8,128)(2,1)S(1)} %collective-permute, ...), custom_call_target="tpu_custom_call", output_to_operand_aliasing={{4}: (2, {}), {3}: (7, {}), {5}: (8, {}), {6}: (9, {}), {0}... | custom-call | flops 1 | bytes 1 | tf_op jit(solution)/shard_map/score/pallas_call | solution.py:373
  25.9 1.0 %collective-permute-done.9.r_3_ = bf16[296,256]{1,0:T(8,128)(2,1)S(1)} collective-permute-done((bf16[296,256]{1,0:T(8,128)(2,1)S(1)}, bf16[296,256]{1,0:T(8,128)(2,1)S(1)}, u32[]{:S(2)}, u32[]{:S(2)}) %collective-permute-start.9) | collective-permute-done | bytes 151584 | tf_op jit(solution)/shard_map/ppermute | solution.py:352
  27.0 6.2 %score.5 = (f32[10,288,768]{2,1,0:T(8,128)S(1)}, f32[288,96]{1,0:T(8,128)S(1)}, f32[11,8,768]{2,1,0:T(8,128)S(1)}, f32[8,128]{1,0:T(8,128)S(1)}, bf16[7680,512]{...) custom-call(bf16[296,256]{1,0:T(8,128)(2,1)S(1)} %collective-permute, ...), custom_call_target="tpu_custom_call", output_to_operand_aliasing={{6}: (4, {}), {7}: (5, {}), {4}: (10, {}), {5}: (11, {}), {... | custom-call | flops 1 | bytes 1 | tf_op jit(solution)/shard_map/score/pallas_call | solution.py:373
  33.1 1.7 %collective-permute-start.12 = (f32[8,128]{1,0:T(8,128)S(1)}, f32[8,128]{1,0:T(8,128)S(1)}, u32[]{:S(2)}, u32[]{:S(2)}) collective-permute-start(f32[8,128]{1,0:T(8,128)S(1)} %get-tuple-element.95.r_0_), channel_id=1, source_target_pairs={{0,3},{1,2},{2,1},{3,0},{4,7},{5,6},{6,5},{7,4},{8,11},{9,10},{10,... | collective-permute-start | bytes 12296 | tf_op jit(solution)/shard_map/ppermute | solution.py:352
  34.8 1.2 %collective-permute-start.11 = (f32[8,128]{1,0:T(8,128)S(1)}, f32[8,128]{1,0:T(8,128)S(1)}, u32[]{:S(2)}, u32[]{:S(2)}) collective-permute-start(f32[8,128]{1,0:T(8,128)S(1)} %get-tuple-element.95.r_0_), channel_id=1, source_target_pairs={{0,2},{1,3},{2,0},{3,1},{4,6},{5,7},{6,4},{7,5},{8,10},{9,11},{10,... | collective-permute-start | bytes 12296 | tf_op jit(solution)/shard_map/ppermute | solution.py:352
  36.7 1.0 %collective-permute-done.12.r_3_ = f32[8,128]{1,0:T(8,128)S(1)} collective-permute-done((f32[8,128]{1,0:T(8,128)S(1)}, f32[8,128]{1,0:T(8,128)S(1)}, u32[]{:S(2)}, u32[]{:S(2)}) %collective-permute-start.12) | collective-permute-done | bytes 4128 | tf_op jit(solution)/shard_map/ppermute | solution.py:352
  38.4 1.2 %collective-permute-done.10.r_1_ = f32[8,128]{1,0:T(8,128)S(1)} collective-permute-done((f32[8,128]{1,0:T(8,128)S(1)}, f32[8,128]{1,0:T(8,128)S(1)}, u32[]{:S(2)}, u32[]{:S(2)}) %collective-permute-start.10) | collective-permute-done | bytes 4128 | tf_op jit(solution)/shard_map/ppermute | solution.py:352
  39.7 4.1 %sums_first.1 = (bf16[10,288,768]{2,1,0:T(8,128)(2,1)S(1)}, bf16[288,96]{1,0:T(8,128)(2,1)S(1)}, f32[288,256]{1,0:T(8,128)S(1)}, bf16[296,256]{1,0:T(8,128)(2,1)...) custom-call(f32[8,128]{1,0:T(8,128)S(1)} %get-tuple-element.95.r_0_,, ...), custom_call_target="tpu_custom_call", output_to_operand_aliasing={{5}: (9, {}), {6}: (10, {}), {7}: (11, {})} | custom-call | flops 1 | bytes 1 | tf_op jit(solution)/shard_map/sums_first/pallas_call | solution.py:373
  43.9 2.5 %sums.3 = (f32[288,256]{1,0:T(8,128)S(1)}, bf16[288,256]{1,0:T(8,128)(2,1)S(1)}, bf16[7680,512]{1,0:T(8,128)(2,1)S(1)}, bf16[7680,512]{1,0:T(8,128)(2,1)S(1)}) custom-call(bf16[10,288,768]{2,1,0:T(8,128)(2,1)S(1)} %get-tuple-element.103.r_0_, bf16[288,96]{1,0:T(8,128)(2,1)S(1)} %get-tuple-element.120.r_1_, ...), custom_call_target="tpu_custom_call", output_to_operand_aliasing={{2}: (4, {}), {3}: (5, {})} | custom-call | flops 1 | bytes 1 | tf_op jit(solution)/shard_map/sums/pallas_call | solution.py:373
  48.0 2.5 %sums.4 = (f32[288,256]{1,0:T(8,128)S(1)}, bf16[288,256]{1,0:T(8,128)(2,1)S(1)}, bf16[7680,512]{1,0:T(8,128)(2,1)S(1)}) custom-call(bf16[10,288,768]{2,1,0:T(8,128)(2,1)S(1)} %get-tuple-element.103.r_0_, bf16[288,96]{1,0:T(8,128)(2,1)S(1)} %get-tuple-element.120.r_1_, ...), custom_call_target="tpu_custom_call", output_to_operand_aliasing={{2}: (4, {})} | custom-call | flops 1 | bytes 1 | tf_op jit(solution)/shard_map/sums/pallas_call | solution.py:373
  52.0 1.0 %collective-permute-done.17.refs_0_ = bf16[296,256]{1,0:T(8,128)(2,1)S(1)} collective-permute-done((bf16[296,256]{1,0:T(8,128)(2,1)S(1)}, bf16[296,256]{1,0:T(8,128)(2,1)S(1)}, u32[]{:S(2)}, u32[]{:S(2)}) %collective-permute-start.17) | collective-permute-done | bytes 151584 | tf_op jit(solution)/shard_map/ppermute | solution.py:352
  53.1 2.7 %collective-permute-start.18 = (bf16[296,256]{1,0:T(8,128)(2,1)S(1)}, bf16[296,256]{1,0:T(8,128)(2,1)S(1)}, u32[]{:S(2)}, u32[]{:S(2)}) collective-permute-start(bf16[296,256]{1,0:T(8,128)(2,1)S(1)} %pair.3), channel_id=1, source_target_pairs={{0,16},{4,20},{8,24},{12,28},{16,0},{20,4},{24,8},{28,12},{1,17},{... | collective-permute-start | bytes 454664 | tf_op jit(solution)/shard_map/ppermute | solution.py:352
  55.7 2.5 %sums.5 = (f32[288,256]{1,0:T(8,128)S(1)}, bf16[288,256]{1,0:T(8,128)(2,1)S(1)}) custom-call(bf16[10,288,768]{2,1,0:T(8,128)(2,1)S(1)} %get-tuple-element.103.r_0_, bf16[288,96]{1,0:T(8,128)(2,1)S(1)} %get-tuple-element.120.r_1_, bf16[7680,512]{1,0:T(8,128)(2,1)S(1)} %get-tuple-element.121.r_2_, bf16[96,2048]{1,0:T(8,128)(2,1)S(1)} %get-tuple-element.71.r_3_.r_6_.r_8_), custom_call_target="tpu_custom_call" | custom-call | flops 1 | bytes 1 | tf_op jit(solution)/shard_map/sums/pallas_call | solution.py:373
  58.3 1.7 %collective-permute-done.15.r_0_ = bf16[296,256]{1,0:T(8,128)(2,1)S(1)} collective-permute-done((bf16[296,256]{1,0:T(8,128)(2,1)S(1)}, bf16[296,256]{1,0:T(8,128)(2,1)S(1)}, u32[]{:S(2)}, u32[]{:S(2)}) %collective-permute-start.15) | collective-permute-done | bytes 151584 | tf_op jit(solution)/shard_map/ppermute | solution.py:352
  60.0 2.5 %collective-permute-done.18.r_1_ = bf16[296,256]{1,0:T(8,128)(2,1)S(1)} collective-permute-done((bf16[296,256]{1,0:T(8,128)(2,1)S(1)}, bf16[296,256]{1,0:T(8,128)(2,1)S(1)}, u32[]{:S(2)}, u32[]{:S(2)}) %collective-permute-start.18) | collective-permute-done | bytes 151584 | tf_op jit(solution)/shard_map/ppermute | solution.py:352
  62.5 0.9 %finish.1 = (f32[288,256]{1,0:T(8,128)}, f32[8,36]{1,0:T(8,128)}) custom-call(bf16[296,256]{1,0:T(8,128)(2,1)S(1)} %collective-permute-done.15.r_0_, bf16[296,256]{1,0:T(8,128)(2,1)S(1)} %collective-permute-done.18.r_1_, f32[288,256]{1,0:T(8,128)S(1)} %get-tuple-element.122.r_2_, bf16[288,256]{1,0:T(8,128)(2,1)S(1)} %collective-permute-done.19.r_3_, ...), custom_call_target="tpu_custom_call" | custom-call | flops 1 | bytes 1 | tf_op jit(solution)/shard_map/finish/pallas_call | solution.py:373
  (29 shorter events, 6.0 us)
Async XLA Ops:
  0.6 10.5 %collective-permute-start.1 = (bf16[96,512]{1,0:T(8,128)(2,1)}, bf16[96,512]{1,0:T(8,128)(2,1)S(1)}, u32[]{:S(2)}, u32[]{:S(2)}) collective-permute-start(bf16[96,512]{1,0:T(8,128)(2,1)} %r_3_.1), channel_id=1, source_target_pairs={{0,1},{1,0},{2,3},{3,2},{4,5},{5,4},{6,7},{7,6},{8,9},{9,8},{10,11... | collective-permute-start | bytes 294920 | tf_op jit(solution)/shard_map/ppermute | solution.py:352
  3.6 7.5 %collective-permute-start.3 = (bf16[96,512]{1,0:T(8,128)(2,1)}, bf16[96,512]{1,0:T(8,128)(2,1)S(1)}, u32[]{:S(2)}, u32[]{:S(2)}) collective-permute-start(bf16[96,512]{1,0:T(8,128)(2,1)} %r_3_.1), channel_id=1, source_target_pairs={{0,3},{1,2},{2,1},{3,0},{4,7},{5,6},{6,5},{7,4},{8,11},{9,10},{10,... | collective-permute-start | bytes 294920 | tf_op jit(solution)/shard_map/ppermute | solution.py:352
  5.1 6.1 %collective-permute-start.2 = (bf16[96,512]{1,0:T(8,128)(2,1)}, bf16[96,512]{1,0:T(8,128)(2,1)S(1)}, u32[]{:S(2)}, u32[]{:S(2)}) collective-permute-start(bf16[96,512]{1,0:T(8,128)(2,1)} %r_3_.1), channel_id=1, source_target_pairs={{0,2},{1,3},{2,0},{3,1},{4,6},{5,7},{6,4},{7,5},{8,10},{9,11},{10,... | collective-permute-start | bytes 294920 | tf_op jit(solution)/shard_map/ppermute | solution.py:352
  6.4 11.0 %collective-permute-start.5 = (bf16[296,256]{1,0:T(8,128)(2,1)S(1)}, bf16[296,256]{1,0:T(8,128)(2,1)S(1)}, u32[]{:S(2)}, u32[]{:S(2)}) collective-permute-start(bf16[296,256]{1,0:T(8,128)(2,1)S(1)} %get-tuple-element.64.r_0_), channel_id=1, source_target_pairs={{0,8},{4,12},{8,0},{12,4},{16,24},{20,28},{24,16},{28,20},{1,9},{5... | collective-permute-start | bytes 454664 | tf_op jit(solution)/shard_map/ppermute | solution.py:352
  8.5 8.9 %collective-permute-start.4 = (bf16[296,256]{1,0:T(8,128)(2,1)S(1)}, bf16[296,256]{1,0:T(8,128)(2,1)S(1)}, u32[]{:S(2)}, u32[]{:S(2)}) collective-permute-start(bf16[296,256]{1,0:T(8,128)(2,1)S(1)} %get-tuple-element.64.r_0_), channel_id=1, source_target_pairs={{0,16},{4,20},{8,24},{12,28},{16,0},{20,4},{24,8},{28,12},{1,17},{... | collective-permute-start | bytes 454664 | tf_op jit(solution)/shard_map/ppermute | solution.py:352
  11.1 8.0 %collective-permute-start = (bf16[296,256]{1,0:T(8,128)(2,1)S(1)}, bf16[296,256]{1,0:T(8,128)(2,1)S(1)}, u32[]{:S(2)}, u32[]{:S(2)}) collective-permute-start(bf16[296,256]{1,0:T(8,128)(2,1)S(1)} %get-tuple-element.64.r_0_), channel_id=1, source_target_pairs={{0,4},{4,0},{8,12},{12,8},{16,20},{20,16},{24,28},{28,24},{1,5},{5... | collective-permute-start | bytes 454664 | tf_op jit(solution)/shard_map/ppermute | solution.py:352
  17.4 4.5 %collective-permute-start.7 = (bf16[296,256]{1,0:T(8,128)(2,1)S(1)}, bf16[296,256]{1,0:T(8,128)(2,1)S(1)}, u32[]{:S(2)}, u32[]{:S(2)}) collective-permute-start(bf16[296,256]{1,0:T(8,128)(2,1)S(1)} %collective-permute-done.5.r_0_), channel_id=1, source_target_pairs={{0,4},{4,0},{8,12},{12,8},{16,20},{20,16},{24,28},{28,24},{1,5},{5... | collective-permute-start | bytes 454664 | tf_op jit(solution)/shard_map/ppermute | solution.py:352
  17.8 7.7 %collective-permute-start.8 = (bf16[296,256]{1,0:T(8,128)(2,1)S(1)}, bf16[296,256]{1,0:T(8,128)(2,1)S(1)}, u32[]{:S(2)}, u32[]{:S(2)}) collective-permute-start(bf16[296,256]{1,0:T(8,128)(2,1)S(1)} %collective-permute-done.4.r_0_), channel_id=1, source_target_pairs={{0,8},{4,12},{8,0},{12,4},{16,24},{20,28},{24,16},{28,20},{1,9},{5... | collective-permute-start | bytes 454664 | tf_op jit(solution)/shard_map/ppermute | solution.py:352
  21.6 4.3 %collective-permute-start.6 = (bf16[296,256]{1,0:T(8,128)(2,1)S(1)}, bf16[296,256]{1,0:T(8,128)(2,1)S(1)}, u32[]{:S(2)}, u32[]{:S(2)}) collective-permute-start(bf16[296,256]{1,0:T(8,128)(2,1)S(1)} %collective-permute-done.4.r_0_), channel_id=1, source_target_pairs={{0,4},{4,0},{8,12},{12,8},{16,20},{20,16},{24,28},{28,24},{1,5},{5... | collective-permute-start | bytes 454664 | tf_op jit(solution)/shard_map/ppermute | solution.py:352
  25.5 1.4 %collective-permute-start.9 = (bf16[296,256]{1,0:T(8,128)(2,1)S(1)}, bf16[296,256]{1,0:T(8,128)(2,1)S(1)}, u32[]{:S(2)}, u32[]{:S(2)}) collective-permute-start(bf16[296,256]{1,0:T(8,128)(2,1)S(1)} %collective-permute-done.8.r_2_), channel_id=1, source_target_pairs={{0,4},{4,0},{8,12},{12,8},{16,20},{20,16},{24,28},{28,24},{1,5},{5... | collective-permute-start | bytes 454664 | tf_op jit(solution)/shard_map/ppermute | solution.py:352
  33.1 4.6 %collective-permute-start.12 = (f32[8,128]{1,0:T(8,128)S(1)}, f32[8,128]{1,0:T(8,128)S(1)}, u32[]{:S(2)}, u32[]{:S(2)}) collective-permute-start(f32[8,128]{1,0:T(8,128)S(1)} %get-tuple-element.95.r_0_), channel_id=1, source_target_pairs={{0,3},{1,2},{2,1},{3,0},{4,7},{5,6},{6,5},{7,4},{8,11},{9,10},{10,... | collective-permute-start | bytes 12296 | tf_op jit(solution)/shard_map/ppermute | solution.py:352
  34.8 3.6 %collective-permute-start.11 = (f32[8,128]{1,0:T(8,128)S(1)}, f32[8,128]{1,0:T(8,128)S(1)}, u32[]{:S(2)}, u32[]{:S(2)}) collective-permute-start(f32[8,128]{1,0:T(8,128)S(1)} %get-tuple-element.95.r_0_), channel_id=1, source_target_pairs={{0,2},{1,3},{2,0},{3,1},{4,6},{5,7},{6,4},{7,5},{8,10},{9,11},{10,... | collective-permute-start | bytes 12296 | tf_op jit(solution)/shard_map/ppermute | solution.py:352
  36.1 3.6 %collective-permute-start.10 = (f32[8,128]{1,0:T(8,128)S(1)}, f32[8,128]{1,0:T(8,128)S(1)}, u32[]{:S(2)}, u32[]{:S(2)}) collective-permute-start(f32[8,128]{1,0:T(8,128)S(1)} %get-tuple-element.95.r_0_), channel_id=1, source_target_pairs={{0,1},{1,0},{2,3},{3,2},{4,5},{5,4},{6,7},{7,6},{8,9},{9,8},{10,11... | collective-permute-start | bytes 12296 | tf_op jit(solution)/shard_map/ppermute | solution.py:352
  43.8 3.1 %collective-permute-start.14 = (bf16[296,256]{1,0:T(8,128)(2,1)S(1)}, bf16[296,256]{1,0:T(8,128)(2,1)S(1)}, u32[]{:S(2)}, u32[]{:S(2)}) collective-permute-start(bf16[296,256]{1,0:T(8,128)(2,1)S(1)} %get-tuple-element.111), channel_id=1, source_target_pairs={{0,4},{4,0},{8,12},{12,8},{16,20},{20,16},{24,28},{28,24},{1,5},{5... | collective-permute-start | bytes 454664 | tf_op jit(solution)/shard_map/ppermute | solution.py:352
  46.4 1.6 %collective-permute-start.13 = (bf16[288,256]{1,0:T(8,128)(2,1)S(1)}, bf16[288,256]{1,0:T(8,128)(2,1)S(1)}, u32[]{:S(2)}, u32[]{:S(2)}) collective-permute-start(bf16[288,256]{1,0:T(8,128)(2,1)S(1)} %get-tuple-element.109), channel_id=1, source_target_pairs={{0,4},{4,0},{8,12},{12,8},{16,20},{20,16},{24,28},{28,24},{1,5},{5... | collective-permute-start | bytes 442376 | tf_op jit(solution)/shard_map/ppermute | solution.py:352
  47.0 5.9 %collective-permute-start.17 = (bf16[296,256]{1,0:T(8,128)(2,1)S(1)}, bf16[296,256]{1,0:T(8,128)(2,1)S(1)}, u32[]{:S(2)}, u32[]{:S(2)}) collective-permute-start(bf16[296,256]{1,0:T(8,128)(2,1)S(1)} %get-tuple-element.119), channel_id=1, source_target_pairs={{0,8},{4,12},{8,0},{12,4},{16,24},{20,28},{24,16},{28,20},{1,9},{5... | collective-permute-start | bytes 454664 | tf_op jit(solution)/shard_map/ppermute | solution.py:352
  50.5 1.4 %collective-permute-start.16 = (bf16[288,256]{1,0:T(8,128)(2,1)S(1)}, bf16[288,256]{1,0:T(8,128)(2,1)S(1)}, u32[]{:S(2)}, u32[]{:S(2)}) collective-permute-start(bf16[288,256]{1,0:T(8,128)(2,1)S(1)} %get-tuple-element.118), channel_id=1, source_target_pairs={{0,4},{4,0},{8,12},{12,8},{16,20},{20,16},{24,28},{28,24},{1,5},{5... | collective-permute-start | bytes 442376 | tf_op jit(solution)/shard_map/ppermute | solution.py:352
  51.0 9.0 %collective-permute-start.15 = (bf16[296,256]{1,0:T(8,128)(2,1)S(1)}, bf16[296,256]{1,0:T(8,128)(2,1)S(1)}, u32[]{:S(2)}, u32[]{:S(2)}) collective-permute-start(bf16[296,256]{1,0:T(8,128)(2,1)S(1)} %pair.2), channel_id=1, source_target_pairs={{0,8},{4,12},{8,0},{12,4},{16,24},{20,28},{24,16},{28,20},{1,9},{5... | collective-permute-start | bytes 454664 | tf_op jit(solution)/shard_map/ppermute | solution.py:352
  53.1 9.5 %collective-permute-start.18 = (bf16[296,256]{1,0:T(8,128)(2,1)S(1)}, bf16[296,256]{1,0:T(8,128)(2,1)S(1)}, u32[]{:S(2)}, u32[]{:S(2)}) collective-permute-start(bf16[296,256]{1,0:T(8,128)(2,1)S(1)} %pair.3), channel_id=1, source_target_pairs={{0,16},{4,20},{8,24},{12,28},{16,0},{20,4},{24,8},{28,12},{1,17},{... | collective-permute-start | bytes 454664 | tf_op jit(solution)/shard_map/ppermute | solution.py:352
  58.2 1.8 %collective-permute-start.19 = (bf16[288,256]{1,0:T(8,128)(2,1)S(1)}, bf16[288,256]{1,0:T(8,128)(2,1)S(1)}, u32[]{:S(2)}, u32[]{:S(2)}) collective-permute-start(bf16[288,256]{1,0:T(8,128)(2,1)S(1)} %get-tuple-element.123), channel_id=1, source_target_pairs={{0,4},{4,0},{8,12},{12,8},{16,20},{20,16},{24,28},{28,24},{1,5},{5... | collective-permute-start | bytes 442376 | tf_op jit(solution)/shard_map/ppermute | solution.py:352
